TPU v7x, 32 devices: a whole 2x2x4 slice. The times are simulated.
32 devices in a mesh: gz: 8 (over z, core), pair: 4 (over y, x).
Axes of the slice: x: 2, y: 2, z: 4, core: 2. Of those that a mesh axis runs over, the one named last changes fastest.
Arguments:
- orbitals: bfloat16 [8, 64, 256, 256], P(None, 'gz'), may hold values from -6 to 6
- pair_index: int32 [4, 2], P('pair'), may hold values from 0 to 7
- pair_weight: float32 [4], P('pair'), may hold values from 0.5 to 2
Outputs:
- potential: float32 [4, 64, 256, 256], P('pair', 'gz')
- residual_norm: float32 [4], P('pair')
- energy: float32 [1], replicated
Inputs may be any that keep to these rules, and one draw needn't show every extreme that they name: `pair_index`: A pair may name one orbital twice.
All inputs are finite; a program needn't handle non-finite values.
Results may differ from a plain program's by a relative error of at most 0.0003.
Values sent between devices are 32-bit elements; how exact they have to be, the bound alone decides.
No kernel may reach another device: no remote copies, remote signals or barrier semaphores. Data moves between devices by JAX's collectives and lax.ppermute only.
A program may use at most 320 MiB of HBM per device.

v0:
```python
import jax
import jax.numpy as jnp
from jax import lax
from jax.sharding import PartitionSpec as P

LEVELS = 4
NU = 2
COARSE = 8


relax = 2.0 / 3.0


def with_halo(block, sides, width):
    for axis, dim in sides:
        count = lax.axis_size(axis)
        forward = [(i, i + 1) for i in range(count - 1)]
        backward = [(target, source) for source, target in forward]
        low = lax.ppermute(
            lax.slice_in_dim(block, block.shape[dim] - width, None, axis=dim), axis, forward
        )
        high = lax.ppermute(lax.slice_in_dim(block, 0, width, axis=dim), axis, backward)
        block = jnp.concatenate([low, block, high], axis=dim)
    return block


def apply_op(field, level):
    extended = with_halo(field, (("gz", 1),), 1)
    padded = jnp.pad(field, ((0, 0), (0, 0), (1, 1), (1, 1)))
    beside = extended[:, 2:] + extended[:, :-2]
    beside = beside + padded[:, :, 2:, 1:-1] + padded[:, :, :-2, 1:-1]
    beside = beside + padded[:, :, 1:-1, 2:] + padded[:, :, 1:-1, :-2]
    return (6.0 * field - beside) * 0.25**level


def local_op(field, level):
    padded = jnp.pad(field, ((0, 0), (1, 1), (1, 1), (1, 1)))
    beside = padded[:, 2:, 1:-1, 1:-1] + padded[:, :-2, 1:-1, 1:-1]
    beside = beside + padded[:, 1:-1, 2:, 1:-1] + padded[:, 1:-1, :-2, 1:-1]
    beside = beside + padded[:, 1:-1, 1:-1, 2:] + padded[:, 1:-1, 1:-1, :-2]
    return (6.0 * field - beside) * 0.25**level


def sweep(field, source, level):
    return field + (source - apply_op(field, level)) * (relax * 4.0**level / 6.0)


def restrict(field):
    pairs, zsize, ysize, xsize = field.shape
    return field.reshape(pairs, zsize // 2, 2, ysize // 2, 2, xsize // 2, 2).mean(axis=(2, 4, 6))


def prolong(field):
    return jnp.repeat(jnp.repeat(jnp.repeat(field, 2, axis=1), 2, axis=2), 2, axis=3)


def coarsest(source, level):
    gathered = lax.all_gather(source, "gz", axis=1, tiled=True)
    field = jnp.zeros_like(gathered)
    for _ in range(COARSE):
        field = field + (gathered - local_op(field, level)) * (relax * 4.0**level / 6.0)
    planes = source.shape[1]
    return lax.dynamic_slice_in_dim(field, lax.axis_index("gz") * planes, planes, 1)


def vcycle(field, source, level):
    if level == LEVELS - 1:
        return coarsest(source, level)
    for _ in range(NU):
        field = sweep(field, source, level)
    remain = source - apply_op(field, level)
    coarse_source = restrict(remain)
    correction = vcycle(jnp.zeros_like(coarse_source), coarse_source, level + 1)
    field = field + prolong(correction)
    for _ in range(NU):
        field = sweep(field, source, level)
    return field


def solve(density):
    field = jnp.zeros_like(density)
    field = vcycle(field, density, 0)
    return field


def per_device(orbitals, pair_index, pair_weight):
    left_orbital = jnp.take(orbitals, pair_index[:, 0], axis=0).astype(jnp.float32)
    right_orbital = jnp.take(orbitals, pair_index[:, 1], axis=0).astype(jnp.float32)
    density = left_orbital * right_orbital
    potential = solve(density)
    final = density - apply_op(potential, 0)
    totals = lax.psum(
        (jnp.sum(final * final, axis=(1, 2, 3)), jnp.sum(density * potential, axis=(1, 2, 3))), "gz"
    )
    cell_count = density.shape[1] * lax.axis_size("gz") * density.shape[2] * density.shape[3]
    residual_norm = jnp.sqrt(totals[0] / cell_count)
    partial_energy = -0.5 * jnp.sum(pair_weight * totals[1]) / cell_count
    energy = lax.psum(partial_energy, "pair").reshape(1)
    return (potential, residual_norm, energy)


def solution(mesh):
    return jax.shard_map(
        per_device,
        mesh=mesh,
        in_specs=(P(None, "gz", None, None), P("pair", None), P("pair")),
        out_specs=(P("pair", "gz", None, None), P("pair"), P()),
        check_vma=False,
    )
```

profile of v0, /device:TPU:0, one launch (start us, length us, event | category | flops | bytes accessed | tf_op | source)
XLA Modules:
  0.0 407.4 jit_solution(4606733979402125156)
XLA Ops:
  2.8 3.7 collective-permute-start.1
  6.5 1.3 fusion.235
  11.7 1.7 constant_dynamic-slice_fusion.1
  15.6 2.7 broadcast_multiply_fusion
  18.7 1.3 collective-permute-start.2
  20.0 4.5 %collective-permute-start.3 = (f32[1,1,256,256]{2,1,3,0:T(1,128)S(1)}, f32[1,1,256,256]{2,1,3,0:T(1,128)S(1)}, u32[]{:S(2)}, u32[]{:S(2)}) collective-permute-start(f32[1,1,256,256]{2,1,3,0:T(1,128)S(1)} %get-tuple-element.46), channel_id=1, source_target_pairs={{0,4},{4,8},{8,12},{12,16},{16,20},{20,24},{24,28},{1,5},{5,9},{9,... | collective-permute-start | bytes 786440 | tf_op jit(solution)/shard_map/ppermute | solution.py:19
  25.7 2.3 fusion.14
  28.3 1.3 collective-permute-start.4
  29.6 6.4 %collective-permute-start.5 = (f32[1,1,256,256]{2,1,3,0:T(1,128)S(1)}, f32[1,1,256,256]{2,1,3,0:T(1,128)S(1)}, u32[]{:S(2)}, u32[]{:S(2)}) collective-permute-start(f32[1,1,256,256]{2,1,3,0:T(1,128)S(1)} %get-tuple-element.44), channel_id=1, source_target_pairs={{0,4},{4,8},{8,12},{12,16},{16,20},{20,24},{24,28},{1,5},{5,9},{9,... | collective-permute-start | bytes 786440 | tf_op jit(solution)/shard_map/ppermute | solution.py:19
  36.1 1.3 collective-permute-start.6
  37.4 5.0 %collective-permute-start.7 = (f32[1,1,128,128]{3,2,1,0:T(8,128)S(1)}, f32[1,1,128,128]{3,2,1,0:T(8,128)S(1)}, u32[]{:S(2)}, u32[]{:S(2)}) collective-permute-start(f32[1,1,128,128]{3,2,1,0:T(8,128)S(1)} %broadcast.203), channel_id=1, source_target_pairs={{0,4},{4,8},{8,12},{12,16},{16,20},{20,24},{24,28},{1,5},{5,9},{9,... | collective-permute-start | bytes 196616 | tf_op jit(solution)/shard_map/ppermute | solution.py:19
  42.4 3.1 fusion.20
  45.5 3.0 copy.35
  48.4 136.2 %reshape.102 = f32[4,2,128,2,128,2]{5,4,3,2,1,0:T(8,128)} reshape(f32[1,8,256,256]{3,2,1,0:T(8,128)} %copy.35) | data formatting | bytes 4194304 | tf_op jit(solution)/shard_map/reshape | solution.py:50
  184.6 40.6 %reduce_sum.60 = f32[4,128,128]{2,1,0:T(8,128)S(1)} reduce(f32[4,2,128,2,128,2]{5,4,3,2,1,0:T(8,128)} %reshape.102, f32[]{:T(128)} %constant.30.clone.1), dimensions={1,3,5}, to_apply=%region_0.0 | reduce | flops 458752 | bytes 2359300 | tf_op jit(solution)/shard_map/reduce_sum | solution.py:50
  225.5 1.3 collective-permute-start.8
  226.8 4.3 %collective-permute-start.9 = (f32[1,1,128,128]{3,2,1,0:T(8,128)S(1)}, f32[1,1,128,128]{3,2,1,0:T(8,128)S(1)}, u32[]{:S(2)}, u32[]{:S(2)}) collective-permute-start(f32[1,1,128,128]{3,2,1,0:T(8,128)S(1)} %get-tuple-element.54), channel_id=1, source_target_pairs={{0,4},{4,8},{8,12},{12,16},{16,20},{20,24},{24,28},{1,5},{5,9},{9,... | collective-permute-start | bytes 196616 | tf_op jit(solution)/shard_map/ppermute | solution.py:19
  232.2 1.3 collective-permute-start.10
  233.5 4.7 %collective-permute-start.11 = (f32[1,1,128,128]{3,2,1,0:T(8,128)S(1)}, f32[1,1,128,128]{3,2,1,0:T(8,128)S(1)}, u32[]{:S(2)}, u32[]{:S(2)}) collective-permute-start(f32[1,1,128,128]{3,2,1,0:T(8,128)S(1)} %get-tuple-element.52), channel_id=1, source_target_pairs={{0,4},{4,8},{8,12},{12,16},{16,20},{20,24},{24,28},{1,5},{5,9},{9,... | collective-permute-start | bytes 196616 | tf_op jit(solution)/shard_map/ppermute | solution.py:19
  238.3 1.3 collective-permute-start.12
  239.6 4.9 %collective-permute-start.13 = (f32[1,1,64,64]{3,2,1,0:T(8,128)S(1)}, f32[1,1,64,64]{3,2,1,0:T(8,128)S(1)}, u32[]{:S(2)}, u32[]{:S(2)}) collective-permute-start(f32[1,1,64,64]{3,2,1,0:T(8,128)S(1)} %broadcast.208), channel_id=1, source_target_pairs={{0,4},{4,8},{8,12},{12,16},{16,20},{20,24},{24,28},{1,5},{5,9},{9,... | collective-permute-start | bytes 49160 | tf_op jit(solution)/shard_map/ppermute | solution.py:19
  244.7 18.1 %reshape.103 = f32[2,2,64,2,64,2]{5,4,3,2,1,0:T(8,128)} reshape(f32[1,4,128,128]{3,2,1,0:T(8,128)S(1)} %fusion.73) | data formatting | bytes 524288 | tf_op jit(solution)/shard_map/reshape | solution.py:50
  262.8 7.0 %reduce_sum.61 = f32[2,64,64]{2,1,0:T(8,128)S(1)} reduce(f32[2,2,64,2,64,2]{5,4,3,2,1,0:T(8,128)} %reshape.103, f32[]{:T(128)} %constant.30.clone.1), dimensions={1,3,5}, to_apply=%region_1.3 | reduce | flops 57344 | bytes 294916 | tf_op jit(solution)/shard_map/reduce_sum | solution.py:50
  270.0 1.3 collective-permute-start.14
  271.3 4.3 %collective-permute-start.15 = (f32[1,1,64,64]{3,2,1,0:T(8,128)S(1)}, f32[1,1,64,64]{3,2,1,0:T(8,128)S(1)}, u32[]{:S(2)}, u32[]{:S(2)}) collective-permute-start(f32[1,1,64,64]{3,2,1,0:T(8,128)S(1)} %get-tuple-element.64), channel_id=1, source_target_pairs={{0,4},{4,8},{8,12},{12,16},{16,20},{20,24},{24,28},{1,5},{5,9},{9,... | collective-permute-start | bytes 49160 | tf_op jit(solution)/shard_map/ppermute | solution.py:19
  276.5 1.3 collective-permute-start.16
  277.8 4.6 %collective-permute-start.17 = (f32[1,1,64,64]{3,2,1,0:T(8,128)S(1)}, f32[1,1,64,64]{3,2,1,0:T(8,128)S(1)}, u32[]{:S(2)}, u32[]{:S(2)}) collective-permute-start(f32[1,1,64,64]{3,2,1,0:T(8,128)S(1)} %get-tuple-element.62), channel_id=1, source_target_pairs={{0,4},{4,8},{8,12},{12,16},{16,20},{20,24},{24,28},{1,5},{5,9},{9,... | collective-permute-start | bytes 49160 | tf_op jit(solution)/shard_map/ppermute | solution.py:19
  283.8 1.8 reduce_sum.63
  285.9 17.4 %all-gather = f32[256,32]{1,0:T(8,128)S(1)} all-gather(f32[32,32]{1,0:T(8,128)S(1)} %broadcast_multiply_fusion.4), channel_id=2, replica_groups=mesh['gz'=8,'pair'=4] {'gz'}, dimensions={0}, use_global_device_ids=true | all-gather | bytes 36864 | tf_op jit(solution)/shard_map/all_gather | solution.py:58
  305.1 1.3 collective-permute-start.18
  306.4 3.0 collective-permute-start.19
  310.4 1.3 collective-permute-start.20
  311.7 4.3 %collective-permute-start.21 = (f32[1,1,64,64]{3,2,1,0:T(8,128)S(1)}, f32[1,1,64,64]{3,2,1,0:T(8,128)S(1)}, u32[]{:S(2)}, u32[]{:S(2)}) collective-permute-start(f32[1,1,64,64]{3,2,1,0:T(8,128)S(1)} %get-tuple-element.58), channel_id=1, source_target_pairs={{0,4},{4,8},{8,12},{12,16},{16,20},{20,24},{24,28},{1,5},{5,9},{9,... | collective-permute-start | bytes 49160 | tf_op jit(solution)/shard_map/ppermute | solution.py:19
  317.5 1.3 collective-permute-start.22
  318.8 5.0 %collective-permute-start.23 = (f32[1,1,128,128]{3,2,1,0:T(8,128)S(1)}, f32[1,1,128,128]{3,2,1,0:T(8,128)S(1)}, u32[]{:S(2)}, u32[]{:S(2)}) collective-permute-start(f32[1,1,128,128]{3,2,1,0:T(8,128)S(1)} %get-tuple-element.50), channel_id=1, source_target_pairs={{0,4},{4,8},{8,12},{12,16},{16,20},{20,24},{24,28},{1,5},{5,9},{9,... | collective-permute-start | bytes 196616 | tf_op jit(solution)/shard_map/ppermute | solution.py:19
  324.9 1.3 collective-permute-start.24
  326.2 5.3 %collective-permute-start.25 = (f32[1,1,128,128]{3,2,1,0:T(8,128)S(1)}, f32[1,1,128,128]{3,2,1,0:T(8,128)S(1)}, u32[]{:S(2)}, u32[]{:S(2)}) collective-permute-start(f32[1,1,128,128]{3,2,1,0:T(8,128)S(1)} %get-tuple-element.48), channel_id=1, source_target_pairs={{0,4},{4,8},{8,12},{12,16},{16,20},{20,24},{24,28},{1,5},{5,9},{9,... | collective-permute-start | bytes 196616 | tf_op jit(solution)/shard_map/ppermute | solution.py:19
  334.0 1.7 copy.43
  335.8 1.8 bitcast_add_fusion
  339.2 5.3 %collective-permute-start.27 = (f32[1,1,256,256]{2,1,3,0:T(1,128)S(1)}, f32[1,1,256,256]{2,1,3,0:T(1,128)S(1)}, u32[]{:S(2)}, u32[]{:S(2)}) collective-permute-start(f32[1,1,256,256]{2,1,3,0:T(1,128)S(1)} %get-tuple-element.42), channel_id=1, source_target_pairs={{0,4},{4,8},{8,12},{12,16},{16,20},{20,24},{24,28},{1,5},{5,9},{9,... | collective-permute-start | bytes 786440 | tf_op jit(solution)/shard_map/ppermute | solution.py:19
  345.7 2.2 fusion.28
  349.5 7.1 %collective-permute-start.29 = (f32[1,1,256,256]{2,1,3,0:T(1,128)S(1)}, f32[1,1,256,256]{2,1,3,0:T(1,128)S(1)}, u32[]{:S(2)}, u32[]{:S(2)}) collective-permute-start(f32[1,1,256,256]{2,1,3,0:T(1,128)S(1)} %get-tuple-element.40), channel_id=1, source_target_pairs={{0,4},{4,8},{8,12},{12,16},{16,20},{20,24},{24,28},{1,5},{5,9},{9,... | collective-permute-start | bytes 786440 | tf_op jit(solution)/shard_map/ppermute | solution.py:19
  357.7 2.2 fusion.36
  361.5 7.2 %collective-permute-start.31 = (f32[1,1,256,256]{2,1,3,0:T(1,128)S(1)}, f32[1,1,256,256]{2,1,3,0:T(1,128)S(1)}, u32[]{:S(2)}, u32[]{:S(2)}) collective-permute-start(f32[1,1,256,256]{2,1,3,0:T(1,128)S(1)} %get-tuple-element.38), channel_id=1, source_target_pairs={{0,4},{4,8},{8,12},{12,16},{16,20},{20,24},{24,28},{1,5},{5,9},{9,... | collective-permute-start | bytes 786440 | tf_op jit(solution)/shard_map/ppermute | solution.py:19
  369.8 2.9 multiply_reduce_fusion
  372.8 18.9 %all-reduce.30 = (f32[1]{0:T(128)}, f32[1]{0:T(128)}) all-reduce(f32[1]{0:T(128)} %bitcast.20, f32[1]{0:T(128)} %bitcast.21), channel_id=1, replica_groups=mesh['gz'=8,'pair'=4] {'gz'}, use_global_device_ids=true, to_apply=%region_5.7 | all-reduce | flops 2 | bytes 16 | tf_op jit(solution)/shard_map/psum | solution.py:92
  392.3 2.9 copy.44
  395.2 10.4 %psum.23 = f32[1]{0:T(128)} all-reduce(f32[1]{0:T(128)S(6)} %div.42), channel_id=1, replica_groups=mesh['gz'=8,'pair'=4] {'pair'}, use_global_device_ids=true, to_apply=%region_8.10 | all-reduce | flops 1 | bytes 8 | tf_op jit(solution)/shard_map/psum | solution.py:98
  (103 shorter events, 25.5 us)
Async XLA Ops:
  1.5 14.0 %collective-permute-start = (f32[1,1,256,256]{2,1,3,0:T(1,128)}, f32[1,1,256,256]{2,1,3,0:T(1,128)S(1)}, u32[]{:S(2)}, u32[]{:S(2)}) collective-permute-start(f32[1,1,256,256]{2,1,3,0:T(1,128)} %broadcast.199), channel_id=1, source_target_pairs={{4,0},{8,4},{12,8},{16,12},{20,16},{24,20},{28,24},{5,1},{9,5},{13... | collective-permute-start | bytes 786440 | tf_op jit(solution)/shard_map/ppermute | solution.py:22
  2.8 12.7 %collective-permute-start.1 = (f32[1,1,256,256]{2,1,3,0:T(1,128)}, f32[1,1,256,256]{2,1,3,0:T(1,128)}, u32[]{:S(2)}, u32[]{:S(2)}) collective-permute-start(f32[1,1,256,256]{2,1,3,0:T(1,128)} %broadcast.199), channel_id=1, source_target_pairs={{0,4},{4,8},{8,12},{12,16},{16,20},{20,24},{24,28},{1,5},{5,9},{9,... | collective-permute-start | bytes 786440 | tf_op jit(solution)/shard_map/ppermute | solution.py:19
  18.7 5.8 %collective-permute-start.2 = (f32[1,1,256,256]{2,1,3,0:T(1,128)S(1)}, f32[1,1,256,256]{2,1,3,0:T(1,128)S(1)}, u32[]{:S(2)}, u32[]{:S(2)}) collective-permute-start(f32[1,1,256,256]{2,1,3,0:T(1,128)S(1)} %get-tuple-element.45), channel_id=1, source_target_pairs={{4,0},{8,4},{12,8},{16,12},{20,16},{24,20},{28,24},{5,1},{9,5},{13... | collective-permute-start | bytes 786440 | tf_op jit(solution)/shard_map/ppermute | solution.py:22
  20.0 5.7 %collective-permute-start.3 = (f32[1,1,256,256]{2,1,3,0:T(1,128)S(1)}, f32[1,1,256,256]{2,1,3,0:T(1,128)S(1)}, u32[]{:S(2)}, u32[]{:S(2)}) collective-permute-start(f32[1,1,256,256]{2,1,3,0:T(1,128)S(1)} %get-tuple-element.46), channel_id=1, source_target_pairs={{0,4},{4,8},{8,12},{12,16},{16,20},{20,24},{24,28},{1,5},{5,9},{9,... | collective-permute-start | bytes 786440 | tf_op jit(solution)/shard_map/ppermute | solution.py:19
  28.0 14.4 %copy-start = (f32[1,8,256,256]{2,1,3,0:T(8,128)}, f32[1,8,256,256]{2,1,3,0:T(8,128)S(1)}, u32[]{:S(2)}) copy-start(f32[1,8,256,256]{2,1,3,0:T(8,128)S(1)} %fusion.14) | copy-start | bytes 6291460
  28.3 14.1 %collective-permute-start.4 = (f32[1,1,256,256]{2,1,3,0:T(1,128)S(1)}, f32[1,1,256,256]{2,1,3,0:T(1,128)S(1)}, u32[]{:S(2)}, u32[]{:S(2)}) collective-permute-start(f32[1,1,256,256]{2,1,3,0:T(1,128)S(1)} %get-tuple-element.43), channel_id=1, source_target_pairs={{4,0},{8,4},{12,8},{16,12},{20,16},{24,20},{28,24},{5,1},{9,5},{13... | collective-permute-start | bytes 786440 | tf_op jit(solution)/shard_map/ppermute | solution.py:22
  29.6 12.8 %collective-permute-start.5 = (f32[1,1,256,256]{2,1,3,0:T(1,128)S(1)}, f32[1,1,256,256]{2,1,3,0:T(1,128)S(1)}, u32[]{:S(2)}, u32[]{:S(2)}) collective-permute-start(f32[1,1,256,256]{2,1,3,0:T(1,128)S(1)} %get-tuple-element.44), channel_id=1, source_target_pairs={{0,4},{4,8},{8,12},{12,16},{16,20},{20,24},{24,28},{1,5},{5,9},{9,... | collective-permute-start | bytes 786440 | tf_op jit(solution)/shard_map/ppermute | solution.py:19
  36.1 189.2 %collective-permute-start.6 = (f32[1,1,128,128]{3,2,1,0:T(8,128)S(1)}, f32[1,1,128,128]{3,2,1,0:T(8,128)S(1)}, u32[]{:S(2)}, u32[]{:S(2)}) collective-permute-start(f32[1,1,128,128]{3,2,1,0:T(8,128)S(1)} %broadcast.203), channel_id=1, source_target_pairs={{4,0},{8,4},{12,8},{16,12},{20,16},{24,20},{28,24},{5,1},{9,5},{13... | collective-permute-start | bytes 196616 | tf_op jit(solution)/shard_map/ppermute | solution.py:22
  37.4 187.9 %collective-permute-start.7 = (f32[1,1,128,128]{3,2,1,0:T(8,128)S(1)}, f32[1,1,128,128]{3,2,1,0:T(8,128)S(1)}, u32[]{:S(2)}, u32[]{:S(2)}) collective-permute-start(f32[1,1,128,128]{3,2,1,0:T(8,128)S(1)} %broadcast.203), channel_id=1, source_target_pairs={{0,4},{4,8},{8,12},{12,16},{16,20},{20,24},{24,28},{1,5},{5,9},{9,... | collective-permute-start | bytes 196616 | tf_op jit(solution)/shard_map/ppermute | solution.py:19
  225.5 5.6 %collective-permute-start.8 = (f32[1,1,128,128]{3,2,1,0:T(8,128)S(1)}, f32[1,1,128,128]{3,2,1,0:T(8,128)S(1)}, u32[]{:S(2)}, u32[]{:S(2)}) collective-permute-start(f32[1,1,128,128]{3,2,1,0:T(8,128)S(1)} %get-tuple-element.53), channel_id=1, source_target_pairs={{4,0},{8,4},{12,8},{16,12},{20,16},{24,20},{28,24},{5,1},{9,5},{13... | collective-permute-start | bytes 196616 | tf_op jit(solution)/shard_map/ppermute | solution.py:22
  226.8 5.2 %collective-permute-start.9 = (f32[1,1,128,128]{3,2,1,0:T(8,128)S(1)}, f32[1,1,128,128]{3,2,1,0:T(8,128)S(1)}, u32[]{:S(2)}, u32[]{:S(2)}) collective-permute-start(f32[1,1,128,128]{3,2,1,0:T(8,128)S(1)} %get-tuple-element.54), channel_id=1, source_target_pairs={{0,4},{4,8},{8,12},{12,16},{16,20},{20,24},{24,28},{1,5},{5,9},{9,... | collective-permute-start | bytes 196616 | tf_op jit(solution)/shard_map/ppermute | solution.py:19
  232.2 12.3 %copy-start.2 = (f32[1,4,128,128]{3,2,1,0:T(8,128)}, f32[1,4,128,128]{3,2,1,0:T(8,128)S(1)}, u32[]{:S(2)}) copy-start(f32[1,4,128,128]{3,2,1,0:T(8,128)S(1)} %fusion.66) | copy-start | bytes 786436
  232.2 12.2 %collective-permute-start.10 = (f32[1,1,128,128]{3,2,1,0:T(8,128)S(1)}, f32[1,1,128,128]{3,2,1,0:T(8,128)S(1)}, u32[]{:S(2)}, u32[]{:S(2)}) collective-permute-start(f32[1,1,128,128]{3,2,1,0:T(8,128)S(1)} %get-tuple-element.51), channel_id=1, source_target_pairs={{4,0},{8,4},{12,8},{16,12},{20,16},{24,20},{28,24},{5,1},{9,5},{13... | collective-permute-start | bytes 196616 | tf_op jit(solution)/shard_map/ppermute | solution.py:22
  233.5 10.9 %collective-permute-start.11 = (f32[1,1,128,128]{3,2,1,0:T(8,128)S(1)}, f32[1,1,128,128]{3,2,1,0:T(8,128)S(1)}, u32[]{:S(2)}, u32[]{:S(2)}) collective-permute-start(f32[1,1,128,128]{3,2,1,0:T(8,128)S(1)} %get-tuple-element.52), channel_id=1, source_target_pairs={{0,4},{4,8},{8,12},{12,16},{16,20},{20,24},{24,28},{1,5},{5,9},{9,... | collective-permute-start | bytes 196616 | tf_op jit(solution)/shard_map/ppermute | solution.py:19
  238.3 31.5 %collective-permute-start.12 = (f32[1,1,64,64]{3,2,1,0:T(8,128)S(1)}, f32[1,1,64,64]{3,2,1,0:T(8,128)S(1)}, u32[]{:S(2)}, u32[]{:S(2)}) collective-permute-start(f32[1,1,64,64]{3,2,1,0:T(8,128)S(1)} %broadcast.208), channel_id=1, source_target_pairs={{4,0},{8,4},{12,8},{16,12},{20,16},{24,20},{28,24},{5,1},{9,5},{13... | collective-permute-start | bytes 49160 | tf_op jit(solution)/shard_map/ppermute | solution.py:22
  239.6 30.2 %collective-permute-start.13 = (f32[1,1,64,64]{3,2,1,0:T(8,128)S(1)}, f32[1,1,64,64]{3,2,1,0:T(8,128)S(1)}, u32[]{:S(2)}, u32[]{:S(2)}) collective-permute-start(f32[1,1,64,64]{3,2,1,0:T(8,128)S(1)} %broadcast.208), channel_id=1, source_target_pairs={{0,4},{4,8},{8,12},{12,16},{16,20},{20,24},{24,28},{1,5},{5,9},{9,... | collective-permute-start | bytes 49160 | tf_op jit(solution)/shard_map/ppermute | solution.py:19
  270.0 5.6 %collective-permute-start.14 = (f32[1,1,64,64]{3,2,1,0:T(8,128)S(1)}, f32[1,1,64,64]{3,2,1,0:T(8,128)S(1)}, u32[]{:S(2)}, u32[]{:S(2)}) collective-permute-start(f32[1,1,64,64]{3,2,1,0:T(8,128)S(1)} %get-tuple-element.63), channel_id=1, source_target_pairs={{4,0},{8,4},{12,8},{16,12},{20,16},{24,20},{28,24},{5,1},{9,5},{13... | collective-permute-start | bytes 49160 | tf_op jit(solution)/shard_map/ppermute | solution.py:22
  271.3 5.1 %collective-permute-start.15 = (f32[1,1,64,64]{3,2,1,0:T(8,128)S(1)}, f32[1,1,64,64]{3,2,1,0:T(8,128)S(1)}, u32[]{:S(2)}, u32[]{:S(2)}) collective-permute-start(f32[1,1,64,64]{3,2,1,0:T(8,128)S(1)} %get-tuple-element.64), channel_id=1, source_target_pairs={{0,4},{4,8},{8,12},{12,16},{16,20},{20,24},{24,28},{1,5},{5,9},{9,... | collective-permute-start | bytes 49160 | tf_op jit(solution)/shard_map/ppermute | solution.py:19
  276.5 5.9 %collective-permute-start.16 = (f32[1,1,64,64]{3,2,1,0:T(8,128)S(1)}, f32[1,1,64,64]{3,2,1,0:T(8,128)S(1)}, u32[]{:S(2)}, u32[]{:S(2)}) collective-permute-start(f32[1,1,64,64]{3,2,1,0:T(8,128)S(1)} %get-tuple-element.61), channel_id=1, source_target_pairs={{4,0},{8,4},{12,8},{16,12},{20,16},{24,20},{28,24},{5,1},{9,5},{13... | collective-permute-start | bytes 49160 | tf_op jit(solution)/shard_map/ppermute | solution.py:22
  277.8 5.3 %collective-permute-start.17 = (f32[1,1,64,64]{3,2,1,0:T(8,128)S(1)}, f32[1,1,64,64]{3,2,1,0:T(8,128)S(1)}, u32[]{:S(2)}, u32[]{:S(2)}) collective-permute-start(f32[1,1,64,64]{3,2,1,0:T(8,128)S(1)} %get-tuple-element.62), channel_id=1, source_target_pairs={{0,4},{4,8},{8,12},{12,16},{16,20},{20,24},{24,28},{1,5},{5,9},{9,... | collective-permute-start | bytes 49160 | tf_op jit(solution)/shard_map/ppermute | solution.py:19
  304.2 13.2 %copy-start.3 = (f32[1,4,128,128]{3,2,1,0:T(8,128)S(1)}, f32[1,4,128,128]{3,2,1,0:T(8,128)}, u32[]{:S(2)}) copy-start(f32[1,4,128,128]{3,2,1,0:T(8,128)} %copy-done.2) | copy-start | bytes 786436
  305.1 4.3 %collective-permute-start.18 = (f32[1,1,64,64]{3,2,1,0:T(8,128)S(1)}, f32[1,1,64,64]{3,2,1,0:T(8,128)S(1)}, u32[]{:S(2)}, u32[]{:S(2)}) collective-permute-start(f32[1,1,64,64]{3,2,1,0:T(8,128)S(1)} %get-tuple-element.59), channel_id=1, source_target_pairs={{4,0},{8,4},{12,8},{16,12},{20,16},{24,20},{28,24},{5,1},{9,5},{13... | collective-permute-start | bytes 49160 | tf_op jit(solution)/shard_map/ppermute | solution.py:22
  306.4 3.9 collective-permute-start.19
  310.4 5.6 %collective-permute-start.20 = (f32[1,1,64,64]{3,2,1,0:T(8,128)S(1)}, f32[1,1,64,64]{3,2,1,0:T(8,128)S(1)}, u32[]{:S(2)}, u32[]{:S(2)}) collective-permute-start(f32[1,1,64,64]{3,2,1,0:T(8,128)S(1)} %get-tuple-element.57), channel_id=1, source_target_pairs={{4,0},{8,4},{12,8},{16,12},{20,16},{24,20},{28,24},{5,1},{9,5},{13... | collective-permute-start | bytes 49160 | tf_op jit(solution)/shard_map/ppermute | solution.py:22
  311.7 5.1 %collective-permute-start.21 = (f32[1,1,64,64]{3,2,1,0:T(8,128)S(1)}, f32[1,1,64,64]{3,2,1,0:T(8,128)S(1)}, u32[]{:S(2)}, u32[]{:S(2)}) collective-permute-start(f32[1,1,64,64]{3,2,1,0:T(8,128)S(1)} %get-tuple-element.58), channel_id=1, source_target_pairs={{0,4},{4,8},{8,12},{12,16},{16,20},{20,24},{24,28},{1,5},{5,9},{9,... | collective-permute-start | bytes 49160 | tf_op jit(solution)/shard_map/ppermute | solution.py:19
  317.5 6.3 %collective-permute-start.22 = (f32[1,1,128,128]{3,2,1,0:T(8,128)S(1)}, f32[1,1,128,128]{3,2,1,0:T(8,128)S(1)}, u32[]{:S(2)}, u32[]{:S(2)}) collective-permute-start(f32[1,1,128,128]{3,2,1,0:T(8,128)S(1)} %get-tuple-element.49), channel_id=1, source_target_pairs={{4,0},{8,4},{12,8},{16,12},{20,16},{24,20},{28,24},{5,1},{9,5},{13... | collective-permute-start | bytes 196616 | tf_op jit(solution)/shard_map/ppermute | solution.py:22
  318.8 5.9 %collective-permute-start.23 = (f32[1,1,128,128]{3,2,1,0:T(8,128)S(1)}, f32[1,1,128,128]{3,2,1,0:T(8,128)S(1)}, u32[]{:S(2)}, u32[]{:S(2)}) collective-permute-start(f32[1,1,128,128]{3,2,1,0:T(8,128)S(1)} %get-tuple-element.50), channel_id=1, source_target_pairs={{0,4},{4,8},{8,12},{12,16},{16,20},{20,24},{24,28},{1,5},{5,9},{9,... | collective-permute-start | bytes 196616 | tf_op jit(solution)/shard_map/ppermute | solution.py:19
  324.9 6.6 %collective-permute-start.24 = (f32[1,1,128,128]{3,2,1,0:T(8,128)S(1)}, f32[1,1,128,128]{3,2,1,0:T(8,128)S(1)}, u32[]{:S(2)}, u32[]{:S(2)}) collective-permute-start(f32[1,1,128,128]{3,2,1,0:T(8,128)S(1)} %get-tuple-element.47), channel_id=1, source_target_pairs={{4,0},{8,4},{12,8},{16,12},{20,16},{24,20},{28,24},{5,1},{9,5},{13... | collective-permute-start | bytes 196616 | tf_op jit(solution)/shard_map/ppermute | solution.py:22
  326.2 6.2 %collective-permute-start.25 = (f32[1,1,128,128]{3,2,1,0:T(8,128)S(1)}, f32[1,1,128,128]{3,2,1,0:T(8,128)S(1)}, u32[]{:S(2)}, u32[]{:S(2)}) collective-permute-start(f32[1,1,128,128]{3,2,1,0:T(8,128)S(1)} %get-tuple-element.48), channel_id=1, source_target_pairs={{0,4},{4,8},{8,12},{12,16},{16,20},{20,24},{24,28},{1,5},{5,9},{9,... | collective-permute-start | bytes 196616 | tf_op jit(solution)/shard_map/ppermute | solution.py:19
  337.9 6.6 %collective-permute-start.26 = (f32[1,1,256,256]{2,1,3,0:T(1,128)S(1)}, f32[1,1,256,256]{2,1,3,0:T(1,128)S(1)}, u32[]{:S(2)}, u32[]{:S(2)}) collective-permute-start(f32[1,1,256,256]{2,1,3,0:T(1,128)S(1)} %get-tuple-element.41), channel_id=1, source_target_pairs={{4,0},{8,4},{12,8},{16,12},{20,16},{24,20},{28,24},{5,1},{9,5},{13... | collective-permute-start | bytes 786440 | tf_op jit(solution)/shard_map/ppermute | solution.py:22
  339.2 6.5 %collective-permute-start.27 = (f32[1,1,256,256]{2,1,3,0:T(1,128)S(1)}, f32[1,1,256,256]{2,1,3,0:T(1,128)S(1)}, u32[]{:S(2)}, u32[]{:S(2)}) collective-permute-start(f32[1,1,256,256]{2,1,3,0:T(1,128)S(1)} %get-tuple-element.42), channel_id=1, source_target_pairs={{0,4},{4,8},{8,12},{12,16},{16,20},{20,24},{24,28},{1,5},{5,9},{9,... | collective-permute-start | bytes 786440 | tf_op jit(solution)/shard_map/ppermute | solution.py:19
  348.2 8.4 %collective-permute-start.28 = (f32[1,1,256,256]{2,1,3,0:T(1,128)S(1)}, f32[1,1,256,256]{2,1,3,0:T(1,128)S(1)}, u32[]{:S(2)}, u32[]{:S(2)}) collective-permute-start(f32[1,1,256,256]{2,1,3,0:T(1,128)S(1)} %get-tuple-element.39), channel_id=1, source_target_pairs={{4,0},{8,4},{12,8},{16,12},{20,16},{24,20},{28,24},{5,1},{9,5},{13... | collective-permute-start | bytes 786440 | tf_op jit(solution)/shard_map/ppermute | solution.py:22
  349.5 8.2 %collective-permute-start.29 = (f32[1,1,256,256]{2,1,3,0:T(1,128)S(1)}, f32[1,1,256,256]{2,1,3,0:T(1,128)S(1)}, u32[]{:S(2)}, u32[]{:S(2)}) collective-permute-start(f32[1,1,256,256]{2,1,3,0:T(1,128)S(1)} %get-tuple-element.40), channel_id=1, source_target_pairs={{0,4},{4,8},{8,12},{12,16},{16,20},{20,24},{24,28},{1,5},{5,9},{9,... | collective-permute-start | bytes 786440 | tf_op jit(solution)/shard_map/ppermute | solution.py:19
  359.9 12.9 %copy-start.1 = (f32[1,8,256,256]{2,1,3,0:T(8,128)}, f32[1,8,256,256]{2,1,3,0:T(8,128)S(1)}, u32[]{:S(2)}) copy-start(f32[1,8,256,256]{2,1,3,0:T(8,128)S(1)} %fusion.36) | copy-start | bytes 6291460
  360.2 9.1 %collective-permute-start.30 = (f32[1,1,256,256]{2,1,3,0:T(1,128)S(1)}, f32[1,1,256,256]{2,1,3,0:T(1,128)S(1)}, u32[]{:S(2)}, u32[]{:S(2)}) collective-permute-start(f32[1,1,256,256]{2,1,3,0:T(1,128)S(1)} %get-tuple-element.37), channel_id=1, source_target_pairs={{4,0},{8,4},{12,8},{16,12},{20,16},{24,20},{28,24},{5,1},{9,5},{13... | collective-permute-start | bytes 786440 | tf_op jit(solution)/shard_map/ppermute | solution.py:22
  361.5 8.3 %collective-permute-start.31 = (f32[1,1,256,256]{2,1,3,0:T(1,128)S(1)}, f32[1,1,256,256]{2,1,3,0:T(1,128)S(1)}, u32[]{:S(2)}, u32[]{:S(2)}) collective-permute-start(f32[1,1,256,256]{2,1,3,0:T(1,128)S(1)} %get-tuple-element.38), channel_id=1, source_target_pairs={{0,4},{4,8},{8,12},{12,16},{16,20},{20,24},{24,28},{1,5},{5,9},{9,... | collective-permute-start | bytes 786440 | tf_op jit(solution)/shard_map/ppermute | solution.py:19
where the time goes:
time: 409 us; the launch traced here: 407 us
  local copies, waits for them, and re-layouts  174 us (43%)
  starting transfers between devices  100 us (24%)
  other arithmetic  68.6 us (17%)
  blocking collectives  46.6 us (11%)
  waiting for transfers between devices  9.63 us (2%)
  between operations  8.59 us (2%)
    reshape x2, local copies, waits for them, and re-layouts, restrict(): field.reshape(pairs, zsize // 2, 2, ysize // 2, 2, xsize // 2, 2)  154 us
    ppermute x16, starting transfers between devices, with_halo(): lax.ppermute(lax.slice_in_dim(block, block.shape[dim] - width, None, axis...  79.6 us
    reduce_sum x4, other arithmetic, restrict(): field.reshape(pairs, zsize // 2, 2, ysize // 2, 2, xsize // 2, 2)  48.5 us
    ppermute x16, starting transfers between devices, with_halo(): lax.ppermute(lax.slice_in_dim(block, 0, width, axis=dim), axis, backward)  20.7 us
    psum x1, blocking collectives, per_device(): lax.psum((jnp.sum(final * final, axis=(1, 2, 3)), jnp.sum(density * poten...  18.9 us
    all_gather x1, blocking collectives, coarsest(): gathered = lax.all_gather(source, 'gz', axis=1, tiled=True)  17.4 us
    psum x1, blocking collectives, per_device(): energy = lax.psum(partial_energy, 'pair').reshape(1)  10.4 us
    ppermute x16, waiting for transfers between devices, with_halo(): lax.ppermute(lax.slice_in_dim(block, block.shape[dim] - width, None, axis...  9.58 us
  transfers between devices with their start and end apart: 32, of which 11 were waited for; matrix products, arithmetic and copies ran while one was open for 52% of the time, Pallas kernels for 0%

commit v1 on v0

v1 whole, which is shorter than its diff:
```python
import functools

import jax
import jax.numpy as jnp
from jax import lax
from jax.experimental import pallas as pl
from jax.experimental.pallas import tpu as pltpu
from jax.sharding import PartitionSpec as P

LANES = 128
PAD = 8
SWEEPS = 8
ROWS = 32
THIRD = 1.0 / 3.0
NINTH = 1.0 / 9.0
F32 = jnp.float32
BF16 = jnp.bfloat16
ANY = pl.BlockSpec(memory_space=pl.ANY)
VMEM = pl.BlockSpec(memory_space=pltpu.VMEM)
SMEM = pl.BlockSpec(memory_space=pltpu.SMEM)


def scale(level):
    return 4.0**level / 9.0


def iota(shape, dim):
    return lax.broadcasted_iota(jnp.int32, shape, dim)


def split_dot(value, matrix):
    high = value.astype(BF16)
    low = (value - high.astype(F32)).astype(BF16)
    return jnp.dot(high, matrix, preferred_element_type=F32) + jnp.dot(low, matrix, preferred_element_type=F32)


def to_bf16(mask, value=1.0):
    return jnp.where(mask, value, 0.0).astype(BF16)


def neighbours(ref, z, row, rows):
    parts = ref.shape[1]
    centre = [ref[z, h, pl.ds(PAD + row, rows), :] for h in range(parts)]
    lane = iota((rows, LANES), 1)
    after = [pltpu.roll(c, 1, 1) for c in centre]
    before = [pltpu.roll(c, LANES - 1, 1) for c in centre]
    sums = []
    for h in range(parts):
        total = ref[z, h, pl.ds(PAD + row - 1, rows), :] + ref[z, h, pl.ds(PAD + row + 1, rows), :]
        total += ref[z - 1, h, pl.ds(PAD + row, rows), :] + ref[z + 1, h, pl.ds(PAD + row, rows), :]
        total += jnp.where(lane == 0, after[h - 1] if h else 0.0, after[h])
        total += jnp.where(lane == LANES - 1, before[h + 1] if h + 1 < parts else 0.0, before[h])
        sums.append(total)
    return centre, sums


def zero_pads(ref, rows):
    blank = jnp.zeros((PAD, LANES), F32)

    def plane(z, _):
        for h in range(ref.shape[1]):
            ref[z, h, pl.ds(0, PAD), :] = blank
            ref[z, h, pl.ds(PAD + rows, PAD), :] = blank
        return 0

    lax.fori_loop(0, ref.shape[0], plane, 0)


def zero_planes(ref, planes, rows):
    for z in planes:
        for h in range(ref.shape[1]):
            ref[z, h, pl.ds(PAD, rows), :] = jnp.zeros((rows, LANES), F32)


def apply_planes(dst, src, first, last, shift, rows):
    def plane(z, _):
        for row in range(0, rows, ROWS):
            centre, sums = neighbours(src, z, row, ROWS)
            for h in range(len(centre)):
                dst[z + shift, h, pl.ds(PAD + row, ROWS), :] = centre[h] * THIRD + sums[h] * NINTH
        return 0

    lax.fori_loop(first, last, plane, 0)


def restrict_pair(ref, z, rows, matrices):
    total = None
    half = rows // 2
    for h in range(ref.shape[1]):

        def at(plane, offset):
            return ref[plane, h, pl.ds(PAD + offset, half, stride=2), :]

        inner = [at(z, k) + at(z + 1, k) for k in (-1, 0, 1, 2)]
        pair = inner[1] + inner[2]
        outer = inner[0] + inner[3] + (at(z - 1, 0) + at(z - 1, 1)) + (at(z + 2, 0) + at(z + 2, 1))
        part = split_dot(pair, matrices[0][h]) + split_dot(outer, matrices[1][h])
        total = part if total is None else total + part
    return total * (NINTH / 8.0)


def restrict_matrices(width, parts, out_shift=0):
    stencil, plain = [], []
    for h in range(parts):
        row = iota((LANES, LANES), 0) + h * LANES
        column = iota((LANES, LANES), 1) - out_shift
        inside = (column >= 0) & (column < width // 2)
        own = (row >> 1) == column
        beside = (row == 2 * column - 1) | (row == 2 * column + 2)
        stencil.append(jnp.where(inside & own, 6.0, jnp.where(inside & beside, 1.0, 0.0)).astype(BF16))
        plain.append(to_bf16(inside & own))
    return stencil, plain


def fine_kernel(size, orbitals, pair_index, own_a, own_b, coarse_a, coarse_b, left, right, source, smooth, sums, in_sem, out_sem):
    planes, rows = left.shape[0], left.shape[1]
    parts = source.shape[1]
    half = planes // 2
    me = lax.axis_index("gz")
    odd = me % 2

    def fetch(z):
        return [
            pltpu.make_async_copy(orbitals.at[pair_index[0, k], z], buffer.at[z], in_sem.at[k, z])
            for k, buffer in ((0, left), (1, right))
        ]

    for z in range(planes):
        for copy in fetch(z):
            copy.start()
    zero_pads(source, rows)
    zero_pads(smooth, rows)
    zero_planes(source, (0, planes + 1), rows)
    zero_planes(smooth, (0, 1, planes + 2, planes + 3), rows)
    matrices = restrict_matrices(parts * LANES, parts)

    for z in range(planes):
        for copy in fetch(z):
            copy.wait()

        for row in range(0, rows, 2 * ROWS):
            for h in range(parts):
                here = (z, pl.ds(row, 2 * ROWS), pl.ds(h * LANES, LANES))
                source[z + 1, h, pl.ds(PAD + row, 2 * ROWS), :] = left[here].astype(F32) * right[here].astype(F32)

    def keep(start, target, k):
        return pltpu.make_async_copy(source.at[pl.ds(start, half), :, pl.ds(PAD, rows), :], target, out_sem.at[k])

    kept = [keep(1 + half * (1 - odd), own_a, 0), keep(1 + half * odd, own_b, 1)]

    apply_planes(smooth, source, 1, planes + 1, 1, rows)

    def spread(target, origin):
        for h in range(parts):
            smooth[target, h, pl.ds(PAD, rows), :] = source[origin, h, pl.ds(PAD, rows), :] * NINTH

    @pl.when(me > 0)
    def _():
        spread(1, 1)

    @pl.when(me < size - 1)
    def _():
        spread(planes + 2, planes)

    for copy in kept:
        copy.start()

    def coarse(q, _):
        sums[q + 1] = restrict_pair(smooth, 2 * q + 2, rows, matrices)
        return 0

    lax.fori_loop(0, half, coarse, 0)
    low = [smooth[1, h, pl.ds(PAD + k, rows // 2, stride=2), :] for h in range(parts) for k in (-1, 0, 1, 2)]
    low_z = [smooth[2, h, pl.ds(PAD + k, rows // 2, stride=2), :] for h in range(parts) for k in (0, 1)]
    high = [smooth[planes + 2, h, pl.ds(PAD + k, rows // 2, stride=2), :] for h in range(parts) for k in (-1, 0, 1, 2)]
    high_z = [smooth[planes + 1, h, pl.ds(PAD + k, rows // 2, stride=2), :] for h in range(parts) for k in (0, 1)]

    def edge(inner, far):
        total = None
        for h in range(parts):
            i = inner[4 * h : 4 * h + 4]
            part = split_dot(i[1] + i[2], matrices[0][h])
            part += split_dot(i[0] + i[3] + (far[2 * h] + far[2 * h + 1]), matrices[1][h])
            total = part if total is None else total + part
        return total * (NINTH / 8.0)

    sums[0] = jnp.where(me > 0, edge(low, low_z), 0.0)
    sums[half + 1] = jnp.where(me < size - 1, edge(high, high_z), 0.0)

    three = (half + 2) // 2

    @pl.when(odd == 0)
    def _():
        coarse_a[...] = sums[pl.ds(three, three)]
        coarse_b[...] = sums[pl.ds(0, three)]

    @pl.when(odd == 1)
    def _():
        coarse_a[...] = sums[pl.ds(0, three)]
        coarse_b[...] = sums[pl.ds(three, three)]

    for copy in kept:
        copy.wait()


def middle_kernel(size, sent_a, sent_b, got_a, got_b, whole, next_a, next_b, packed, field, smooth):
    rows = sent_a.shape[1]
    planes = whole.shape[0] - 4
    me = lax.axis_index("gz")
    zero_pads(field, rows)
    zero_pads(smooth, rows)
    first, second = restrict_matrices(LANES, 1), restrict_matrices(LANES, 1, LANES // 2)

    def gather(own, low, high):
        centre = pl.ds(PAD, rows)
        n = planes
        for plane in range(n + 4):
            value = None
            if 1 <= plane <= n + 2:
                source, at = own[(plane - 1) // ((n + 2) // 2)], (plane - 1) % ((n + 2) // 2)
                value = source[at]
            if plane < 3:
                value = low[plane] if value is None else value + low[plane]
            if plane > n:
                value = high[plane - n - 1] if value is None else value + high[plane - n - 1]
            whole[plane] = value
            field[plane, 0, centre, :] = value

    @pl.when(me % 2 == 0)
    def _():
        gather((sent_b, sent_a), got_b, got_a)

    @pl.when(me % 2 == 1)
    def _():
        gather((sent_a, sent_b), got_a, got_b)

    apply_planes(smooth, field, jnp.where(me == 0, 2, 1), jnp.where(me == size - 1, planes + 2, planes + 3), 0, rows)

    @pl.when(me == 0)
    def _():
        zero_planes(smooth, (1,), rows)

    @pl.when(me == size - 1)
    def _():
        zero_planes(smooth, (planes + 2,), rows)

    packed[...] = restrict_pair(smooth, 2, rows, first) + restrict_pair(smooth, 4, rows, second)

    up, down = whole[pl.ds(1, 3)], whole[pl.ds(planes, 3)]

    @pl.when(me % 2 == 0)
    def _():
        next_a[...] = up
        next_b[...] = down

    @pl.when(me % 2 == 1)
    def _():
        next_a[...] = down
        next_b[...] = up


def packed_apply(ref, block, rows):
    centre = ref[block, pl.ds(PAD, rows), :]
    lane = iota((rows, LANES), 1)
    half = LANES // 2
    total = ref[block, pl.ds(PAD - 1, rows), :] + ref[block, pl.ds(PAD + 1, rows), :]
    other = jnp.where(lane >= half, ref[block - 1, pl.ds(PAD, rows), :], ref[block + 1, pl.ds(PAD, rows), :])
    total += pltpu.roll(centre + other, half, 1)
    total += jnp.where((lane & (half - 1)) == 0, 0.0, pltpu.roll(centre, 1, 1))
    total += jnp.where((lane & (half - 1)) == half - 1, 0.0, pltpu.roll(centre, LANES - 1, 1))
    return centre * THIRD + total * NINTH


def last_apply(ref, plane, rows, width):
    centre = ref[plane, pl.ds(PAD, rows), :]
    lane = iota((rows, LANES), 1)
    total = ref[plane, pl.ds(PAD - 1, rows), :] + ref[plane, pl.ds(PAD + 1, rows), :]
    total += ref[plane - 1, pl.ds(PAD, rows), :] + ref[plane + 1, pl.ds(PAD, rows), :]
    total += pltpu.roll(centre, 1, 1) + pltpu.roll(centre, LANES - 1, 1)
    return jnp.where(lane < width, centre * THIRD + total * NINTH, 0.0)


def coarse_levels(size, source, result, blocks, smooth, bottom, spare):
    rows = source.shape[1] - 2 * PAD
    half = rows // 2
    width = LANES // 4
    c2, c3 = scale(2), scale(3)
    row, column = iota((LANES, LANES), 0), iota((LANES, LANES), 1)
    gather = to_bf16(((row & (LANES // 2 - 1)) >> 1) == column)
    scatter = to_bf16(((column & (LANES // 2 - 1)) >> 1) == row)
    centre = pl.ds(PAD, rows)
    inner = pl.ds(PAD, half)

    for b in range(1, size + 1):
        smooth[b, centre, :] = packed_apply(source, b, rows)
    for b in range(1, size + 1):
        spare[b] = packed_apply(smooth, b, rows)
    for b in range(1, size + 1):
        pairs = spare[b, pl.ds(0, half, stride=2), :] + spare[b, pl.ds(1, half, stride=2), :]
        value = split_dot(pairs, gather) * (c3 / 8.0)
        bottom[2, b, inner, :] = value
        bottom[0, b, inner, :] = value
    now = 0
    for _ in range(SWEEPS - 1):
        for b in range(1, size + 1):
            bottom[1 - now, b, inner, :] = last_apply(bottom.at[now], b, half, width) + bottom[2, b, inner, :]
        now = 1 - now
    for b in range(1, size + 1):
        value = split_dot(bottom[now, b, inner, :], scatter)
        spare[b, pl.ds(0, half, stride=2), :] = value
        spare[b, pl.ds(1, half, stride=2), :] = value
    for b in range(1, size + 1):
        source_b = source[b, centre, :] * c2
        blocks[b, centre, :] = source_b + smooth[b, centre, :] * c2 + spare[b]
    for b in range(1, size + 1):
        smooth[b, centre, :] = packed_apply(blocks, b, rows) + source[b, centre, :] * c2
    for b in range(1, size + 1):
        result[b, centre, :] = packed_apply(smooth, b, rows) + source[b, centre, :] * c2


def last_kernel(
    size, partners, cells, own_a, own_b, got_a, got_b, whole, next_a, next_b, *rest
):
    arrived = rest[: len(partners)]
    weight, potential, sums = rest[len(partners) : len(partners) + 3]
    scratch = rest[len(partners) + 3 :]
    (field, first, second, third, grown, mid, mid_first, mid_second, mid_third, mid_grown) = scratch[:10]
    (low_source, low_result, low_blocks, low_smooth, bottom, spare, in_sem, out_sem) = scratch[10:]
    parts, rows = own_a.shape[1], own_a.shape[2]
    half = own_a.shape[0]
    planes = 2 * half
    mid_rows = whole.shape[1]
    mid_planes = whole.shape[0] - 4
    low_rows = arrived[0].shape[0]
    me = lax.axis_index("gz")
    odd = me % 2
    is_first, is_last = me == 0, me == size - 1

    def bring(k, origin, plane):
        return pltpu.make_async_copy(origin, field.at[pl.ds(plane, half), :, pl.ds(PAD, rows), :], in_sem.at[k])

    copies = [
        bring(0, own_a, half + half * (1 - odd)),
        bring(1, own_b, half + half * odd),
        bring(2, got_a, 3 * half * (1 - odd)),
        bring(3, got_b, 3 * half * odd),
    ]
    for copy in copies:
        copy.start()

    blank = jnp.zeros((PAD, LANES), F32)
    for ref in (field, first, second, third):
        zero_pads(ref, rows)
    for ref in (mid, mid_first, mid_second):
        zero_pads(ref, mid_rows)
    for ref in (low_source, low_blocks, low_smooth):
        for b in range(size + 2):
            ref[b, pl.ds(0, PAD), :] = blank
            ref[b, pl.ds(PAD + low_rows, PAD), :] = blank
        for b in (0, size + 1):
            ref[b, pl.ds(PAD, low_rows), :] = jnp.zeros((low_rows, LANES), F32)
    for k in range(2):
        for b in range(size + 2):
            bottom[k, b, pl.ds(0, PAD), :] = blank
            bottom[k, b, pl.ds(PAD + low_rows // 2, PAD), :] = blank
        for b in (0, size + 1):
            bottom[k, b] = jnp.zeros(bottom.shape[2:], F32)
    for b in (0, size + 1):
        low_result[b, pl.ds(PAD, low_rows), :] = jnp.zeros((low_rows, LANES), F32)

    for partner, ref in zip(partners, arrived):
        low_source[jnp.bitwise_xor(me, partner) + 1, pl.ds(PAD, low_rows), :] = ref[...]

    coarse_levels(size, low_source, low_result, low_blocks, low_smooth, bottom, spare)

    edge = 3
    middle = pl.ds(PAD, mid_rows)
    for plane in range(mid_planes + 4):
        mid[edge + plane, 0, middle, :] = whole[plane]

    def sides(low, high):
        for k in range(edge):
            mid[k, 0, middle, :] = low[k]
            mid[edge + mid_planes + 4 + k, 0, middle, :] = high[k]

    @pl.when(odd == 0)
    def _():
        sides(next_b, next_a)

    @pl.when(odd == 1)
    def _():
        sides(next_a, next_b)

    row, column = iota((LANES, LANES), 0), iota((LANES, LANES), 1)
    for k in range(3):
        block = low_result[me + k, pl.ds(PAD, low_rows), :]
        for side in range(2):
            matrix = to_bf16((column >> 1) + side * (LANES // 2) == row)
            value = split_dot(block, matrix)
            mid_grown[2 * k + side, 0, pl.ds(0, low_rows, stride=2), :] = value
            mid_grown[2 * k + side, 0, pl.ds(1, low_rows, stride=2), :] = value

    def start(dst, src, grown_ref, first_plane, last_plane, shift, offset, level, n):
        c = scale(level)

        def plane(z, _):
            for r in range(0, n, ROWS):
                centre, total = neighbours(src, z, r, ROWS)
                for h in range(len(centre)):
                    value = centre[h] * (c * (1.0 + THIRD)) + total[h] * (c * NINTH)
                    dst[z + shift, h, pl.ds(PAD + r, ROWS), :] = value + grown_ref[(z + offset) >> 1, h, pl.ds(r, ROWS), :]
            return 0

        lax.fori_loop(first_plane, last_plane, plane, 0)

    def again(dst, src, source, first_plane, last_plane, shift, offset, level, n):
        c = scale(level)

        def plane(z, _):
            for r in range(0, n, ROWS):
                centre, total = neighbours(src, z, r, ROWS)
                for h in range(len(centre)):
                    value = centre[h] * THIRD + total[h] * NINTH
                    dst[z + shift, h, pl.ds(PAD + r, ROWS), :] = value + source[z + offset, h, pl.ds(PAD + r, ROWS), :] * c
            return 0

        lax.fori_loop(first_plane, last_plane, plane, 0)

    def blank_outside(ref, halo, inside, n):
        @pl.when(is_first)
        def _():
            zero_planes(ref, range(halo), n)

        @pl.when(is_last)
        def _():
            zero_planes(ref, range(halo + inside, 2 * halo + inside), n)

    def span(halo, inside):
        return jnp.where(is_first, halo, 0), jnp.where(is_last, halo + inside, 2 * halo + inside)

    n = mid_planes
    low, high = span(4, n)
    start(mid_first, mid, mid_grown, low + 1, high + 1, -1, -1, 1, mid_rows)
    blank_outside(mid_first, 4, n, mid_rows)
    low, high = span(3, n)
    again(mid_second, mid_first, mid, low + 1, high + 1, -1, 1, 1, mid_rows)
    blank_outside(mid_second, 3, n, mid_rows)
    low, high = span(2, n)

    spread = [to_bf16((column + h * LANES) >> 1 == row) for h in range(parts)]
    c1 = scale(1)

    def correct(z, _):
        for r in range(0, mid_rows, ROWS):
            centre, total = neighbours(mid_second, z + 1, r, ROWS)
            mid_third[pl.ds(r, ROWS), :] = centre[0] * THIRD + total[0] * NINTH + mid[z + 3, 0, pl.ds(PAD + r, ROWS), :] * c1
        value = mid_third[...]
        for h in range(parts):
            wide = split_dot(value, spread[h])
            grown[z, h, pl.ds(0, mid_rows, stride=2), :] = wide
            grown[z, h, pl.ds(1, mid_rows, stride=2), :] = wide
        return 0

    lax.fori_loop(low, high, correct, 0)

    for copy in copies:
        copy.wait()

    n = planes
    low, high = span(3, n)
    start(first, field, grown, low + 1, high + 1, -1, 0, 0, rows)
    blank_outside(first, 3, n, rows)
    low, high = span(2, n)
    again(second, first, field, low + 1, high + 1, -1, 1, 0, rows)
    blank_outside(second, 2, n, rows)
    low, high = span(1, n)
    again(third, second, field, low + 1, high + 1, -1, 2, 0, rows)
    blank_outside(third, 1, n, rows)

    def give(z, h):
        target = potential.at[0, z, :, pl.ds(h * LANES, LANES)]
        return pltpu.make_async_copy(third.at[z + 1, h, pl.ds(PAD, rows), :], target, out_sem.at[z, h])

    for z in range(n):
        for h in range(parts):
            give(z, h).start()

    def final(z, totals):
        squares, products = totals
        for r in range(0, rows, ROWS):
            centre, total = neighbours(third, z + 1, r, ROWS)
            for h in range(parts):
                f = field[z + half, h, pl.ds(PAD + r, ROWS), :]
                rest_of = f - 6.0 * centre[h] + total[h]
                squares += jnp.sum((rest_of * rest_of).reshape(ROWS // 8, 8, LANES), axis=0)
                products += jnp.sum((f * centre[h]).reshape(ROWS // 8, 8, LANES), axis=0)
        return squares, products

    squares, products = lax.fori_loop(0, n, final, (jnp.zeros((8, LANES), F32),) * 2)
    products = products * (weight[0] * (-0.5 / cells))
    both = jnp.concatenate([jnp.sum(squares, axis=0, keepdims=True), jnp.sum(products, axis=0, keepdims=True)], axis=0)
    sums[...] = jnp.broadcast_to(both[None], sums.shape)
    for z in range(n):
        for h in range(parts):
            give(z, h).wait()


def exchange(value, pairs):
    return lax.ppermute(value, "gz", [move for a, b in pairs for move in ((a, b), (b, a))])


def params(mib):
    return pltpu.CompilerParams(vmem_limit_bytes=mib << 20)


def per_device(orbitals, pair_index, pair_weight):
    size = lax.axis_size("gz")
    groups = lax.axis_size("pair")
    _, planes, rows, columns = orbitals.shape
    parts = columns // LANES
    assert planes == 8 and columns == 2 * LANES and rows % (4 * ROWS) == 0 and pair_index.shape[0] == 1 and size % 2 == 0
    half, quarter = planes // 2, planes // 4
    mid_rows, low_rows = rows // 2, rows // 4
    tall, mid_tall, low_tall = rows + 2 * PAD, mid_rows + 2 * PAD, low_rows + 2 * PAD
    inner = [(i, i + 1) for i in range(0, size, 2)]
    outer = [(i, i + 1) for i in range(1, size - 1, 2)]

    def shape(*dims):
        return jax.ShapeDtypeStruct(dims, F32)

    def scratch(*dims):
        return pltpu.VMEM(dims, F32)

    three = (half + 2) // 2
    own_a, own_b, coarse_a, coarse_b = pl.pallas_call(
        functools.partial(fine_kernel, size),
        out_shape=[shape(half, parts, rows, LANES)] * 2 + [shape(three, mid_rows, LANES)] * 2,
        in_specs=[ANY, SMEM],
        out_specs=[ANY, ANY, VMEM, VMEM],
        scratch_shapes=[
            pltpu.VMEM((planes, rows, columns), orbitals.dtype),
            pltpu.VMEM((planes, rows, columns), orbitals.dtype),
            scratch(planes + 2, parts, tall, LANES),
            scratch(planes + 4, parts, tall, LANES),
            scratch(half + 2, mid_rows, LANES),
            pltpu.SemaphoreType.DMA((2, planes)),
            pltpu.SemaphoreType.DMA((2,)),
        ],
        compiler_params=params(24),
        name="fine",
    )(orbitals, pair_index)

    coarse_got_a = exchange(coarse_a, inner)
    coarse_got_b = exchange(coarse_b, outer)
    own_got_a = exchange(own_a, inner)
    own_got_b = exchange(own_b, outer)

    whole, next_a, next_b, packed = pl.pallas_call(
        functools.partial(middle_kernel, size),
        out_shape=[shape(half + 4, mid_rows, LANES)] + [shape(3, mid_rows, LANES)] * 2 + [shape(low_rows, LANES)],
        in_specs=[VMEM] * 4,
        out_specs=[VMEM] * 4,
        scratch_shapes=[scratch(half + 4, 1, mid_tall, LANES)] * 2,
        compiler_params=params(8),
        name="middle",
    )(coarse_a, coarse_b, coarse_got_a, coarse_got_b)

    partners = list(range(0, size, 2))
    arrived = [packed] + [exchange(packed, [(i, i ^ k) for i in range(size) if i < i ^ k]) for k in partners[1:]]
    arrived += [exchange(value, inner) for value in arrived]
    partners += [k ^ 1 for k in partners]
    next_got_a = exchange(next_a, inner)
    next_got_b = exchange(next_b, outer)

    cells = planes * size * rows * columns
    potential, sums = pl.pallas_call(
        functools.partial(last_kernel, size, tuple(partners), cells),
        out_shape=[shape(1, planes, rows, columns), shape(size * groups, 2, LANES)],
        in_specs=[ANY] * 4 + [VMEM] * (3 + len(partners)) + [SMEM],
        out_specs=[ANY, VMEM],
        scratch_shapes=[
            scratch(planes + 8, parts, tall, LANES),
            scratch(planes + 6, parts, tall, LANES),
            scratch(planes + 4, parts, tall, LANES),
            scratch(planes + 2, parts, tall, LANES),
            scratch(half + 4, parts, rows, LANES),
            scratch(half + 10, 1, mid_tall, LANES),
            scratch(half + 8, 1, mid_tall, LANES),
            scratch(half + 6, 1, mid_tall, LANES),
            scratch(mid_rows, LANES),
            scratch(6, 1, mid_rows, LANES),
            scratch(size + 2, low_tall, LANES),
            scratch(size + 2, low_tall, LANES),
            scratch(size + 2, low_tall, LANES),
            scratch(size + 2, low_tall, LANES),
            scratch(3, size + 2, low_rows // 2 + 2 * PAD, LANES),
            scratch(size + 2, low_rows, LANES),
            pltpu.SemaphoreType.DMA((4,)),
            pltpu.SemaphoreType.DMA((planes, parts)),
        ],
        compiler_params=params(32),
        name="last",
    )(own_a, own_b, own_got_a, own_got_b, whole, next_got_a, next_got_b, *arrived, pair_weight)

    everyone = lax.all_to_all(sums, ("gz", "pair"), 0, 0).reshape(size, groups, 2, LANES)
    mine = iota((size, groups, LANES), 1) == lax.axis_index("pair")
    squares = jnp.sum(jnp.where(mine, everyone[:, :, 0], 0.0))
    energy = jnp.sum(everyone[:, :, 1])
    return (potential, jnp.sqrt(squares / cells).reshape(1), energy.reshape(1))


def solution(mesh):
    return jax.shard_map(
        per_device,
        mesh=mesh,
        in_specs=(P(None, "gz", None, None), P("pair", None), P("pair")),
        out_specs=(P("pair", "gz", None, None), P("pair"), P()),
        check_vma=False,
    )
```

time: 409 us -> 93.7 us (0.23)
  local copies, waits for them, and re-layouts: 174 us -> 14.7 us
  other arithmetic: 68.6 us -> 1.32 us
  starting transfers between devices: 100 us -> 33.5 us
  blocking collectives: 46.6 us -> 0 us
  Pallas kernels: 0 us -> 23.8 us
  waiting for transfers between devices: 9.63 us -> 16.4 us
  between operations: 8.59 us -> 3.21 us
    reshape x2 -> x0, local copies, waits for them, and re-layouts: 154 us -> none  [restrict(): field.reshape(pairs, zsize // 2, 2, ysize // 2, 2, xsize // 2, 2)]
    ppermute x32 -> x13, starting transfers between devices: 100 us -> 27.6 us  [exchange(): lax.ppermute(value, 'gz', [move for a, b in pairs for move in ((a, b), (b...]
    reduce_sum x5 -> x2, other arithmetic: 51.5 us -> 1.31 us  [the longest x1 0.67 us: per_device(): squares = jnp.sum(jnp.where(mine, everyone[:, :, 0], 0.0))]
    psum x2 -> x0, blocking collectives: 29.3 us -> none  [the longest x1 18.9 us: per_device(): lax.psum((jnp.sum(final * final, axis=(1, 2, 3)), jnp.sum(density * poten...]
    pallas_call x0 -> x3, Pallas kernels: none -> 23.8 us  [the longest x1 15 us: per_device(): pl.pallas_call(functools.partial(last_kernel, size, tuple(partners), cell...]
    all_gather x1 -> x0, blocking collectives: 17.4 us -> none  [coarsest(): gathered = lax.all_gather(source, 'gz', axis=1, tiled=True)]
    add x20 -> x0, other arithmetic: 10.7 us -> none  [the longest x9 7.67 us: sweep(): field + (source - apply_op(field, level)) * (relax * 4.0 ** level / 6.0)]
    unnamed x11 -> x34, local copies, waits for them, and re-layouts: 4.94 us -> 14.7 us
  transfers between devices with their start and end apart: 32 -> 14, of which waited for: 11 -> 8; matrix products, arithmetic and copies ran while one was open for 52% -> 0% of each run, Pallas kernels for 0% -> 2%
where the time goes in v1:
time: 93.7 us; the launch traced here: 92.9 us
  starting transfers between devices  33.5 us (36%)
  Pallas kernels  23.8 us (25%)
  waiting for transfers between devices  16.4 us (18%)
  local copies, waits for them, and re-layouts  14.7 us (16%)
  between operations  3.21 us (3%)
  other arithmetic  1.32 us (1%)
    ppermute x13, starting transfers between devices, exchange(): lax.ppermute(value, 'gz', [move for a, b in pairs for move in ((a, b), (b...  27.6 us
    pallas_call x1, Pallas kernels, per_device(): pl.pallas_call(functools.partial(last_kernel, size, tuple(partners), cell...  15 us
    unnamed x34, local copies, waits for them, and re-layouts  14.7 us
    ppermute x13, waiting for transfers between devices, exchange(): lax.ppermute(value, 'gz', [move for a, b in pairs for move in ((a, b), (b...  9.08 us
    all_to_all x1, waiting for transfers between devices, per_device(): lax.all_to_all(sums, ('gz', 'pair'), 0, 0).reshape(size, groups, 2, LANES)  7.28 us
    pallas_call x1, Pallas kernels, per_device(): pl.pallas_call(functools.partial(fine_kernel, size), out_shape=[shape(hal...  7.06 us
    all_to_all x1, starting transfers between devices, per_device(): lax.all_to_all(sums, ('gz', 'pair'), 0, 0).reshape(size, groups, 2, LANES)  5.97 us
  transfers between devices with their start and end apart: 14, of which 8 were waited for; matrix products, arithmetic and copies ran while one was open for 0% of the time, Pallas kernels for 2%

profile of v1, /device:TPU:0, one launch (start us, length us, event | category | flops | bytes accessed | tf_op | source)
XLA Modules:
  0.0 92.9 jit_solution(3607518084993389550)
XLA Ops:
  0.6 3.4 %copy-done = bf16[8,8,256,256]{3,2,1,0:T(8,128)(2,1)S(1)} copy-done((bf16[8,8,256,256]{3,2,1,0:T(8,128)(2,1)S(1)}, bf16[8,8,256,256]{3,2,1,0:T(8,128)(2,1)}, u32[]{:S(2)}) %copy-start) | copy-done | bytes 8388632
  4.0 0.7 copy-done.16
  4.7 7.1 %fine.1 = (f32[4,2,256,128]{3,2,1,0:T(8,128)S(1)}, f32[4,2,256,128]{3,2,1,0:T(8,128)S(1)}, f32[3,128,128]{2,1,0:T(8,128)S(1)}, f32[3,128,128]{2,1,0:T(8,128)S(1)}) custom-call(bf16[8,8,256,256]{3,2,1,0:T(8,128)(2,1)S(1)} %copy-done, s32[1,2]{1,0:T(1,128)S(1)} %copy-done.16), custom_call_target="tpu_custom_call" | custom-call | tf_op jit(solution)/shard_map/fine/pallas_call | solution.py:535
  11.7 0.6 collective-permute-start
  12.3 1.6 %collective-permute-start.1 = (f32[4,2,256,128]{3,2,1,0:T(8,128)S(1)}, f32[4,2,256,128]{3,2,1,0:T(8,128)}, u32[]{:S(2)}, u32[]{:S(2)}) collective-permute-start(f32[4,2,256,128]{3,2,1,0:T(8,128)S(1)} %get-tuple-element.14.own_b), channel_id=1, source_target_pairs={{4,8},{8,4},{12,16},{16,12},{20,24},{24,20},{5,9},{9,5},{13,17},{1... | collective-permute-start | bytes 3145736 | tf_op jit(solution)/shard_map/ppermute | solution.py:509
  14.0 3.0 %collective-permute-start.2 = (f32[3,128,128]{2,1,0:T(8,128)S(1)}, f32[3,128,128]{2,1,0:T(8,128)S(1)}, u32[]{:S(2)}, u32[]{:S(2)}) collective-permute-start(f32[3,128,128]{2,1,0:T(8,128)S(1)} %get-tuple-element.15.sent_a), channel_id=1, source_target_pairs={{0,4},{4,0},{8,12},{12,8},{16,20},{20,16},{24,28},{28,24},{1,5},{5... | collective-permute-start | bytes 589832 | tf_op jit(solution)/shard_map/ppermute | solution.py:509
  17.0 0.7 collective-permute-start.3
  17.7 0.4 collective-permute-done.2.got_a
  18.1 0.0 collective-permute-done.3.got_b
  18.1 1.7 %middle.1 = (f32[8,128,128]{2,1,0:T(8,128)S(1)}, f32[3,128,128]{2,1,0:T(8,128)}, f32[3,128,128]{2,1,0:T(8,128)}, f32[64,128]{1,0:T(8,128)S(1)}) custom-call(f32[3,128,128]{2,1,0:T(8,128)S(1)} %get-tuple-element.15.sent_a, f32[3,128,128]{2,1,0:T(8,128)S(1)} %get-tuple-element.16.sent_b, f32[3,128,128]{2,1,0:T(8,128)S(1)} %collective-permute-done.2.got_a, ...), custom_call_target="tpu_custom_call" | custom-call | tf_op jit(solution)/shard_map/middle/pallas_call | solution.py:558
  19.8 0.8 copy-done.1
  20.6 15.1 %collective-permute-start.6 = (f32[64,128]{1,0:T(8,128)S(1)}, f32[64,128]{1,0:T(8,128)S(1)}, u32[]{:S(2)}, u32[]{:S(2)}) collective-permute-start(f32[64,128]{1,0:T(8,128)S(1)} %get-tuple-element.20.rest_0_), channel_id=1, source_target_pairs={{0,8},{8,0},{4,12},{12,4},{16,24},{24,16},{20,28},{28,20},{1,9},{9... | collective-permute-start | bytes 98312 | tf_op jit(solution)/shard_map/ppermute | solution.py:509
  35.7 2.6 %collective-permute-start.7 = (f32[64,128]{1,0:T(8,128)S(1)}, f32[64,128]{1,0:T(8,128)S(1)}, u32[]{:S(2)}, u32[]{:S(2)}) collective-permute-start(f32[64,128]{1,0:T(8,128)S(1)} %get-tuple-element.20.rest_0_), channel_id=1, source_target_pairs={{0,16},{16,0},{4,20},{20,4},{8,24},{24,8},{12,28},{28,12},{1,17},{... | collective-permute-start | bytes 98312 | tf_op jit(solution)/shard_map/ppermute | solution.py:509
  38.3 0.7 collective-permute-start.5
  39.0 1.9 %collective-permute-done.7.rest_2_ = f32[64,128]{1,0:T(8,128)S(1)} collective-permute-done((f32[64,128]{1,0:T(8,128)S(1)}, f32[64,128]{1,0:T(8,128)S(1)}, u32[]{:S(2)}, u32[]{:S(2)}) %collective-permute-start.7) | collective-permute-done | bytes 32800 | tf_op jit(solution)/shard_map/ppermute | solution.py:509
  40.9 2.8 %collective-permute-start.8 = (f32[64,128]{1,0:T(8,128)S(1)}, f32[64,128]{1,0:T(8,128)}, u32[]{:S(2)}, u32[]{:S(2)}) collective-permute-start(f32[64,128]{1,0:T(8,128)S(1)} %get-tuple-element.20.rest_0_), channel_id=1, source_target_pairs={{0,24},{24,0},{4,28},{28,4},{8,16},{16,8},{12,20},{20,12},{1,25},{... | collective-permute-start | bytes 98312 | tf_op jit(solution)/shard_map/ppermute | solution.py:509
  43.6 4.6 %collective-permute-done.8.rest_3_ = f32[64,128]{1,0:T(8,128)} collective-permute-done((f32[64,128]{1,0:T(8,128)S(1)}, f32[64,128]{1,0:T(8,128)}, u32[]{:S(2)}, u32[]{:S(2)}) %collective-permute-start.8) | collective-permute-done | bytes 32800 | tf_op jit(solution)/shard_map/ppermute | solution.py:509
  48.2 0.6 copy-done.3
  48.8 0.6 collective-permute-done.9.rest_4_
  49.4 0.6 copy-done.9
  50.0 0.2 collective-permute-start.10
  50.2 0.6 copy-done.5
  50.8 0.4 collective-permute-done.10.rest_5_
  51.2 0.6 copy-done.11
  51.9 0.2 collective-permute-start.11
  52.0 0.6 copy-done.7
  52.6 0.4 collective-permute-done.11.rest_6_
  53.1 0.6 copy-done.13
  53.7 0.2 collective-permute-start.12
  54.5 0.7 collective-permute-done.12.rest_7_
  55.2 0.0 collective-permute-done.4.next_a
  55.2 0.0 collective-permute-done.5.next_b
  55.2 0.0 collective-permute-done.got_a
  55.2 0.0 collective-permute-done.1.got_b
  55.3 0.0 copy-start.2
  55.3 1.0 %copy-done.2 = f32[8,128,128]{2,1,0:T(8,128)S(1)} copy-done((f32[8,128,128]{2,1,0:T(8,128)S(1)}, f32[8,128,128]{2,1,0:T(8,128)}, u32[]{:S(2)}) %copy-start.2) | copy-done | bytes 524312
  56.3 0.8 copy-done.4
  57.1 0.8 copy-done.6
  57.8 0.8 copy-done.8
  58.6 0.8 copy-done.10
  59.3 0.8 copy-done.12
  60.1 0.8 copy-done.14
  60.9 15.0 %last.1 = (f32[1,8,256,256]{3,2,1,0:T(8,128)}, f32[32,2,128]{2,1,0:T(2,128)S(1)}) custom-call(f32[4,2,256,128]{3,2,1,0:T(8,128)S(1)} %get-tuple-element.13.own_a, f32[4,2,256,128]{3,2,1,0:T(8,128)S(1)} %get-tuple-element.14.own_b, f32[4,2,256,128]{3,2,1,0:T(8,128)S(1)} %collective-permute-done.got_a, f32[4,2,256,128]{3,2,1,0:T(8,128)} %collective-permute-done.1.got_b, ...), custom_call_target="tpu_custom_call" | custom-call | tf_op jit(solution)/shard_map/last/pallas_call | solution.py:576
  75.9 0.6 copy-done.15
  76.5 6.0 %all-to-all-start = ((f32[32,2,128]{2,1,0:T(2,128)}), f32[32,2,128]{2,1,0:T(2,128)S(1)}, u32[]{:S(2)}, u32[]{:S(2)}) async-start(f32[32,2,128]{2,1,0:T(2,128)} %copy-done.15), calls=%async_computation | async-start | bytes 65536 | tf_op jit(solution)/shard_map/all_to_all | solution.py:605
  82.5 7.3 %all-to-all-done = f32[32,2,128]{2,1,0:T(2,128)S(1)} async-done(((f32[32,2,128]{2,1,0:T(2,128)}), f32[32,2,128]{2,1,0:T(2,128)S(1)}, u32[]{:S(2)}, u32[]{:S(2)}) %all-to-all-start) | async-done | bytes 32800 | tf_op jit(solution)/shard_map/all_to_all | solution.py:605
  89.8 0.6 slice_reduce_fusion
  90.4 0.7 select_reduce_fusion
  (20 shorter events, 0.0 us)
Async XLA Ops:
  0.6 3.4 %copy-start = (bf16[8,8,256,256]{3,2,1,0:T(8,128)(2,1)S(1)}, bf16[8,8,256,256]{3,2,1,0:T(8,128)(2,1)}, u32[]{:S(2)}) copy-start(bf16[8,8,256,256]{3,2,1,0:T(8,128)(2,1)} %orbitals.1) | copy-start | bytes 25165828
  4.0 0.7 copy-start.16
  11.7 43.5 %collective-permute-start = (f32[4,2,256,128]{3,2,1,0:T(8,128)S(1)}, f32[4,2,256,128]{3,2,1,0:T(8,128)S(1)}, u32[]{:S(2)}, u32[]{:S(2)}) collective-permute-start(f32[4,2,256,128]{3,2,1,0:T(8,128)S(1)} %get-tuple-element.13.own_a), channel_id=1, source_target_pairs={{0,4},{4,0},{8,12},{12,8},{16,20},{20,16},{24,28},{28,24},{1,5},{5... | collective-permute-start | bytes 3145736 | tf_op jit(solution)/shard_map/ppermute | solution.py:509
  12.3 42.9 %collective-permute-start.1 = (f32[4,2,256,128]{3,2,1,0:T(8,128)S(1)}, f32[4,2,256,128]{3,2,1,0:T(8,128)}, u32[]{:S(2)}, u32[]{:S(2)}) collective-permute-start(f32[4,2,256,128]{3,2,1,0:T(8,128)S(1)} %get-tuple-element.14.own_b), channel_id=1, source_target_pairs={{4,8},{8,4},{12,16},{16,12},{20,24},{24,20},{5,9},{9,5},{13,17},{1... | collective-permute-start | bytes 3145736 | tf_op jit(solution)/shard_map/ppermute | solution.py:509
  14.0 4.1 %collective-permute-start.2 = (f32[3,128,128]{2,1,0:T(8,128)S(1)}, f32[3,128,128]{2,1,0:T(8,128)S(1)}, u32[]{:S(2)}, u32[]{:S(2)}) collective-permute-start(f32[3,128,128]{2,1,0:T(8,128)S(1)} %get-tuple-element.15.sent_a), channel_id=1, source_target_pairs={{0,4},{4,0},{8,12},{12,8},{16,20},{20,16},{24,28},{28,24},{1,5},{5... | collective-permute-start | bytes 589832 | tf_op jit(solution)/shard_map/ppermute | solution.py:509
  17.0 1.1 %collective-permute-start.3 = (f32[3,128,128]{2,1,0:T(8,128)S(1)}, f32[3,128,128]{2,1,0:T(8,128)S(1)}, u32[]{:S(2)}, u32[]{:S(2)}) collective-permute-start(f32[3,128,128]{2,1,0:T(8,128)S(1)} %get-tuple-element.16.sent_b), channel_id=1, source_target_pairs={{4,8},{8,4},{12,16},{16,12},{20,24},{24,20},{5,9},{9,5},{13,17},{1... | collective-permute-start | bytes 589832 | tf_op jit(solution)/shard_map/ppermute | solution.py:509
  19.8 0.8 copy-start.1
  20.6 17.7 %collective-permute-start.6 = (f32[64,128]{1,0:T(8,128)S(1)}, f32[64,128]{1,0:T(8,128)S(1)}, u32[]{:S(2)}, u32[]{:S(2)}) collective-permute-start(f32[64,128]{1,0:T(8,128)S(1)} %get-tuple-element.20.rest_0_), channel_id=1, source_target_pairs={{0,8},{8,0},{4,12},{12,4},{16,24},{24,16},{20,28},{28,20},{1,9},{9... | collective-permute-start | bytes 98312 | tf_op jit(solution)/shard_map/ppermute | solution.py:509
  35.7 5.2 %collective-permute-start.7 = (f32[64,128]{1,0:T(8,128)S(1)}, f32[64,128]{1,0:T(8,128)S(1)}, u32[]{:S(2)}, u32[]{:S(2)}) collective-permute-start(f32[64,128]{1,0:T(8,128)S(1)} %get-tuple-element.20.rest_0_), channel_id=1, source_target_pairs={{0,16},{16,0},{4,20},{20,4},{8,24},{24,8},{12,28},{28,12},{1,17},{... | collective-permute-start | bytes 98312 | tf_op jit(solution)/shard_map/ppermute | solution.py:509
  38.3 16.9 %collective-permute-start.4 = (f32[3,128,128]{2,1,0:T(8,128)}, f32[3,128,128]{2,1,0:T(8,128)S(1)}, u32[]{:S(2)}, u32[]{:S(2)}) collective-permute-start(f32[3,128,128]{2,1,0:T(8,128)} %get-tuple-element.18), channel_id=1, source_target_pairs={{0,4},{4,0},{8,12},{12,8},{16,20},{20,16},{24,28},{28,24},{1,5},{5... | collective-permute-start | bytes 589832 | tf_op jit(solution)/shard_map/ppermute | solution.py:509
  38.3 16.9 %collective-permute-start.5 = (f32[3,128,128]{2,1,0:T(8,128)}, f32[3,128,128]{2,1,0:T(8,128)S(1)}, u32[]{:S(2)}, u32[]{:S(2)}) collective-permute-start(f32[3,128,128]{2,1,0:T(8,128)} %get-tuple-element.19), channel_id=1, source_target_pairs={{4,8},{8,4},{12,16},{16,12},{20,24},{24,20},{5,9},{9,5},{13,17},{1... | collective-permute-start | bytes 589832 | tf_op jit(solution)/shard_map/ppermute | solution.py:509
  40.9 7.3 %collective-permute-start.8 = (f32[64,128]{1,0:T(8,128)S(1)}, f32[64,128]{1,0:T(8,128)}, u32[]{:S(2)}, u32[]{:S(2)}) collective-permute-start(f32[64,128]{1,0:T(8,128)S(1)} %get-tuple-element.20.rest_0_), channel_id=1, source_target_pairs={{0,24},{24,0},{4,28},{28,4},{8,16},{16,8},{12,20},{20,12},{1,25},{... | collective-permute-start | bytes 98312 | tf_op jit(solution)/shard_map/ppermute | solution.py:509
  48.2 1.2 %collective-permute-start.9 = (f32[64,128]{1,0:T(8,128)S(1)}, f32[64,128]{1,0:T(8,128)S(1)}, u32[]{:S(2)}, u32[]{:S(2)}) collective-permute-start(f32[64,128]{1,0:T(8,128)S(1)} %get-tuple-element.20.rest_0_), channel_id=1, source_target_pairs={{0,4},{4,0},{8,12},{12,8},{16,20},{20,16},{24,28},{28,24},{1,5},{5... | collective-permute-start | bytes 98312 | tf_op jit(solution)/shard_map/ppermute | solution.py:509
  48.2 0.6 copy-start.3
  49.4 0.6 copy-start.9
  50.0 1.2 %collective-permute-start.10 = (f32[64,128]{1,0:T(8,128)S(1)}, f32[64,128]{1,0:T(8,128)S(1)}, u32[]{:S(2)}, u32[]{:S(2)}) collective-permute-start(f32[64,128]{1,0:T(8,128)S(1)} %collective-permute-done.6.rest_1_), channel_id=1, source_target_pairs={{0,4},{4,0},{8,12},{12,8},{16,20},{20,16},{24,28},{28,24},{1,5},{5... | collective-permute-start | bytes 98312 | tf_op jit(solution)/shard_map/ppermute | solution.py:509
  50.2 0.6 copy-start.5
  51.2 0.6 copy-start.11
  51.9 1.2 %collective-permute-start.11 = (f32[64,128]{1,0:T(8,128)S(1)}, f32[64,128]{1,0:T(8,128)S(1)}, u32[]{:S(2)}, u32[]{:S(2)}) collective-permute-start(f32[64,128]{1,0:T(8,128)S(1)} %collective-permute-done.7.rest_2_), channel_id=1, source_target_pairs={{0,4},{4,0},{8,12},{12,8},{16,20},{20,16},{24,28},{28,24},{1,5},{5... | collective-permute-start | bytes 98312 | tf_op jit(solution)/shard_map/ppermute | solution.py:509
  52.0 0.6 copy-start.7
  53.1 0.6 copy-start.13
  53.7 1.6 %collective-permute-start.12 = (f32[64,128]{1,0:T(8,128)}, f32[64,128]{1,0:T(8,128)}, u32[]{:S(2)}, u32[]{:S(2)}) collective-permute-start(f32[64,128]{1,0:T(8,128)} %collective-permute-done.8.rest_3_), channel_id=1, source_target_pairs={{0,4},{4,0},{8,12},{12,8},{16,20},{20,16},{24,28},{28,24},{1,5},{5... | collective-permute-start | bytes 98312 | tf_op jit(solution)/shard_map/ppermute | solution.py:509
  55.3 1.0 %copy-start.2 = (f32[8,128,128]{2,1,0:T(8,128)S(1)}, f32[8,128,128]{2,1,0:T(8,128)}, u32[]{:S(2)}) copy-start(f32[8,128,128]{2,1,0:T(8,128)} %copy-done.1) | copy-start | bytes 1572868
  56.3 0.8 copy-start.4
  57.1 0.8 copy-start.6
  57.8 0.8 copy-start.8
  58.6 0.8 copy-start.10
  59.3 0.8 copy-start.12
  60.1 0.8 copy-start.14
  75.9 0.6 copy-start.15
  76.5 13.3 %all-to-all-start = ((f32[32,2,128]{2,1,0:T(2,128)}), f32[32,2,128]{2,1,0:T(2,128)S(1)}, u32[]{:S(2)}, u32[]{:S(2)}) async-start(f32[32,2,128]{2,1,0:T(2,128)} %copy-done.15), calls=%async_computation | async-start | bytes 65536 | tf_op jit(solution)/shard_map/all_to_all | solution.py:605

commit v2 on v1

--- a/solution.py
+++ b/solution.py
@@ -6,6 +6,7 @@
 from jax.experimental import pallas as pl
 from jax.experimental.pallas import tpu as pltpu
 from jax.sharding import PartitionSpec as P
+
 
 LANES = 128
 PAD = 8
@@ -18,6 +19,7 @@
 ANY = pl.BlockSpec(memory_space=pl.ANY)
 VMEM = pl.BlockSpec(memory_space=pltpu.VMEM)
 SMEM = pl.BlockSpec(memory_space=pltpu.SMEM)
+HBM = pl.BlockSpec(memory_space=pltpu.HBM)
 
 
 def scale(level):
@@ -121,7 +123,7 @@
 
     def fetch(z):
         return [
-            pltpu.make_async_copy(orbitals.at[pair_index[0, k], z], buffer.at[z], in_sem.at[k, z])
+            pltpu.make_async_copy(orbitals.at[pair_index[k], z], buffer.at[z], in_sem.at[k, z])
             for k, buffer in ((0, left), (1, right))
         ]
 
@@ -318,47 +320,93 @@
         result[b, centre, :] = packed_apply(smooth, b, rows) + source[b, centre, :] * c2
 
 
-def last_kernel(
-    size, partners, cells, own_a, own_b, got_a, got_b, whole, next_a, next_b, *rest
-):
-    arrived = rest[: len(partners)]
-    weight, potential, sums = rest[len(partners) : len(partners) + 3]
-    scratch = rest[len(partners) + 3 :]
-    (field, first, second, third, grown, mid, mid_first, mid_second, mid_third, mid_grown) = scratch[:10]
-    (low_source, low_result, low_blocks, low_smooth, bottom, spare, in_sem, out_sem) = scratch[10:]
-    parts, rows = own_a.shape[1], own_a.shape[2]
-    half = own_a.shape[0]
-    planes = 2 * half
-    mid_rows = whole.shape[1]
-    mid_planes = whole.shape[0] - 4
+def bring_all(pairs, sem):
+    copies = [pltpu.make_async_copy(origin, target, sem.at[k]) for k, (origin, target) in enumerate(pairs)]
+    for copy in copies:
+        copy.start()
+    return copies
+
+
+def start_level(dst, src, grown, planes, shift, offset, level, rows):
+    c = scale(level)
+
+    def plane(z, _):
+        for r in range(0, rows, ROWS):
+            centre, total = neighbours(src, z, r, ROWS)
+            for h in range(len(centre)):
+                value = centre[h] * (c * (1.0 + THIRD)) + total[h] * (c * NINTH)
+                dst[z + shift, h, pl.ds(PAD + r, ROWS), :] = value + grown[(z + offset) >> 1, h, pl.ds(r, ROWS), :]
+        return 0
+
+    lax.fori_loop(*planes, plane, 0)
+
+
+def sweep_level(dst, src, source, planes, shift, offset, level, rows):
+    c = scale(level)
+
+    def plane(z, _):
+        for r in range(0, rows, ROWS):
+            centre, total = neighbours(src, z, r, ROWS)
+            for h in range(len(centre)):
+                value = centre[h] * THIRD + total[h] * NINTH
+                dst[z + shift, h, pl.ds(PAD + r, ROWS), :] = value + source[z + offset, h, pl.ds(PAD + r, ROWS), :] * c
+        return 0
+
+    lax.fori_loop(*planes, plane, 0)
+
+
+def span(me, size, halo, inside, shift=0):
+    low = jnp.where(me == 0, halo, 0)
+    high = jnp.where(me == size - 1, halo + inside, 2 * halo + inside)
+    return low + shift, high + shift
+
+
+def blank_outside(ref, me, size, halo, inside, rows):
+    @pl.when(me == 0)
+    def _():
+        zero_planes(ref, range(halo), rows)
+
+    @pl.when(me == size - 1)
+    def _():
+        zero_planes(ref, range(halo + inside, 2 * halo + inside), rows)
+
+
+def low_kernel(size, partners, whole, next_a, next_b, *rest):
+    arrived, (result,) = rest[: len(partners)], rest[len(partners) : len(partners) + 1]
+    (mid, first, second, _, grown) = rest[len(partners) + 1 : len(partners) + 6]
+    (low_source, low_result, low_blocks, low_smooth, bottom, spare, low_sem, mid_sem) = rest[len(partners) + 6 :]
+    rows = whole.shape[1]
+    planes = whole.shape[0] - 4
     low_rows = arrived[0].shape[0]
     me = lax.axis_index("gz")
     odd = me % 2
-    is_first, is_last = me == 0, me == size - 1
-
-    def bring(k, origin, plane):
-        return pltpu.make_async_copy(origin, field.at[pl.ds(plane, half), :, pl.ds(PAD, rows), :], in_sem.at[k])
-
-    copies = [
-        bring(0, own_a, half + half * (1 - odd)),
-        bring(1, own_b, half + half * odd),
-        bring(2, got_a, 3 * half * (1 - odd)),
-        bring(3, got_b, 3 * half * odd),
+    blank = jnp.zeros((PAD, LANES), F32)
+    inner = pl.ds(PAD, low_rows)
+    middle = pl.ds(PAD, rows)
+    edge = 3
+
+    blocks = [
+        (ref, low_source.at[jnp.bitwise_xor(me, partner) + 1, inner]) for partner, ref in zip(partners, arrived)
     ]
-    for copy in copies:
-        copy.start()
-
-    blank = jnp.zeros((PAD, LANES), F32)
-    for ref in (field, first, second, third):
+    low_copies = bring_all(blocks, low_sem)
+    top = edge + planes + 4
+    mid_copies = bring_all(
+        [
+            (whole, mid.at[pl.ds(edge, planes + 4), 0, middle]),
+            (next_a, mid.at[pl.ds(top * (1 - odd), edge), 0, middle]),
+            (next_b, mid.at[pl.ds(top * odd, edge), 0, middle]),
+        ],
+        mid_sem,
+    )
+
+    for ref in (mid, first, second):
         zero_pads(ref, rows)
-    for ref in (mid, mid_first, mid_second):
-        zero_pads(ref, mid_rows)
     for ref in (low_source, low_blocks, low_smooth):
         for b in range(size + 2):
             ref[b, pl.ds(0, PAD), :] = blank
             ref[b, pl.ds(PAD + low_rows, PAD), :] = blank
         for b in (0, size + 1):
-            ref[b, pl.ds(PAD, low_rows), :] = jnp.zeros((low_rows, LANES), F32)
+            ref[b, inner, :] = jnp.zeros((low_rows, LANES), F32)
     for k in range(2):
         for b in range(size + 2):
             bottom[k, b, pl.ds(0, PAD), :] = blank
@@ -366,122 +414,88 @@
         for b in (0, size + 1):
             bottom[k, b] = jnp.zeros(bottom.shape[2:], F32)
     for b in (0, size + 1):
-        low_result[b, pl.ds(PAD, low_rows), :] = jnp.zeros((low_rows, LANES), F32)
-
-    for partner, ref in zip(partners, arrived):
-        low_source[jnp.bitwise_xor(me, partner) + 1, pl.ds(PAD, low_rows), :] = ref[...]
-
+        low_result[b, inner, :] = jnp.zeros((low_rows, LANES), F32)
+    blank_outside(first, me, size, 4, planes, rows)
+    blank_outside(second, me, size, 3, planes, rows)
+
+    for copy in low_copies:
+        copy.wait()
     coarse_levels(size, low_source, low_result, low_blocks, low_smooth, bottom, spare)
-
-    edge = 3
-    middle = pl.ds(PAD, mid_rows)
-    for plane in range(mid_planes + 4):
-        mid[edge + plane, 0, middle, :] = whole[plane]
-
-    def sides(low, high):
-        for k in range(edge):
-            mid[k, 0, middle, :] = low[k]
-            mid[edge + mid_planes + 4 + k, 0, middle, :] = high[k]
-
-    @pl.when(odd == 0)
-    def _():
-        sides(next_b, next_a)
-
-    @pl.when(odd == 1)
-    def _():
-        sides(next_a, next_b)
 
     row, column = iota((LANES, LANES), 0), iota((LANES, LANES), 1)
     for k in range(3):
-        block = low_result[me + k, pl.ds(PAD, low_rows), :]
+        block = low_result[me + k, inner, :]
         for side in range(2):
-            matrix = to_bf16((column >> 1) + side * (LANES // 2) == row)
-            value = split_dot(block, matrix)
-            mid_grown[2 * k + side, 0, pl.ds(0, low_rows, stride=2), :] = value
-            mid_grown[2 * k + side, 0, pl.ds(1, low_rows, stride=2), :] = value
-
-    def start(dst, src, grown_ref, first_plane, last_plane, shift, offset, level, n):
-        c = scale(level)
-
-        def plane(z, _):
-            for r in range(0, n, ROWS):
-                centre, total = neighbours(src, z, r, ROWS)
-                for h in range(len(centre)):
-                    value = centre[h] * (c * (1.0 + THIRD)) + total[h] * (c * NINTH)
-                    dst[z + shift, h, pl.ds(PAD + r, ROWS), :] = value + grown_ref[(z + offset) >> 1, h, pl.ds(r, ROWS), :]
-            return 0
-
-        lax.fori_loop(first_plane, last_plane, plane, 0)
-
-    def again(dst, src, source, first_plane, last_plane, shift, offset, level, n):
-        c = scale(level)
-
-        def plane(z, _):
-            for r in range(0, n, ROWS):
-                centre, total = neighbours(src, z, r, ROWS)
-                for h in range(len(centre)):
-                    value = centre[h] * THIRD + total[h] * NINTH
-                    dst[z + shift, h, pl.ds(PAD + r, ROWS), :] = value + source[z + offset, h, pl.ds(PAD + r, ROWS), :] * c
-            return 0
-
-        lax.fori_loop(first_plane, last_plane, plane, 0)
-
-    def blank_outside(ref, halo, inside, n):
-        @pl.when(is_first)
-        def _():
-            zero_planes(ref, range(halo), n)
-
-        @pl.when(is_last)
-        def _():
-            zero_planes(ref, range(halo + inside, 2 * halo + inside), n)
-
-    def span(halo, inside):
-        return jnp.where(is_first, halo, 0), jnp.where(is_last, halo + inside, 2 * halo + inside)
-
-    n = mid_planes
-    low, high = span(4, n)
-    start(mid_first, mid, mid_grown, low + 1, high + 1, -1, -1, 1, mid_rows)
-    blank_outside(mid_first, 4, n, mid_rows)
-    low, high = span(3, n)
-    again(mid_second, mid_first, mid, low + 1, high + 1, -1, 1, 1, mid_rows)
-    blank_outside(mid_second, 3, n, mid_rows)
-    low, high = span(2, n)
-
+            value = split_dot(block, to_bf16((column >> 1) + side * (LANES // 2) == row))
+            grown[2 * k + side, 0, pl.ds(0, low_rows, stride=2), :] = value
+            grown[2 * k + side, 0, pl.ds(1, low_rows, stride=2), :] = value
+
+    for copy in mid_copies:
+        copy.wait()
+    start_level(first, mid, grown, span(me, size, 4, planes, 1), -1, -1, 1, rows)
+    sweep_level(second, first, mid, span(me, size, 3, planes, 1), -1, 1, 1, rows)
+    c1 = scale(1)
+
+    def last(z, _):
+        for r in range(0, rows, ROWS):
+            centre, total = neighbours(second, z + 1, r, ROWS)
+            value = centre[0] * THIRD + total[0] * NINTH
+            result[z, pl.ds(r, ROWS), :] = value + mid[z + 3, 0, pl.ds(PAD + r, ROWS), :] * c1
+        return 0
+
+    lax.fori_loop(*span(me, size, 2, planes), last, 0)
+
+
+def top_kernel(size, cells, own_a, own_b, got_a, got_b, correction, weight, potential, sums, *scratch):
+    field, first, second, third, grown, in_sem, out_sem = scratch
+    half, parts, rows = own_a.shape[0], own_a.shape[1], own_a.shape[2]
+    planes = 2 * half
+    mid_rows = correction.shape[1]
+    me = lax.axis_index("gz")
+    odd = me % 2
+
+    def into(plane):
+        return field.at[pl.ds(plane, half), :, pl.ds(PAD, rows), :]
+
+    copies = bring_all(
+        [
+            (own_a, into(half + half * (1 - odd))),
+            (own_b, into(half + half * odd)),
+            (got_a, into(3 * half * (1 - odd))),
+            (got_b, into(3 * half * odd)),
+        ],
+        in_sem,
+    )
+    for ref in (field, first, second, third):
+        zero_pads(ref, rows)
+    blank_outside(first, me, size, 3, planes, rows)
+    blank_outside(second, me, size, 2, planes, rows)
+    blank_outside(third, me, size, 1, planes, rows)
+
+    row, column = iota((LANES, LANES), 0), iota((LANES, LANES), 1)
     spread = [to_bf16((column + h * LANES) >> 1 == row) for h in range(parts)]
-    c1 = scale(1)
-
-    def correct(z, _):
-        for r in range(0, mid_rows, ROWS):
-            centre, total = neighbours(mid_second, z + 1, r, ROWS)
-            mid_third[pl.ds(r, ROWS), :] = centre[0] * THIRD + total[0] * NINTH + mid[z + 3, 0, pl.ds(PAD + r, ROWS), :] * c1
-        value = mid_third[...]
+
+    def widen(z, _):
+        value = correction[z]
         for h in range(parts):
             wide = split_dot(value, spread[h])
             grown[z, h, pl.ds(0, mid_rows, stride=2), :] = wide
             grown[z, h, pl.ds(1, mid_rows, stride=2), :] = wide
         return 0
 
-    lax.fori_loop(low, high, correct, 0)
+    lax.fori_loop(*span(me, size, 2, half), widen, 0)
 
     for copy in copies:
         copy.wait()
-
-    n = planes
-    low, high = span(3, n)
-    start(first, field, grown, low + 1, high + 1, -1, 0, 0, rows)
-    blank_outside(first, 3, n, rows)
-    low, high = span(2, n)
-    again(second, first, field, low + 1, high + 1, -1, 1, 0, rows)
-    blank_outside(second, 2, n, rows)
-    low, high = span(1, n)
-    again(third, second, field, low + 1, high + 1, -1, 2, 0, rows)
-    blank_outside(third, 1, n, rows)
+    start_level(first, field, grown, span(me, size, 3, planes, 1), -1, 0, 0, rows)
+    sweep_level(second, first, field, span(me, size, 2, planes, 1), -1, 1, 0, rows)
+    sweep_level(third, second, field, span(me, size, 1, planes, 1), -1, 2, 0, rows)
 
     def give(z, h):
         target = potential.at[0, z, :, pl.ds(h * LANES, LANES)]
         return pltpu.make_async_copy(third.at[z + 1, h, pl.ds(PAD, rows), :], target, out_sem.at[z, h])
 
-    for z in range(n):
+    for z in range(planes):
         for h in range(parts):
             give(z, h).start()
 
@@ -491,18 +505,27 @@
             centre, total = neighbours(third, z + 1, r, ROWS)
             for h in range(parts):
                 f = field[z + half, h, pl.ds(PAD + r, ROWS), :]
-                rest_of = f - 6.0 * centre[h] + total[h]
-                squares += jnp.sum((rest_of * rest_of).reshape(ROWS // 8, 8, LANES), axis=0)
+                remain = f - 6.0 * centre[h] + total[h]
+                squares += jnp.sum((remain * remain).reshape(ROWS // 8, 8, LANES), axis=0)
                 products += jnp.sum((f * centre[h]).reshape(ROWS // 8, 8, LANES), axis=0)
         return squares, products
 
-    squares, products = lax.fori_loop(0, n, final, (jnp.zeros((8, LANES), F32),) * 2)
+    squares, products = lax.fori_loop(0, planes, final, (jnp.zeros((8, LANES), F32),) * 2)
     products = products * (weight[0] * (-0.5 / cells))
     both = jnp.concatenate([jnp.sum(squares, axis=0, keepdims=True), jnp.sum(products, axis=0, keepdims=True)], axis=0)
     sums[...] = jnp.broadcast_to(both[None], sums.shape)
-    for z in range(n):
+    for z in range(planes):
         for h in range(parts):
             give(z, h).wait()
+
+
+def total_kernel(groups, cells, everyone, norm, energy):
+    values = everyone[...]
+    mine = iota(values.shape, 0) % groups == lax.axis_index("pair")
+    first = iota(values.shape, 1) == 0
+    squares = jnp.sum(jnp.where(first & mine, values, 0.0))
+    norm[0] = jnp.sqrt(jnp.full((1, 1), squares * (1.0 / cells), F32))[0, 0]
+    energy[0] = jnp.sum(jnp.where(first, 0.0, values))
 
 
 def exchange(value, pairs):
@@ -519,7 +542,7 @@
     _, planes, rows, columns = orbitals.shape
     parts = columns // LANES
     assert planes == 8 and columns == 2 * LANES and rows % (4 * ROWS) == 0 and pair_index.shape[0] == 1 and size % 2 == 0
-    half, quarter = planes // 2, planes // 4
+    half = planes // 2
     mid_rows, low_rows = rows // 2, rows // 4
     tall, mid_tall, low_tall = rows + 2 * PAD, mid_rows + 2 * PAD, low_rows + 2 * PAD
     inner = [(i, i + 1) for i in range(0, size, 2)]
@@ -535,7 +558,7 @@
     own_a, own_b, coarse_a, coarse_b = pl.pallas_call(
         functools.partial(fine_kernel, size),
         out_shape=[shape(half, parts, rows, LANES)] * 2 + [shape(three, mid_rows, LANES)] * 2,
-        in_specs=[ANY, SMEM],
+        in_specs=[HBM, SMEM],
         out_specs=[ANY, ANY, VMEM, VMEM],
         scratch_shapes=[
             pltpu.VMEM((planes, rows, columns), orbitals.dtype),
@@ -546,14 +569,12 @@
             pltpu.SemaphoreType.DMA((2, planes)),
             pltpu.SemaphoreType.DMA((2,)),
         ],
-        compiler_params=params(24),
+        compiler_params=params(58),
         name="fine",
-    )(orbitals, pair_index)
+    )(orbitals, pair_index.reshape(2))
 
     coarse_got_a = exchange(coarse_a, inner)
     coarse_got_b = exchange(coarse_b, outer)
-    own_got_a = exchange(own_a, inner)
-    own_got_b = exchange(own_b, outer)
 
     whole, next_a, next_b, packed = pl.pallas_call(
         functools.partial(middle_kernel, size),
@@ -566,24 +587,22 @@
     )(coarse_a, coarse_b, coarse_got_a, coarse_got_b)
 
     partners = list(range(0, size, 2))
-    arrived = [packed] + [exchange(packed, [(i, i ^ k) for i in range(size) if i < i ^ k]) for k in partners[1:]]
+    arrived = [packed]
+    for k in partners[1:]:
+        arrived.append(exchange(packed, [(i, i ^ k) for i in range(size) if i < i ^ k]))
+    next_got_a = exchange(next_a, inner)
+    next_got_b = exchange(next_b, outer)
+    own_got_a = exchange(own_a, inner)
+    own_got_b = exchange(own_b, outer)
     arrived += [exchange(value, inner) for value in arrived]
     partners += [k ^ 1 for k in partners]
-    next_got_a = exchange(next_a, inner)
-    next_got_b = exchange(next_b, outer)
-
-    cells = planes * size * rows * columns
-    potential, sums = pl.pallas_call(
-        functools.partial(last_kernel, size, tuple(partners), cells),
-        out_shape=[shape(1, planes, rows, columns), shape(size * groups, 2, LANES)],
-        in_specs=[ANY] * 4 + [VMEM] * (3 + len(partners)) + [SMEM],
-        out_specs=[ANY, VMEM],
+
+    correction = pl.pallas_call(
+        functools.partial(low_kernel, size, tuple(partners)),
+        out_shape=shape(half + 4, mid_rows, LANES),
+        in_specs=[ANY] * (3 + len(partners)),
+        out_specs=VMEM,
         scratch_shapes=[
-            scratch(planes + 8, parts, tall, LANES),
-            scratch(planes + 6, parts, tall, LANES),
-            scratch(planes + 4, parts, tall, LANES),
-            scratch(planes + 2, parts, tall, LANES),
-            scratch(half + 4, parts, rows, LANES),
             scratch(half + 10, 1, mid_tall, LANES),
             scratch(half + 8, 1, mid_tall, LANES),
             scratch(half + 6, 1, mid_tall, LANES),
@@ -595,18 +614,41 @@
             scratch(size + 2, low_tall, LANES),
             scratch(3, size + 2, low_rows // 2 + 2 * PAD, LANES),
             scratch(size + 2, low_rows, LANES),
+            pltpu.SemaphoreType.DMA((len(partners),)),
+            pltpu.SemaphoreType.DMA((3,)),
+        ],
+        compiler_params=params(12),
+        name="low",
+    )(whole, next_got_a, next_got_b, *arrived)
+
+    cells = planes * size * rows * columns
+    potential, sums = pl.pallas_call(
+        functools.partial(top_kernel, size, cells),
+        out_shape=[shape(1, planes, rows, columns), shape(size * groups, 2, LANES)],
+        in_specs=[ANY] * 4 + [VMEM, SMEM],
+        out_specs=[ANY, VMEM],
+        scratch_shapes=[
+            scratch(planes + 8, parts, tall, LANES),
+            scratch(planes + 6, parts, tall, LANES),
+            scratch(planes + 4, parts, tall, LANES),
+            scratch(planes + 2, parts, tall, LANES),
+            scratch(half + 4, parts, rows, LANES),
             pltpu.SemaphoreType.DMA((4,)),
             pltpu.SemaphoreType.DMA((planes, parts)),
         ],
-        compiler_params=params(32),
-        name="last",
-    )(own_a, own_b, own_got_a, own_got_b, whole, next_got_a, next_got_b, *arrived, pair_weight)
-
-    everyone = lax.all_to_all(sums, ("gz", "pair"), 0, 0).reshape(size, groups, 2, LANES)
-    mine = iota((size, groups, LANES), 1) == lax.axis_index("pair")
-    squares = jnp.sum(jnp.where(mine, everyone[:, :, 0], 0.0))
-    energy = jnp.sum(everyone[:, :, 1])
-    return (potential, jnp.sqrt(squares / cells).reshape(1), energy.reshape(1))
+        compiler_params=params(24),
+        name="top",
+    )(own_a, own_b, own_got_a, own_got_b, correction, pair_weight)
+
+    everyone = lax.all_to_all(sums, ("gz", "pair"), 0, 0)
+    norm, energy = pl.pallas_call(
+        functools.partial(total_kernel, groups, cells),
+        out_shape=[shape(1)] * 2,
+        in_specs=[VMEM],
+        out_specs=[SMEM] * 2,
+        name="total",
+    )(everyone)
+    return (potential, norm, energy)
 
 
 def solution(mesh):

time: 93.7 us -> 83.1 us (0.89)
  blocking collectives: 0 us -> 14.2 us
  local copies, waits for them, and re-layouts: 14.7 us -> 4.3 us
  starting transfers between devices: 33.5 us -> 26.7 us
  waiting for transfers between devices: 16.4 us -> 12.3 us
  between operations: 3.21 us -> 1.38 us
  other arithmetic: 1.32 us -> 0 us
    all_to_all x0 -> x1, blocking collectives: none -> 14.2 us  [per_device(): everyone = lax.all_to_all(sums, ('gz', 'pair'), 0, 0)]
    unnamed x34 -> x8, local copies, waits for them, and re-layouts: 14.7 us -> 4.3 us
    all_to_all x1 -> x0, waiting for transfers between devices: 7.28 us -> none  [per_device(): lax.all_to_all(sums, ('gz', 'pair'), 0, 0).reshape(size, groups, 2, LANES)]
    all_to_all x1 -> x0, starting transfers between devices: 5.97 us -> none  [per_device(): lax.all_to_all(sums, ('gz', 'pair'), 0, 0).reshape(size, groups, 2, LANES)]
    ppermute x13, waiting for transfers between devices: 9.08 us -> 12.3 us  [exchange(): lax.ppermute(value, 'gz', [move for a, b in pairs for move in ((a, b), (b...]
    pallas_call x1 -> x3, Pallas kernels: 15 us -> 16.6 us  [the longest x1 9.9 us: per_device(): pl.pallas_call(functools.partial(top_kernel, size, cells), out_shape=[sha...]
    reduce_sum x2 -> x0, other arithmetic: 1.31 us -> none  [the longest x1 0.67 us: per_device(): squares = jnp.sum(jnp.where(mine, everyone[:, :, 0], 0.0))]
  transfers between devices with their start and end apart: 14 -> 13, of which waited for: 8 -> 7; matrix products, arithmetic and copies ran while one was open for 0% -> 0% of each run, Pallas kernels for 2% -> 7%
where the time goes in v2:
time: 83.1 us; the launch traced here: 82.6 us
  starting transfers between devices  26.7 us (32%)
  Pallas kernels  23.8 us (29%)
  blocking collectives  14.2 us (17%)
  waiting for transfers between devices  12.3 us (15%)
  local copies, waits for them, and re-layouts  4.3 us (5%)
  between operations  1.38 us (2%)
    ppermute x13, starting transfers between devices, exchange(): lax.ppermute(value, 'gz', [move for a, b in pairs for move in ((a, b), (b...  26.7 us
    all_to_all x1, blocking collectives, per_device(): everyone = lax.all_to_all(sums, ('gz', 'pair'), 0, 0)  14.2 us
    ppermute x13, waiting for transfers between devices, exchange(): lax.ppermute(value, 'gz', [move for a, b in pairs for move in ((a, b), (b...  12.3 us
    pallas_call x1, Pallas kernels, per_device(): pl.pallas_call(functools.partial(top_kernel, size, cells), out_shape=[sha...  9.9 us
    pallas_call x1, Pallas kernels, per_device(): pl.pallas_call(functools.partial(fine_kernel, size), out_shape=[shape(hal...  6.23 us
    pallas_call x1, Pallas kernels, per_device(): pl.pallas_call(functools.partial(low_kernel, size, tuple(partners)), out_...  5.25 us
    unnamed x8, local copies, waits for them, and re-layouts  4.3 us
  transfers between devices with their start and end apart: 13, of which 7 were waited for; matrix products, arithmetic and copies ran while one was open for 0% of the time, Pallas kernels for 7%

profile of v2, /device:TPU:0, one launch (start us, length us, event | category | flops | bytes accessed | tf_op | source)
XLA Modules:
  0.0 82.6 jit_solution(15177115581687028128)
XLA Ops:
  0.6 6.2 %fine.1 = (f32[4,2,256,128]{3,2,1,0:T(8,128)}, f32[4,2,256,128]{3,2,1,0:T(8,128)}, f32[3,128,128]{2,1,0:T(8,128)}, f32[3,128,128]{2,1,0:T(8,128)}) custom-call(bf16[8,8,256,256]{3,2,1,0:T(8,128)(2,1)} %orbitals.1, s32[2]{0:T(128)} %bitcast.1), custom_call_target="tpu_custom_call" | custom-call | tf_op jit(solution)/shard_map/fine/pallas_call | solution.py:558
  6.9 0.6 collective-permute-start
  7.4 0.7 collective-permute-start.1
  8.2 3.9 %collective-permute-start.2 = (f32[3,128,128]{2,1,0:T(8,128)}, f32[3,128,128]{2,1,0:T(8,128)S(1)}, u32[]{:S(2)}, u32[]{:S(2)}) collective-permute-start(f32[3,128,128]{2,1,0:T(8,128)} %get-tuple-element.17.sent_a), channel_id=1, source_target_pairs={{0,4},{4,0},{8,12},{12,8},{16,20},{20,16},{24,28},{28,24},{1,5},{5... | collective-permute-start | bytes 589832 | tf_op jit(solution)/shard_map/ppermute | solution.py:532
  12.1 0.7 collective-permute-start.3
  12.8 0.6 collective-permute-done.2.got_a
  13.4 0.0 collective-permute-done.3.got_b
  13.4 0.0 copy-start.2
  13.4 0.9 %copy-done.2 = f32[3,128,128]{2,1,0:T(8,128)S(1)} copy-done((f32[3,128,128]{2,1,0:T(8,128)S(1)}, f32[3,128,128]{2,1,0:T(8,128)}, u32[]{:S(2)}) %copy-start.2) | copy-done | bytes 196632
  14.3 0.0 copy-start.3
  14.3 0.9 %copy-done.3 = f32[3,128,128]{2,1,0:T(8,128)S(1)} copy-done((f32[3,128,128]{2,1,0:T(8,128)S(1)}, f32[3,128,128]{2,1,0:T(8,128)}, u32[]{:S(2)}) %copy-start.3) | copy-done | bytes 196632
  15.3 0.9 %middle.1 = (f32[8,128,128]{2,1,0:T(8,128)S(1)}, f32[3,128,128]{2,1,0:T(8,128)S(1)}, f32[3,128,128]{2,1,0:T(8,128)S(1)}, f32[64,128]{1,0:T(8,128)S(1)}) custom-call(f32[3,128,128]{2,1,0:T(8,128)S(1)} %copy-done.2, f32[3,128,128]{2,1,0:T(8,128)S(1)} %copy-done.3, f32[3,128,128]{2,1,0:T(8,128)S(1)} %collective-permute-done.2.got_a, ...), custom_call_target="tpu_custom_call" | custom-call | tf_op jit(solution)/shard_map/middle/pallas_call | solution.py:579
  16.2 13.6 %collective-permute-start.9 = (f32[64,128]{1,0:T(8,128)S(1)}, f32[64,128]{1,0:T(8,128)S(1)}, u32[]{:S(2)}, u32[]{:S(2)}) collective-permute-start(f32[64,128]{1,0:T(8,128)S(1)} %get-tuple-element.22.rest_0_), channel_id=1, source_target_pairs={{0,4},{4,0},{8,12},{12,8},{16,20},{20,16},{24,28},{28,24},{1,5},{5... | collective-permute-start | bytes 98312 | tf_op jit(solution)/shard_map/ppermute | solution.py:532
  29.8 3.7 %collective-permute-start.8 = (f32[64,128]{1,0:T(8,128)S(1)}, f32[64,128]{1,0:T(8,128)S(1)}, u32[]{:S(2)}, u32[]{:S(2)}) collective-permute-start(f32[64,128]{1,0:T(8,128)S(1)} %get-tuple-element.22.rest_0_), channel_id=1, source_target_pairs={{0,24},{24,0},{4,28},{28,4},{8,16},{16,8},{12,20},{20,12},{1,25},{... | collective-permute-start | bytes 98312 | tf_op jit(solution)/shard_map/ppermute | solution.py:532
  33.5 0.2 collective-permute-start.4
  33.7 0.0 collective-permute-done.9.rest_4_
  33.7 0.7 collective-permute-start.5
  34.4 1.2 %collective-permute-done.8.rest_3_ = f32[64,128]{1,0:T(8,128)S(1)} collective-permute-done((f32[64,128]{1,0:T(8,128)S(1)}, f32[64,128]{1,0:T(8,128)S(1)}, u32[]{:S(2)}, u32[]{:S(2)}) %collective-permute-start.8) | collective-permute-done | bytes 32800 | tf_op jit(solution)/shard_map/ppermute | solution.py:532
  35.6 1.5 %collective-permute-start.7 = (f32[64,128]{1,0:T(8,128)S(1)}, f32[64,128]{1,0:T(8,128)S(1)}, u32[]{:S(2)}, u32[]{:S(2)}) collective-permute-start(f32[64,128]{1,0:T(8,128)S(1)} %get-tuple-element.22.rest_0_), channel_id=1, source_target_pairs={{0,16},{16,0},{4,20},{20,4},{8,24},{24,8},{12,28},{28,12},{1,17},{... | collective-permute-start | bytes 98312 | tf_op jit(solution)/shard_map/ppermute | solution.py:532
  37.1 4.7 %collective-permute-done.7.rest_2_ = f32[64,128]{1,0:T(8,128)S(1)} collective-permute-done((f32[64,128]{1,0:T(8,128)S(1)}, f32[64,128]{1,0:T(8,128)S(1)}, u32[]{:S(2)}, u32[]{:S(2)}) %collective-permute-start.7) | collective-permute-done | bytes 32800 | tf_op jit(solution)/shard_map/ppermute | solution.py:532
  41.8 0.8 collective-permute-start.6
  42.6 3.1 %collective-permute-done.6.rest_1_ = f32[64,128]{1,0:T(8,128)S(1)} collective-permute-done((f32[64,128]{1,0:T(8,128)S(1)}, f32[64,128]{1,0:T(8,128)S(1)}, u32[]{:S(2)}, u32[]{:S(2)}) %collective-permute-start.6) | collective-permute-done | bytes 32800 | tf_op jit(solution)/shard_map/ppermute | solution.py:532
  45.7 0.0 collective-permute-start.12
  45.7 1.2 %collective-permute-done.12.rest_7_ = f32[64,128]{1,0:T(8,128)S(1)} collective-permute-done((f32[64,128]{1,0:T(8,128)S(1)}, f32[64,128]{1,0:T(8,128)S(1)}, u32[]{:S(2)}, u32[]{:S(2)}) %collective-permute-start.12) | collective-permute-done | bytes 32800 | tf_op jit(solution)/shard_map/ppermute | solution.py:532
  46.9 0.2 collective-permute-start.11
  47.1 1.0 %collective-permute-done.11.rest_6_ = f32[64,128]{1,0:T(8,128)S(1)} collective-permute-done((f32[64,128]{1,0:T(8,128)S(1)}, f32[64,128]{1,0:T(8,128)S(1)}, u32[]{:S(2)}, u32[]{:S(2)}) %collective-permute-start.11) | collective-permute-done | bytes 32800 | tf_op jit(solution)/shard_map/ppermute | solution.py:532
  48.1 0.2 collective-permute-start.10
  48.9 0.4 collective-permute-done.10.rest_5_
  49.3 0.0 collective-permute-done.4.next_a
  49.3 0.0 collective-permute-done.5.next_b
  49.3 5.2 %low.1.correction = f32[8,128,128]{2,1,0:T(8,128)S(1)} custom-call(f32[8,128,128]{2,1,0:T(8,128)S(1)} %get-tuple-element.19.whole, f32[3,128,128]{2,1,0:T(8,128)S(1)} %collective-permute-done.4.next_a, f32[3,128,128]{2,1,0:T(8,128)S(1)} %collective-permute-done.5.next_b, f32[64,128]{1,0:T(8,128)S(1)} %get-tuple-element.22.rest_0_, ...), custom_call_target="tpu_custom_call" | custom-call | tf_op jit(solution)/shard_map/low/pallas_call | solution.py:600
  54.6 0.0 collective-permute-done.got_a
  54.6 0.0 collective-permute-done.1.got_b
  54.6 0.0 copy-start
  54.6 1.2 %copy-done = f32[4,2,256,128]{3,2,1,0:T(8,128)S(1)} copy-done((f32[4,2,256,128]{3,2,1,0:T(8,128)S(1)}, f32[4,2,256,128]{3,2,1,0:T(8,128)}, u32[]{:S(2)}) %copy-start) | copy-done | bytes 1048600
  55.8 0.0 copy-start.1
  55.8 1.2 %copy-done.1 = f32[4,2,256,128]{3,2,1,0:T(8,128)S(1)} copy-done((f32[4,2,256,128]{3,2,1,0:T(8,128)S(1)}, f32[4,2,256,128]{3,2,1,0:T(8,128)}, u32[]{:S(2)}) %copy-start.1) | copy-done | bytes 1048600
  57.0 9.9 %top.1 = (f32[1,8,256,256]{3,2,1,0:T(8,128)}, f32[32,2,128]{2,1,0:T(2,128)S(1)}) custom-call(f32[4,2,256,128]{3,2,1,0:T(8,128)S(1)} %copy-done, f32[4,2,256,128]{3,2,1,0:T(8,128)S(1)} %copy-done.1, f32[4,2,256,128]{3,2,1,0:T(8,128)S(1)} %collective-permute-done.got_a, f32[4,2,256,128]{3,2,1,0:T(8,128)S(1)} %collective-permute-done.1.got_b, ...), custom_call_target="tpu_custom_call" | custom-call | tf_op jit(solution)/shard_map/top/pallas_call | solution.py:625
  67.0 14.2 %all_to_all.5.everyone = f32[32,2,128]{2,1,0:T(2,128)} all-to-all(f32[32,2,128]{2,1,0:T(2,128)S(1)} %get-tuple-element.24), channel_id=1, replica_groups=mesh['gz'=8,'pair'=4] {'gz','pair'}, dimensions={0} | all-to-all | bytes 65536 | tf_op jit(solution)/shard_map/all_to_all | solution.py:643
  81.2 1.5 %total.1 = (f32[1]{0:T(128)}, f32[1]{0:T(128)}) custom-call(f32[32,2,128]{2,1,0:T(2,128)} %all_to_all.5.everyone), custom_call_target="tpu_custom_call" | custom-call | tf_op jit(solution)/shard_map/total/pallas_call | solution.py:644
Async XLA Ops:
  6.9 47.7 %collective-permute-start = (f32[4,2,256,128]{3,2,1,0:T(8,128)}, f32[4,2,256,128]{3,2,1,0:T(8,128)S(1)}, u32[]{:S(2)}, u32[]{:S(2)}) collective-permute-start(f32[4,2,256,128]{3,2,1,0:T(8,128)} %get-tuple-element.15.own_a), channel_id=1, source_target_pairs={{0,4},{4,0},{8,12},{12,8},{16,20},{20,16},{24,28},{28,24},{1,5},{5... | collective-permute-start | bytes 3145736 | tf_op jit(solution)/shard_map/ppermute | solution.py:532
  7.4 47.1 %collective-permute-start.1 = (f32[4,2,256,128]{3,2,1,0:T(8,128)}, f32[4,2,256,128]{3,2,1,0:T(8,128)S(1)}, u32[]{:S(2)}, u32[]{:S(2)}) collective-permute-start(f32[4,2,256,128]{3,2,1,0:T(8,128)} %get-tuple-element.16.own_b), channel_id=1, source_target_pairs={{4,8},{8,4},{12,16},{16,12},{20,24},{24,20},{5,9},{9,5},{13,17},{1... | collective-permute-start | bytes 3145736 | tf_op jit(solution)/shard_map/ppermute | solution.py:532
  8.2 5.2 %collective-permute-start.2 = (f32[3,128,128]{2,1,0:T(8,128)}, f32[3,128,128]{2,1,0:T(8,128)S(1)}, u32[]{:S(2)}, u32[]{:S(2)}) collective-permute-start(f32[3,128,128]{2,1,0:T(8,128)} %get-tuple-element.17.sent_a), channel_id=1, source_target_pairs={{0,4},{4,0},{8,12},{12,8},{16,20},{20,16},{24,28},{28,24},{1,5},{5... | collective-permute-start | bytes 589832 | tf_op jit(solution)/shard_map/ppermute | solution.py:532
  12.1 1.3 %collective-permute-start.3 = (f32[3,128,128]{2,1,0:T(8,128)}, f32[3,128,128]{2,1,0:T(8,128)S(1)}, u32[]{:S(2)}, u32[]{:S(2)}) collective-permute-start(f32[3,128,128]{2,1,0:T(8,128)} %get-tuple-element.18.sent_b), channel_id=1, source_target_pairs={{4,8},{8,4},{12,16},{16,12},{20,24},{24,20},{5,9},{9,5},{13,17},{1... | collective-permute-start | bytes 589832 | tf_op jit(solution)/shard_map/ppermute | solution.py:532
  13.4 0.9 %copy-start.2 = (f32[3,128,128]{2,1,0:T(8,128)S(1)}, f32[3,128,128]{2,1,0:T(8,128)}, u32[]{:S(2)}) copy-start(f32[3,128,128]{2,1,0:T(8,128)} %get-tuple-element.17.sent_a) | copy-start | bytes 589828
  14.3 0.9 %copy-start.3 = (f32[3,128,128]{2,1,0:T(8,128)S(1)}, f32[3,128,128]{2,1,0:T(8,128)}, u32[]{:S(2)}) copy-start(f32[3,128,128]{2,1,0:T(8,128)} %get-tuple-element.18.sent_b) | copy-start | bytes 589828
  16.2 17.5 %collective-permute-start.9 = (f32[64,128]{1,0:T(8,128)S(1)}, f32[64,128]{1,0:T(8,128)S(1)}, u32[]{:S(2)}, u32[]{:S(2)}) collective-permute-start(f32[64,128]{1,0:T(8,128)S(1)} %get-tuple-element.22.rest_0_), channel_id=1, source_target_pairs={{0,4},{4,0},{8,12},{12,8},{16,20},{20,16},{24,28},{28,24},{1,5},{5... | collective-permute-start | bytes 98312 | tf_op jit(solution)/shard_map/ppermute | solution.py:532
  29.8 5.8 %collective-permute-start.8 = (f32[64,128]{1,0:T(8,128)S(1)}, f32[64,128]{1,0:T(8,128)S(1)}, u32[]{:S(2)}, u32[]{:S(2)}) collective-permute-start(f32[64,128]{1,0:T(8,128)S(1)} %get-tuple-element.22.rest_0_), channel_id=1, source_target_pairs={{0,24},{24,0},{4,28},{28,4},{8,16},{16,8},{12,20},{20,12},{1,25},{... | collective-permute-start | bytes 98312 | tf_op jit(solution)/shard_map/ppermute | solution.py:532
  33.5 15.8 %collective-permute-start.4 = (f32[3,128,128]{2,1,0:T(8,128)S(1)}, f32[3,128,128]{2,1,0:T(8,128)S(1)}, u32[]{:S(2)}, u32[]{:S(2)}) collective-permute-start(f32[3,128,128]{2,1,0:T(8,128)S(1)} %get-tuple-element.20), channel_id=1, source_target_pairs={{0,4},{4,0},{8,12},{12,8},{16,20},{20,16},{24,28},{28,24},{1,5},{5... | collective-permute-start | bytes 589832 | tf_op jit(solution)/shard_map/ppermute | solution.py:532
  33.7 15.6 %collective-permute-start.5 = (f32[3,128,128]{2,1,0:T(8,128)S(1)}, f32[3,128,128]{2,1,0:T(8,128)S(1)}, u32[]{:S(2)}, u32[]{:S(2)}) collective-permute-start(f32[3,128,128]{2,1,0:T(8,128)S(1)} %get-tuple-element.21), channel_id=1, source_target_pairs={{4,8},{8,4},{12,16},{16,12},{20,24},{24,20},{5,9},{9,5},{13,17},{1... | collective-permute-start | bytes 589832 | tf_op jit(solution)/shard_map/ppermute | solution.py:532
  35.6 6.2 %collective-permute-start.7 = (f32[64,128]{1,0:T(8,128)S(1)}, f32[64,128]{1,0:T(8,128)S(1)}, u32[]{:S(2)}, u32[]{:S(2)}) collective-permute-start(f32[64,128]{1,0:T(8,128)S(1)} %get-tuple-element.22.rest_0_), channel_id=1, source_target_pairs={{0,16},{16,0},{4,20},{20,4},{8,24},{24,8},{12,28},{28,12},{1,17},{... | collective-permute-start | bytes 98312 | tf_op jit(solution)/shard_map/ppermute | solution.py:532
  41.8 3.9 %collective-permute-start.6 = (f32[64,128]{1,0:T(8,128)S(1)}, f32[64,128]{1,0:T(8,128)S(1)}, u32[]{:S(2)}, u32[]{:S(2)}) collective-permute-start(f32[64,128]{1,0:T(8,128)S(1)} %get-tuple-element.22.rest_0_), channel_id=1, source_target_pairs={{0,8},{8,0},{4,12},{12,4},{16,24},{24,16},{20,28},{28,20},{1,9},{9... | collective-permute-start | bytes 98312 | tf_op jit(solution)/shard_map/ppermute | solution.py:532
  45.7 1.2 %collective-permute-start.12 = (f32[64,128]{1,0:T(8,128)S(1)}, f32[64,128]{1,0:T(8,128)S(1)}, u32[]{:S(2)}, u32[]{:S(2)}) collective-permute-start(f32[64,128]{1,0:T(8,128)S(1)} %collective-permute-done.8.rest_3_), channel_id=1, source_target_pairs={{0,4},{4,0},{8,12},{12,8},{16,20},{20,16},{24,28},{28,24},{1,5},{5... | collective-permute-start | bytes 98312 | tf_op jit(solution)/shard_map/ppermute | solution.py:532
  46.9 1.2 %collective-permute-start.11 = (f32[64,128]{1,0:T(8,128)S(1)}, f32[64,128]{1,0:T(8,128)S(1)}, u32[]{:S(2)}, u32[]{:S(2)}) collective-permute-start(f32[64,128]{1,0:T(8,128)S(1)} %collective-permute-done.7.rest_2_), channel_id=1, source_target_pairs={{0,4},{4,0},{8,12},{12,8},{16,20},{20,16},{24,28},{28,24},{1,5},{5... | collective-permute-start | bytes 98312 | tf_op jit(solution)/shard_map/ppermute | solution.py:532
  48.1 1.2 %collective-permute-start.10 = (f32[64,128]{1,0:T(8,128)S(1)}, f32[64,128]{1,0:T(8,128)S(1)}, u32[]{:S(2)}, u32[]{:S(2)}) collective-permute-start(f32[64,128]{1,0:T(8,128)S(1)} %collective-permute-done.6.rest_1_), channel_id=1, source_target_pairs={{0,4},{4,0},{8,12},{12,8},{16,20},{20,16},{24,28},{28,24},{1,5},{5... | collective-permute-start | bytes 98312 | tf_op jit(solution)/shard_map/ppermute | solution.py:532
  54.6 1.2 %copy-start = (f32[4,2,256,128]{3,2,1,0:T(8,128)S(1)}, f32[4,2,256,128]{3,2,1,0:T(8,128)}, u32[]{:S(2)}) copy-start(f32[4,2,256,128]{3,2,1,0:T(8,128)} %get-tuple-element.15.own_a) | copy-start | bytes 3145732
  55.8 1.2 %copy-start.1 = (f32[4,2,256,128]{3,2,1,0:T(8,128)S(1)}, f32[4,2,256,128]{3,2,1,0:T(8,128)}, u32[]{:S(2)}) copy-start(f32[4,2,256,128]{3,2,1,0:T(8,128)} %get-tuple-element.16.own_b) | copy-start | bytes 3145732

commit v3 on v2

--- a/solution.py
+++ b/solution.py
@@ -42,16 +42,17 @@
 
 def neighbours(ref, z, row, rows):
     parts = ref.shape[1]
-    centre = [ref[z, h, pl.ds(PAD + row, rows), :] for h in range(parts)]
+    here = pl.ds(PAD + row, rows)
+    centre = [ref[z, h, here, :] for h in range(parts)]
     lane = iota((rows, LANES), 1)
-    after = [pltpu.roll(c, 1, 1) for c in centre]
-    before = [pltpu.roll(c, LANES - 1, 1) for c in centre]
+    after = jnp.where(lane == 0, 0.0, pltpu.roll(centre[-1], 1, 1))
+    before = jnp.where(lane == LANES - 1, 0.0, pltpu.roll(centre[0], LANES - 1, 1))
     sums = []
     for h in range(parts):
         total = ref[z, h, pl.ds(PAD + row - 1, rows), :] + ref[z, h, pl.ds(PAD + row + 1, rows), :]
-        total += ref[z - 1, h, pl.ds(PAD + row, rows), :] + ref[z + 1, h, pl.ds(PAD + row, rows), :]
-        total += jnp.where(lane == 0, after[h - 1] if h else 0.0, after[h])
-        total += jnp.where(lane == LANES - 1, before[h + 1] if h + 1 < parts else 0.0, before[h])
+        total += ref[z - 1, h, here, :] + ref[z + 1, h, here, :]
+        total += centre[h - 1] if h else after
+        total += centre[h + 1] if h + 1 < parts else before
         sums.append(total)
     return centre, sums
 
@@ -79,42 +80,63 @@
         for row in range(0, rows, ROWS):
             centre, sums = neighbours(src, z, row, ROWS)
             for h in range(len(centre)):
-                dst[z + shift, h, pl.ds(PAD + row, ROWS), :] = centre[h] * THIRD + sums[h] * NINTH
+                dst[z + shift, h, pl.ds(PAD + row, ROWS), :] = (centre[h] * 3.0 + sums[h]) * NINTH
         return 0
 
     lax.fori_loop(first, last, plane, 0)
 
 
+def paired_rows(ref, z, rows, offset):
+    return [ref[z, h, pl.ds(PAD + offset, rows // 2, stride=2), :] for h in range(ref.shape[1])]
+
+
+def restrict_columns(inner, far):
+    lane = iota(far.shape, 1)
+    pair = [a + b for a, b in zip(inner[1], inner[2])]
+    outer = far + (inner[0][0] + inner[3][0]) + (inner[0][1] + inner[3][1])
+    outer += jnp.where(lane == 0, 0.0, pltpu.roll(pair[1], 1, 1))
+    outer += jnp.where(lane == LANES - 1, 0.0, pltpu.roll(pair[0], LANES - 1, 1))
+    return ((pair[0] + pair[1]) * 6.0 + outer) * (NINTH / 8.0)
+
+
+def total_of(*lists):
+    return functools.reduce(lambda a, b: a + b, [v for values in lists for v in values])
+
+
+def restrict_fine(ref, z, rows):
+    inner = [[a + b for a, b in zip(paired_rows(ref, z, rows, k), paired_rows(ref, z + 1, rows, k))] for k in (-1, 0, 1, 2)]
+    far = total_of(*(paired_rows(ref, p, rows, k) for p in (z - 1, z + 2) for k in (0, 1)))
+    return restrict_columns(inner, far)
+
+
 def restrict_pair(ref, z, rows, matrices):
-    total = None
     half = rows // 2
-    for h in range(ref.shape[1]):
-
-        def at(plane, offset):
-            return ref[plane, h, pl.ds(PAD + offset, half, stride=2), :]
-
-        inner = [at(z, k) + at(z + 1, k) for k in (-1, 0, 1, 2)]
-        pair = inner[1] + inner[2]
-        outer = inner[0] + inner[3] + (at(z - 1, 0) + at(z - 1, 1)) + (at(z + 2, 0) + at(z + 2, 1))
-        part = split_dot(pair, matrices[0][h]) + split_dot(outer, matrices[1][h])
-        total = part if total is None else total + part
+
+    def at(plane, offset):
+        return ref[plane, 0, pl.ds(PAD + offset, half, stride=2), :]
+
+    inner = [at(z, k) + at(z + 1, k) for k in (-1, 0, 1, 2)]
+    outer = inner[0] + inner[3] + (at(z - 1, 0) + at(z - 1, 1)) + (at(z + 2, 0) + at(z + 2, 1))
+    total = split_dot(inner[1] + inner[2], matrices[0]) + split_dot(outer, matrices[1])
     return total * (NINTH / 8.0)
 
 
-def restrict_matrices(width, parts, out_shift=0):
-    stencil, plain = [], []
-    for h in range(parts):
-        row = iota((LANES, LANES), 0) + h * LANES
-        column = iota((LANES, LANES), 1) - out_shift
-        inside = (column >= 0) & (column < width // 2)
-        own = (row >> 1) == column
-        beside = (row == 2 * column - 1) | (row == 2 * column + 2)
-        stencil.append(jnp.where(inside & own, 6.0, jnp.where(inside & beside, 1.0, 0.0)).astype(BF16))
-        plain.append(to_bf16(inside & own))
-    return stencil, plain
-
-
-def fine_kernel(size, orbitals, pair_index, own_a, own_b, coarse_a, coarse_b, left, right, source, smooth, sums, in_sem, out_sem):
+def restrict_matrices(out_shift):
+    row, column = iota((LANES, LANES), 0), iota((LANES, LANES), 1) - out_shift
+    inside = (column >= 0) & (column < LANES // 2)
+    own = (row >> 1) == column
+    beside = (row == 2 * column - 1) | (row == 2 * column + 2)
+    stencil = jnp.where(inside & own, 6.0, jnp.where(inside & beside, 1.0, 0.0)).astype(BF16)
+    return stencil, to_bf16(inside & own)
+
+
+def deal(parts):
+    n = parts * LANES
+    row, column = iota((n, n), 0), iota((n, n), 1)
+    return to_bf16(row == parts * (column & (LANES - 1)) + (column >> 7))
+
+
+def fine_kernel(size, orbitals, pair_index, own_a, own_b, coarse_a, coarse_b, once, left, right, source, smooth, sums, in_sem, out_sem):
     planes, rows = left.shape[0], left.shape[1]
     parts = source.shape[1]
     half = planes // 2
@@ -134,16 +156,17 @@
     zero_pads(smooth, rows)
     zero_planes(source, (0, planes + 1), rows)
     zero_planes(smooth, (0, 1, planes + 2, planes + 3), rows)
-    matrices = restrict_matrices(parts * LANES, parts)
-
-    for z in range(planes):
+    dealt = deal(parts)
+
+    def multiply(z, _):
         for copy in fetch(z):
             copy.wait()
-
-        for row in range(0, rows, 2 * ROWS):
-            for h in range(parts):
-                here = (z, pl.ds(row, 2 * ROWS), pl.ds(h * LANES, LANES))
-                source[z + 1, h, pl.ds(PAD + row, 2 * ROWS), :] = left[here].astype(F32) * right[here].astype(F32)
+        product = jnp.dot(left[z], dealt, preferred_element_type=F32) * jnp.dot(right[z], dealt, preferred_element_type=F32)
+        for h in range(parts):
+            source[z + 1, h, pl.ds(PAD, rows), :] = product[:, h * LANES : (h + 1) * LANES]
+        return 0
+
+    lax.fori_loop(0, planes, multiply, 0)
 
     def keep(start, target, k):
         return pltpu.make_async_copy(source.at[pl.ds(start, half), :, pl.ds(PAD, rows), :], target, out_sem.at[k])
@@ -167,27 +190,21 @@
     for copy in kept:
         copy.start()
 
+    kept.append(pltpu.make_async_copy(smooth.at[pl.ds(2, planes), :, pl.ds(PAD, rows), :], once, out_sem.at[2]))
+    kept[-1].start()
+
     def coarse(q, _):
-        sums[q + 1] = restrict_pair(smooth, 2 * q + 2, rows, matrices)
+        sums[q + 1] = restrict_fine(smooth, 2 * q + 2, rows)
         return 0
 
     lax.fori_loop(0, half, coarse, 0)
-    low = [smooth[1, h, pl.ds(PAD + k, rows // 2, stride=2), :] for h in range(parts) for k in (-1, 0, 1, 2)]
-    low_z = [smooth[2, h, pl.ds(PAD + k, rows // 2, stride=2), :] for h in range(parts) for k in (0, 1)]
-    high = [smooth[planes + 2, h, pl.ds(PAD + k, rows // 2, stride=2), :] for h in range(parts) for k in (-1, 0, 1, 2)]
-    high_z = [smooth[planes + 1, h, pl.ds(PAD + k, rows // 2, stride=2), :] for h in range(parts) for k in (0, 1)]
-
-    def edge(inner, far):
-        total = None
-        for h in range(parts):
-            i = inner[4 * h : 4 * h + 4]
-            part = split_dot(i[1] + i[2], matrices[0][h])
-            part += split_dot(i[0] + i[3] + (far[2 * h] + far[2 * h + 1]), matrices[1][h])
-            total = part if total is None else total + part
-        return total * (NINTH / 8.0)
-
-    sums[0] = jnp.where(me > 0, edge(low, low_z), 0.0)
-    sums[half + 1] = jnp.where(me < size - 1, edge(high, high_z), 0.0)
+
+    def edge(plane, far):
+        inner = [paired_rows(smooth, plane, rows, k) for k in (-1, 0, 1, 2)]
+        return restrict_columns(inner, total_of(*(paired_rows(smooth, far, rows, k) for k in (0, 1))))
+
+    sums[0] = jnp.where(me > 0, edge(1, 2), 0.0)
+    sums[half + 1] = jnp.where(me < size - 1, edge(planes + 2, planes + 1), 0.0)
 
     three = (half + 2) // 2
 
@@ -211,7 +228,7 @@
     me = lax.axis_index("gz")
     zero_pads(field, rows)
     zero_pads(smooth, rows)
-    first, second = restrict_matrices(LANES, 1), restrict_matrices(LANES, 1, LANES // 2)
+    first, second = restrict_matrices(0), restrict_matrices(LANES // 2)
 
     def gather(own, low, high):
         centre = pl.ds(PAD, rows)
@@ -328,28 +345,29 @@
 
 
 def start_level(dst, src, grown, planes, shift, offset, level, rows):
-    c = scale(level)
+    c = scale(level) * NINTH
 
     def plane(z, _):
         for r in range(0, rows, ROWS):
             centre, total = neighbours(src, z, r, ROWS)
             for h in range(len(centre)):
-                value = centre[h] * (c * (1.0 + THIRD)) + total[h] * (c * NINTH)
-                dst[z + shift, h, pl.ds(PAD + r, ROWS), :] = value + grown[(z + offset) >> 1, h, pl.ds(r, ROWS), :]
+                value = (centre[h] * 12.0 + total[h]) * c
+                dst[z + shift, h, pl.ds(PAD + r, ROWS), :] = value + grown[(z + offset) >> 1, pl.ds(r, ROWS), :]
         return 0
 
     lax.fori_loop(*planes, plane, 0)
 
 
 def sweep_level(dst, src, source, planes, shift, offset, level, rows):
-    c = scale(level)
+    ratio = scale(level) / NINTH
 
     def plane(z, _):
         for r in range(0, rows, ROWS):
             centre, total = neighbours(src, z, r, ROWS)
             for h in range(len(centre)):
-                value = centre[h] * THIRD + total[h] * NINTH
-                dst[z + shift, h, pl.ds(PAD + r, ROWS), :] = value + source[z + offset, h, pl.ds(PAD + r, ROWS), :] * c
+                value = source[z + offset, h, pl.ds(PAD + r, ROWS), :]
+                value = value if ratio == 1.0 else value * ratio
+                dst[z + shift, h, pl.ds(PAD + r, ROWS), :] = (centre[h] * 3.0 + total[h] + value) * NINTH
         return 0
 
     lax.fori_loop(*planes, plane, 0)
@@ -371,13 +389,17 @@
         zero_planes(ref, range(halo + inside, 2 * halo + inside), rows)
 
 
-def low_kernel(size, partners, whole, next_a, next_b, *rest):
-    arrived, (result,) = rest[: len(partners)], rest[len(partners) : len(partners) + 1]
-    (mid, first, second, _, grown) = rest[len(partners) + 1 : len(partners) + 6]
-    (low_source, low_result, low_blocks, low_smooth, bottom, spare, low_sem, mid_sem) = rest[len(partners) + 6 :]
+def pack_kernel(*refs):
+    for k, ref in enumerate(refs[:-1]):
+        refs[-1][k] = ref[...]
+
+
+def low_kernel(size, partners, whole, next_a, next_b, mine, other, result, *scratch):
+    (mid, first, second, _, grown) = scratch[:5]
+    (low_source, low_result, low_blocks, low_smooth, bottom, spare, low_sem, mid_sem) = scratch[5:]
     rows = whole.shape[1]
     planes = whole.shape[0] - 4
-    low_rows = arrived[0].shape[0]
+    low_rows = mine.shape[1]
     me = lax.axis_index("gz")
     odd = me % 2
     blank = jnp.zeros((PAD, LANES), F32)
@@ -386,7 +408,9 @@
     edge = 3
 
     blocks = [
-        (ref, low_source.at[jnp.bitwise_xor(me, partner) + 1, inner]) for partner, ref in zip(partners, arrived)
+        (ref.at[k], low_source.at[jnp.bitwise_xor(me, partner ^ far) + 1, inner])
+        for far, ref in ((0, mine), (1, other))
+        for k, partner in enumerate(partners)
     ]
     low_copies = bring_all(blocks, low_sem)
     top = edge + planes + 4
@@ -427,8 +451,8 @@
         block = low_result[me + k, inner, :]
         for side in range(2):
             value = split_dot(block, to_bf16((column >> 1) + side * (LANES // 2) == row))
-            grown[2 * k + side, 0, pl.ds(0, low_rows, stride=2), :] = value
-            grown[2 * k + side, 0, pl.ds(1, low_rows, stride=2), :] = value
+            grown[2 * k + side, pl.ds(0, low_rows, stride=2), :] = value
+            grown[2 * k + side, pl.ds(1, low_rows, stride=2), :] = value
 
     for copy in mid_copies:
         copy.wait()
@@ -446,8 +470,8 @@
     lax.fori_loop(*span(me, size, 2, planes), last, 0)
 
 
-def top_kernel(size, cells, own_a, own_b, got_a, got_b, correction, weight, potential, sums, *scratch):
-    field, first, second, third, grown, in_sem, out_sem = scratch
+def top_kernel(size, cells, own_a, own_b, got_a, got_b, once, correction, weight, potential, sums, *scratch):
+    field, first, second, third, grown, plain, in_sem, out_sem = scratch
     half, parts, rows = own_a.shape[0], own_a.shape[1], own_a.shape[2]
     planes = 2 * half
     mid_rows = correction.shape[1]
@@ -472,35 +496,51 @@
     blank_outside(second, me, size, 2, planes, rows)
     blank_outside(third, me, size, 1, planes, rows)
 
-    row, column = iota((LANES, LANES), 0), iota((LANES, LANES), 1)
-    spread = [to_bf16((column + h * LANES) >> 1 == row) for h in range(parts)]
-
     def widen(z, _):
         value = correction[z]
-        for h in range(parts):
-            wide = split_dot(value, spread[h])
-            grown[z, h, pl.ds(0, mid_rows, stride=2), :] = wide
-            grown[z, h, pl.ds(1, mid_rows, stride=2), :] = wide
+        grown[z, pl.ds(0, mid_rows, stride=2), :] = value
+        grown[z, pl.ds(1, mid_rows, stride=2), :] = value
         return 0
 
     lax.fori_loop(*span(me, size, 2, half), widen, 0)
 
     for copy in copies:
         copy.wait()
-    start_level(first, field, grown, span(me, size, 3, planes, 1), -1, 0, 0, rows)
+    low, high = span(me, size, 3, planes, 1)
+    start_level(first, field, grown, (low, 4), -1, 0, 0, rows)
+    start_level(first, field, grown, (4 + planes, high), -1, 0, 0, rows)
+    c0 = scale(0)
+
+    def begin(z, beside=None):
+        for r in range(0, rows, ROWS):
+            spread = grown[(z + half) >> 1, pl.ds(r, ROWS), :]
+            for h in range(parts):
+                value = field[z + half, h, pl.ds(PAD + r, ROWS), :] + once[z, h, pl.ds(r, ROWS), :]
+                if beside is not None:
+                    value += field[beside, h, pl.ds(PAD + r, ROWS), :] * NINTH
+                first[z + 3, h, pl.ds(PAD + r, ROWS), :] = value * c0 + spread
+        return 0
+
+    begin(0, half - 1)
+    lax.fori_loop(1, planes - 1, lambda z, _: begin(z), 0)
+    begin(planes - 1, half + planes)
     sweep_level(second, first, field, span(me, size, 2, planes, 1), -1, 1, 0, rows)
     sweep_level(third, second, field, span(me, size, 1, planes, 1), -1, 2, 0, rows)
 
-    def give(z, h):
-        target = potential.at[0, z, :, pl.ds(h * LANES, LANES)]
-        return pltpu.make_async_copy(third.at[z + 1, h, pl.ds(PAD, rows), :], target, out_sem.at[z, h])
-
-    for z in range(planes):
-        for h in range(parts):
-            give(z, h).start()
+    def give(z):
+        return pltpu.make_async_copy(plain.at[z], potential.at[0, z], out_sem.at[z])
+
+    row, column = iota((2 * parts * LANES, parts * LANES), 0), iota((2 * parts * LANES, parts * LANES), 1)
+    in_order = to_bf16(column == parts * (row & (LANES - 1)) + ((row >> 7) & (parts - 1)))
 
     def final(z, totals):
         squares, products = totals
+        here = pl.ds(PAD, rows)
+        whole = [third[z + 1, h, here, :] for h in range(parts)]
+        upper = [value.astype(BF16) for value in whole]
+        lower = [(value - part.astype(F32)).astype(BF16) for value, part in zip(whole, upper)]
+        plain[z] = jnp.dot(jnp.concatenate(upper + lower, axis=1), in_order, preferred_element_type=F32)
+        give(z).start()
         for r in range(0, rows, ROWS):
             centre, total = neighbours(third, z + 1, r, ROWS)
             for h in range(parts):
@@ -515,8 +555,7 @@
     both = jnp.concatenate([jnp.sum(squares, axis=0, keepdims=True), jnp.sum(products, axis=0, keepdims=True)], axis=0)
     sums[...] = jnp.broadcast_to(both[None], sums.shape)
     for z in range(planes):
-        for h in range(parts):
-            give(z, h).wait()
+        give(z).wait()
 
 
 def total_kernel(groups, cells, everyone, norm, energy):
@@ -555,11 +594,11 @@
         return pltpu.VMEM(dims, F32)
 
     three = (half + 2) // 2
-    own_a, own_b, coarse_a, coarse_b = pl.pallas_call(
+    own_a, own_b, coarse_a, coarse_b, once = pl.pallas_call(
         functools.partial(fine_kernel, size),
-        out_shape=[shape(half, parts, rows, LANES)] * 2 + [shape(three, mid_rows, LANES)] * 2,
+        out_shape=[shape(half, parts, rows, LANES)] * 2 + [shape(three, mid_rows, LANES)] * 2 + [shape(planes, parts, rows, LANES)],
         in_specs=[HBM, SMEM],
-        out_specs=[ANY, ANY, VMEM, VMEM],
+        out_specs=[ANY, ANY, VMEM, VMEM, ANY],
         scratch_shapes=[
             pltpu.VMEM((planes, rows, columns), orbitals.dtype),
             pltpu.VMEM((planes, rows, columns), orbitals.dtype),
@@ -567,9 +606,9 @@
             scratch(planes + 4, parts, tall, LANES),
             scratch(half + 2, mid_rows, LANES),
             pltpu.SemaphoreType.DMA((2, planes)),
-            pltpu.SemaphoreType.DMA((2,)),
+            pltpu.SemaphoreType.DMA((3,)),
         ],
-        compiler_params=params(58),
+        compiler_params=params(48),
         name="fine",
     )(orbitals, pair_index.reshape(2))
 
@@ -594,51 +633,59 @@
     next_got_b = exchange(next_b, outer)
     own_got_a = exchange(own_a, inner)
     own_got_b = exchange(own_b, outer)
-    arrived += [exchange(value, inner) for value in arrived]
-    partners += [k ^ 1 for k in partners]
+    mine = pl.pallas_call(
+        pack_kernel,
+        out_shape=shape(len(partners), low_rows, LANES),
+        in_specs=[VMEM] * len(partners),
+        out_specs=VMEM,
+        compiler_params=params(4),
+        name="pack",
+    )(*arrived)
+    other = exchange(mine, inner)
 
     correction = pl.pallas_call(
         functools.partial(low_kernel, size, tuple(partners)),
         out_shape=shape(half + 4, mid_rows, LANES),
-        in_specs=[ANY] * (3 + len(partners)),
+        in_specs=[ANY] * 5,
         out_specs=VMEM,
         scratch_shapes=[
             scratch(half + 10, 1, mid_tall, LANES),
             scratch(half + 8, 1, mid_tall, LANES),
             scratch(half + 6, 1, mid_tall, LANES),
             scratch(mid_rows, LANES),
-            scratch(6, 1, mid_rows, LANES),
+            scratch(6, mid_rows, LANES),
             scratch(size + 2, low_tall, LANES),
             scratch(size + 2, low_tall, LANES),
             scratch(size + 2, low_tall, LANES),
             scratch(size + 2, low_tall, LANES),
             scratch(3, size + 2, low_rows // 2 + 2 * PAD, LANES),
             scratch(size + 2, low_rows, LANES),
-            pltpu.SemaphoreType.DMA((len(partners),)),
+            pltpu.SemaphoreType.DMA((2 * len(partners),)),
             pltpu.SemaphoreType.DMA((3,)),
         ],
         compiler_params=params(12),
         name="low",
-    )(whole, next_got_a, next_got_b, *arrived)
+    )(whole, next_got_a, next_got_b, mine, other)
 
     cells = planes * size * rows * columns
     potential, sums = pl.pallas_call(
         functools.partial(top_kernel, size, cells),
         out_shape=[shape(1, planes, rows, columns), shape(size * groups, 2, LANES)],
-        in_specs=[ANY] * 4 + [VMEM, SMEM],
+        in_specs=[ANY] * 4 + [VMEM, VMEM, SMEM],
         out_specs=[ANY, VMEM],
         scratch_shapes=[
             scratch(planes + 8, parts, tall, LANES),
             scratch(planes + 6, parts, tall, LANES),
             scratch(planes + 4, parts, tall, LANES),
             scratch(planes + 2, parts, tall, LANES),
-            scratch(half + 4, parts, rows, LANES),
+            scratch(half + 4, rows, LANES),
+            scratch(planes, rows, columns),
             pltpu.SemaphoreType.DMA((4,)),
-            pltpu.SemaphoreType.DMA((planes, parts)),
+            pltpu.SemaphoreType.DMA((planes,)),
         ],
         compiler_params=params(24),
         name="top",
-    )(own_a, own_b, own_got_a, own_got_b, correction, pair_weight)
+    )(own_a, own_b, own_got_a, own_got_b, once, correction, pair_weight)
 
     everyone = lax.all_to_all(sums, ("gz", "pair"), 0, 0)
     norm, energy = pl.pallas_call(

time: 83.1 us -> 71.3 us (0.86)
  local copies, waits for them, and re-layouts: 4.3 us -> 0.65 us
  Pallas kernels: 23.8 us -> 20.7 us
  waiting for transfers between devices: 12.3 us -> 9.41 us
  starting transfers between devices: 26.7 us -> 24 us
    unnamed x8 -> x2, local copies, waits for them, and re-layouts: 4.3 us -> 0.65 us
    ppermute x13 -> x10, waiting for transfers between devices: 12.3 us -> 9.41 us  [exchange(): lax.ppermute(value, 'gz', [move for a, b in pairs for move in ((a, b), (b...]
    ppermute x13 -> x10, starting transfers between devices: 26.7 us -> 24 us  [exchange(): lax.ppermute(value, 'gz', [move for a, b in pairs for move in ((a, b), (b...]
    pallas_call x1, Pallas kernels: 9.9 us -> 7.43 us  [per_device(): pl.pallas_call(functools.partial(top_kernel, size, cells), out_shape=[sha...]
  transfers between devices with their start and end apart: 13 -> 10, of which waited for: 7 -> 5; matrix products, arithmetic and copies ran while one was open for 0% -> 0% of each run, Pallas kernels for 7% -> 9%
where the time goes in v3:
time: 71.3 us; the launch traced here: 71 us
  starting transfers between devices  24 us (34%)
  Pallas kernels  20.7 us (29%)
  blocking collectives  15 us (21%)
  waiting for transfers between devices  9.41 us (13%)
  between operations  1.38 us (2%)
    ppermute x10, starting transfers between devices, exchange(): lax.ppermute(value, 'gz', [move for a, b in pairs for move in ((a, b), (b...  24 us
    all_to_all x1, blocking collectives, per_device(): everyone = lax.all_to_all(sums, ('gz', 'pair'), 0, 0)  15 us
    ppermute x10, waiting for transfers between devices, exchange(): lax.ppermute(value, 'gz', [move for a, b in pairs for move in ((a, b), (b...  9.41 us
    pallas_call x1, Pallas kernels, per_device(): pl.pallas_call(functools.partial(top_kernel, size, cells), out_shape=[sha...  7.43 us
    pallas_call x1, Pallas kernels, per_device(): pl.pallas_call(functools.partial(fine_kernel, size), out_shape=[shape(hal...  5.5 us
    pallas_call x1, Pallas kernels, per_device(): pl.pallas_call(functools.partial(low_kernel, size, tuple(partners)), out_...  5.28 us
    pallas_call x1, Pallas kernels, per_device(): pl.pallas_call(functools.partial(total_kernel, groups, cells), out_shape=...  1.48 us
  transfers between devices with their start and end apart: 10, of which 5 were waited for; matrix products, arithmetic and copies ran while one was open for 0% of the time, Pallas kernels for 9%

profile of v3, /device:TPU:0, one launch (start us, length us, event | category | flops | bytes accessed | tf_op | source)
XLA Modules:
  0.0 71.0 jit_solution(17175965967981021565)
XLA Ops:
  0.6 0.0 copy-start
  0.6 0.6 copy-done
  1.3 5.5 %fine.1 = (f32[4,2,256,128]{3,2,1,0:T(8,128)S(1)}, f32[4,2,256,128]{3,2,1,0:T(8,128)S(1)}, f32[3,128,128]{2,1,0:T(8,128)S(1)}, f32[3,128,128]{2,1,0:T(8,128)S(1)}, f32[8,2,256,128]{3,2,1,0:T(8,128)S(1)}) custom-call(bf16[8,8,256,256]{3,2,1,0:T(8,128)(2,1)} %orbitals.1, s32[2]{0:T(128)S(1)} %bitcast.1), custom_call_target="tpu_custom_call" | custom-call | tf_op jit(solution)/shard_map/fine/pallas_call | solution.py:597
  6.8 0.7 collective-permute-start
  7.4 0.7 %collective-permute-start.1 = (f32[4,2,256,128]{3,2,1,0:T(8,128)S(1)}, f32[4,2,256,128]{3,2,1,0:T(8,128)S(1)}, u32[]{:S(2)}, u32[]{:S(2)}) collective-permute-start(f32[4,2,256,128]{3,2,1,0:T(8,128)S(1)} %get-tuple-element.17.own_b), channel_id=1, source_target_pairs={{4,8},{8,4},{12,16},{16,12},{20,24},{24,20},{5,9},{9,5},{13,17},{1... | collective-permute-start | bytes 3145736 | tf_op jit(solution)/shard_map/ppermute | solution.py:571
  8.2 3.9 %collective-permute-start.2 = (f32[3,128,128]{2,1,0:T(8,128)S(1)}, f32[3,128,128]{2,1,0:T(8,128)S(1)}, u32[]{:S(2)}, u32[]{:S(2)}) collective-permute-start(f32[3,128,128]{2,1,0:T(8,128)S(1)} %get-tuple-element.19.sent_a), channel_id=1, source_target_pairs={{0,4},{4,0},{8,12},{12,8},{16,20},{20,16},{24,28},{28,24},{1,5},{5... | collective-permute-start | bytes 589832 | tf_op jit(solution)/shard_map/ppermute | solution.py:571
  12.0 0.7 collective-permute-start.3
  12.7 0.4 collective-permute-done.2.got_a
  13.1 0.0 collective-permute-done.3.got_b
  13.1 1.0 %middle.1 = (f32[8,128,128]{2,1,0:T(8,128)S(1)}, f32[3,128,128]{2,1,0:T(8,128)S(1)}, f32[3,128,128]{2,1,0:T(8,128)S(1)}, f32[64,128]{1,0:T(8,128)S(1)}) custom-call(f32[3,128,128]{2,1,0:T(8,128)S(1)} %get-tuple-element.19.sent_a, f32[3,128,128]{2,1,0:T(8,128)S(1)} %get-tuple-element.20.sent_b, f32[3,128,128]{2,1,0:T(8,128)S(1)} %collective-permute-done.2.got_a, ...), custom_call_target="tpu_custom_call" | custom-call | tf_op jit(solution)/shard_map/middle/pallas_call | solution.py:618
  14.1 17.3 %collective-permute-start.8 = (f32[64,128]{1,0:T(8,128)S(1)}, f32[64,128]{1,0:T(8,128)S(1)}, u32[]{:S(2)}, u32[]{:S(2)}) collective-permute-start(f32[64,128]{1,0:T(8,128)S(1)} %get-tuple-element.24.refs_0_), channel_id=1, source_target_pairs={{0,24},{24,0},{4,28},{28,4},{8,16},{16,8},{12,20},{20,12},{1,25},{... | collective-permute-start | bytes 98312 | tf_op jit(solution)/shard_map/ppermute | solution.py:571
  31.4 0.0 collective-permute-start.7
  31.4 0.0 collective-permute-start.4
  31.4 1.9 %collective-permute-done.8.refs_3_ = f32[64,128]{1,0:T(8,128)S(1)} collective-permute-done((f32[64,128]{1,0:T(8,128)S(1)}, f32[64,128]{1,0:T(8,128)S(1)}, u32[]{:S(2)}, u32[]{:S(2)}) %collective-permute-start.8) | collective-permute-done | bytes 32800 | tf_op jit(solution)/shard_map/ppermute | solution.py:571
  33.3 0.7 collective-permute-start.5
  34.0 2.2 %collective-permute-done.7.refs_2_ = f32[64,128]{1,0:T(8,128)S(1)} collective-permute-done((f32[64,128]{1,0:T(8,128)S(1)}, f32[64,128]{1,0:T(8,128)S(1)}, u32[]{:S(2)}, u32[]{:S(2)}) %collective-permute-start.7) | collective-permute-done | bytes 32800 | tf_op jit(solution)/shard_map/ppermute | solution.py:571
  36.2 0.0 collective-permute-start.6
  36.2 4.2 %collective-permute-done.6.refs_1_ = f32[64,128]{1,0:T(8,128)S(1)} collective-permute-done((f32[64,128]{1,0:T(8,128)S(1)}, f32[64,128]{1,0:T(8,128)S(1)}, u32[]{:S(2)}, u32[]{:S(2)}) %collective-permute-start.6) | collective-permute-done | bytes 32800 | tf_op jit(solution)/shard_map/ppermute | solution.py:571
  40.4 0.1 collective-permute-start.9
  41.1 0.7 collective-permute-done.9.other
  41.8 0.0 collective-permute-done.4.next_a
  41.8 0.0 collective-permute-done.5.next_b
  41.8 5.3 %low.1.correction = f32[8,128,128]{2,1,0:T(8,128)S(1)} custom-call(f32[8,128,128]{2,1,0:T(8,128)S(1)} %get-tuple-element.21.whole, f32[3,128,128]{2,1,0:T(8,128)S(1)} %collective-permute-done.4.next_a, f32[3,128,128]{2,1,0:T(8,128)S(1)} %collective-permute-done.5.next_b, f32[4,64,128]{2,1,0:T(8,128)S(1)} %pack.1.mine, ...), custom_call_target="tpu_custom_call" | custom-call | tf_op jit(solution)/shard_map/low/pallas_call | solution.py:646
  47.1 0.0 collective-permute-done.got_a
  47.1 0.0 collective-permute-done.1.got_b
  47.1 7.4 %top.1 = (f32[1,8,256,256]{3,2,1,0:T(8,128)}, f32[32,2,128]{2,1,0:T(2,128)S(1)}) custom-call(f32[4,2,256,128]{3,2,1,0:T(8,128)S(1)} %get-tuple-element.16.own_a, f32[4,2,256,128]{3,2,1,0:T(8,128)S(1)} %get-tuple-element.17.own_b, f32[4,2,256,128]{3,2,1,0:T(8,128)S(1)} %collective-permute-done.got_a, f32[4,2,256,128]{3,2,1,0:T(8,128)S(1)} %collective-permute-done.1.got_b, ...), custom_call_target="tpu_custom_call" | custom-call | tf_op jit(solution)/shard_map/top/pallas_call | solution.py:671
  54.6 15.0 %all_to_all.5.everyone = f32[32,2,128]{2,1,0:T(2,128)} all-to-all(f32[32,2,128]{2,1,0:T(2,128)S(1)} %get-tuple-element.26), channel_id=1, replica_groups=mesh['gz'=8,'pair'=4] {'gz','pair'}, dimensions={0} | all-to-all | bytes 65536 | tf_op jit(solution)/shard_map/all_to_all | solution.py:690
  69.5 1.5 %total.1 = (f32[1]{0:T(128)}, f32[1]{0:T(128)}) custom-call(f32[32,2,128]{2,1,0:T(2,128)} %all_to_all.5.everyone), custom_call_target="tpu_custom_call" | custom-call | tf_op jit(solution)/shard_map/total/pallas_call | solution.py:691
  (1 shorter events, 0.0 us)
Async XLA Ops:
  0.6 0.7 copy-start
  6.8 40.3 %collective-permute-start = (f32[4,2,256,128]{3,2,1,0:T(8,128)S(1)}, f32[4,2,256,128]{3,2,1,0:T(8,128)S(1)}, u32[]{:S(2)}, u32[]{:S(2)}) collective-permute-start(f32[4,2,256,128]{3,2,1,0:T(8,128)S(1)} %get-tuple-element.16.own_a), channel_id=1, source_target_pairs={{0,4},{4,0},{8,12},{12,8},{16,20},{20,16},{24,28},{28,24},{1,5},{5... | collective-permute-start | bytes 3145736 | tf_op jit(solution)/shard_map/ppermute | solution.py:571
  7.4 39.7 %collective-permute-start.1 = (f32[4,2,256,128]{3,2,1,0:T(8,128)S(1)}, f32[4,2,256,128]{3,2,1,0:T(8,128)S(1)}, u32[]{:S(2)}, u32[]{:S(2)}) collective-permute-start(f32[4,2,256,128]{3,2,1,0:T(8,128)S(1)} %get-tuple-element.17.own_b), channel_id=1, source_target_pairs={{4,8},{8,4},{12,16},{16,12},{20,24},{24,20},{5,9},{9,5},{13,17},{1... | collective-permute-start | bytes 3145736 | tf_op jit(solution)/shard_map/ppermute | solution.py:571
  8.2 4.9 %collective-permute-start.2 = (f32[3,128,128]{2,1,0:T(8,128)S(1)}, f32[3,128,128]{2,1,0:T(8,128)S(1)}, u32[]{:S(2)}, u32[]{:S(2)}) collective-permute-start(f32[3,128,128]{2,1,0:T(8,128)S(1)} %get-tuple-element.19.sent_a), channel_id=1, source_target_pairs={{0,4},{4,0},{8,12},{12,8},{16,20},{20,16},{24,28},{28,24},{1,5},{5... | collective-permute-start | bytes 589832 | tf_op jit(solution)/shard_map/ppermute | solution.py:571
  12.0 1.1 %collective-permute-start.3 = (f32[3,128,128]{2,1,0:T(8,128)S(1)}, f32[3,128,128]{2,1,0:T(8,128)S(1)}, u32[]{:S(2)}, u32[]{:S(2)}) collective-permute-start(f32[3,128,128]{2,1,0:T(8,128)S(1)} %get-tuple-element.20.sent_b), channel_id=1, source_target_pairs={{4,8},{8,4},{12,16},{16,12},{20,24},{24,20},{5,9},{9,5},{13,17},{1... | collective-permute-start | bytes 589832 | tf_op jit(solution)/shard_map/ppermute | solution.py:571
  14.1 19.2 %collective-permute-start.8 = (f32[64,128]{1,0:T(8,128)S(1)}, f32[64,128]{1,0:T(8,128)S(1)}, u32[]{:S(2)}, u32[]{:S(2)}) collective-permute-start(f32[64,128]{1,0:T(8,128)S(1)} %get-tuple-element.24.refs_0_), channel_id=1, source_target_pairs={{0,24},{24,0},{4,28},{28,4},{8,16},{16,8},{12,20},{20,12},{1,25},{... | collective-permute-start | bytes 98312 | tf_op jit(solution)/shard_map/ppermute | solution.py:571
  31.4 4.8 %collective-permute-start.7 = (f32[64,128]{1,0:T(8,128)S(1)}, f32[64,128]{1,0:T(8,128)S(1)}, u32[]{:S(2)}, u32[]{:S(2)}) collective-permute-start(f32[64,128]{1,0:T(8,128)S(1)} %get-tuple-element.24.refs_0_), channel_id=1, source_target_pairs={{0,16},{16,0},{4,20},{20,4},{8,24},{24,8},{12,28},{28,12},{1,17},{... | collective-permute-start | bytes 98312 | tf_op jit(solution)/shard_map/ppermute | solution.py:571
  31.4 10.4 %collective-permute-start.4 = (f32[3,128,128]{2,1,0:T(8,128)S(1)}, f32[3,128,128]{2,1,0:T(8,128)S(1)}, u32[]{:S(2)}, u32[]{:S(2)}) collective-permute-start(f32[3,128,128]{2,1,0:T(8,128)S(1)} %get-tuple-element.22), channel_id=1, source_target_pairs={{0,4},{4,0},{8,12},{12,8},{16,20},{20,16},{24,28},{28,24},{1,5},{5... | collective-permute-start | bytes 589832 | tf_op jit(solution)/shard_map/ppermute | solution.py:571
  33.3 8.5 %collective-permute-start.5 = (f32[3,128,128]{2,1,0:T(8,128)S(1)}, f32[3,128,128]{2,1,0:T(8,128)S(1)}, u32[]{:S(2)}, u32[]{:S(2)}) collective-permute-start(f32[3,128,128]{2,1,0:T(8,128)S(1)} %get-tuple-element.23), channel_id=1, source_target_pairs={{4,8},{8,4},{12,16},{16,12},{20,24},{24,20},{5,9},{9,5},{13,17},{1... | collective-permute-start | bytes 589832 | tf_op jit(solution)/shard_map/ppermute | solution.py:571
  36.2 4.2 %collective-permute-start.6 = (f32[64,128]{1,0:T(8,128)S(1)}, f32[64,128]{1,0:T(8,128)S(1)}, u32[]{:S(2)}, u32[]{:S(2)}) collective-permute-start(f32[64,128]{1,0:T(8,128)S(1)} %get-tuple-element.24.refs_0_), channel_id=1, source_target_pairs={{0,8},{8,0},{4,12},{12,4},{16,24},{24,16},{20,28},{28,20},{1,9},{9... | collective-permute-start | bytes 98312 | tf_op jit(solution)/shard_map/ppermute | solution.py:571
  40.4 1.4 %collective-permute-start.9 = (f32[4,64,128]{2,1,0:T(8,128)S(1)}, f32[4,64,128]{2,1,0:T(8,128)S(1)}, u32[]{:S(2)}, u32[]{:S(2)}) collective-permute-start(f32[4,64,128]{2,1,0:T(8,128)S(1)} %pack.1.mine), channel_id=1, source_target_pairs={{0,4},{4,0},{8,12},{12,8},{16,20},{20,16},{24,28},{28,24},{1,5},{5... | collective-permute-start | bytes 393224 | tf_op jit(solution)/shard_map/ppermute | solution.py:571

commit v4 on v3

--- a/solution.py
+++ b/solution.py
@@ -76,14 +76,13 @@
 
 
 def apply_planes(dst, src, first, last, shift, rows):
-    def plane(z, _):
+    def plane(z):
         for row in range(0, rows, ROWS):
             centre, sums = neighbours(src, z, row, ROWS)
             for h in range(len(centre)):
                 dst[z + shift, h, pl.ds(PAD + row, ROWS), :] = (centre[h] * 3.0 + sums[h]) * NINTH
-        return 0
-
-    lax.fori_loop(first, last, plane, 0)
+
+    each_plane(first, last, plane)
 
 
 def paired_rows(ref, z, rows, offset):
@@ -136,7 +135,8 @@
     return to_bf16(row == parts * (column & (LANES - 1)) + (column >> 7))
 
 
-def fine_kernel(size, orbitals, pair_index, own_a, own_b, coarse_a, coarse_b, once, left, right, source, smooth, sums, in_sem, out_sem):
+def fine_kernel(size, cuts, orbitals, pair_index, *refs):
+    own, (coarse_a, coarse_b, once, left, right, source, smooth, sums, in_sem, out_sem) = refs[: 2 * len(cuts)], refs[2 * len(cuts) :]
     planes, rows = left.shape[0], left.shape[1]
     parts = source.shape[1]
     half = planes // 2
@@ -169,9 +169,12 @@
     lax.fori_loop(0, planes, multiply, 0)
 
     def keep(start, target, k):
-        return pltpu.make_async_copy(source.at[pl.ds(start, half), :, pl.ds(PAD, rows), :], target, out_sem.at[k])
-
-    kept = [keep(1 + half * (1 - odd), own_a, 0), keep(1 + half * odd, own_b, 1)]
+        return pltpu.make_async_copy(source.at[pl.ds(start, target.shape[0]), :, pl.ds(PAD, rows), :], target, out_sem.at[k])
+
+    kept = []
+    for k, cut in enumerate(cuts):
+        kept.append(keep(1 + half * (1 - odd) + cut, own[2 * k], 2 * k))
+        kept.append(keep(1 + half * odd + cut, own[2 * k + 1], 2 * k + 1))
 
     apply_planes(smooth, source, 1, planes + 1, 1, rows)
 
@@ -190,7 +193,7 @@
     for copy in kept:
         copy.start()
 
-    kept.append(pltpu.make_async_copy(smooth.at[pl.ds(2, planes), :, pl.ds(PAD, rows), :], once, out_sem.at[2]))
+    kept.append(pltpu.make_async_copy(smooth.at[pl.ds(2, planes), :, pl.ds(PAD, rows), :], once, out_sem.at[2 * len(cuts)]))
     kept[-1].start()
 
     def coarse(q, _):
@@ -253,7 +256,7 @@
     def _():
         gather((sent_a, sent_b), got_a, got_b)
 
-    apply_planes(smooth, field, jnp.where(me == 0, 2, 1), jnp.where(me == size - 1, planes + 2, planes + 3), 0, rows)
+    apply_planes(smooth, field, 1, planes + 3, 0, rows)
 
     @pl.when(me == 0)
     def _():
@@ -337,6 +340,17 @@
         result[b, centre, :] = packed_apply(smooth, b, rows) + source[b, centre, :] * c2
 
 
+def each_plane(first, last, body, step=2):
+    def several(k, _):
+        for i in range(step):
+            body(first + step * k + i)
+        return 0
+
+    lax.fori_loop(0, (last - first) // step, several, 0)
+    for z in range(last - (last - first) % step, last):
+        body(z)
+
+
 def bring_all(pairs, sem):
     copies = [pltpu.make_async_copy(origin, target, sem.at[k]) for k, (origin, target) in enumerate(pairs)]
     for copy in copies:
@@ -347,36 +361,28 @@
 def start_level(dst, src, grown, planes, shift, offset, level, rows):
     c = scale(level) * NINTH
 
-    def plane(z, _):
+    def plane(z):
         for r in range(0, rows, ROWS):
             centre, total = neighbours(src, z, r, ROWS)
             for h in range(len(centre)):
                 value = (centre[h] * 12.0 + total[h]) * c
                 dst[z + shift, h, pl.ds(PAD + r, ROWS), :] = value + grown[(z + offset) >> 1, pl.ds(r, ROWS), :]
-        return 0
-
-    lax.fori_loop(*planes, plane, 0)
+
+    each_plane(*planes, plane)
 
 
 def sweep_level(dst, src, source, planes, shift, offset, level, rows):
     ratio = scale(level) / NINTH
 
-    def plane(z, _):
+    def plane(z):
         for r in range(0, rows, ROWS):
             centre, total = neighbours(src, z, r, ROWS)
             for h in range(len(centre)):
                 value = source[z + offset, h, pl.ds(PAD + r, ROWS), :]
                 value = value if ratio == 1.0 else value * ratio
                 dst[z + shift, h, pl.ds(PAD + r, ROWS), :] = (centre[h] * 3.0 + total[h] + value) * NINTH
-        return 0
-
-    lax.fori_loop(*planes, plane, 0)
-
-
-def span(me, size, halo, inside, shift=0):
-    low = jnp.where(me == 0, halo, 0)
-    high = jnp.where(me == size - 1, halo + inside, 2 * halo + inside)
-    return low + shift, high + shift
+
+    each_plane(*planes, plane)
 
 
 def blank_outside(ref, me, size, halo, inside, rows):
@@ -439,9 +445,6 @@
             bottom[k, b] = jnp.zeros(bottom.shape[2:], F32)
     for b in (0, size + 1):
         low_result[b, inner, :] = jnp.zeros((low_rows, LANES), F32)
-    blank_outside(first, me, size, 4, planes, rows)
-    blank_outside(second, me, size, 3, planes, rows)
-
     for copy in low_copies:
         copy.wait()
     coarse_levels(size, low_source, low_result, low_blocks, low_smooth, bottom, spare)
@@ -456,59 +459,57 @@
 
     for copy in mid_copies:
         copy.wait()
-    start_level(first, mid, grown, span(me, size, 4, planes, 1), -1, -1, 1, rows)
-    sweep_level(second, first, mid, span(me, size, 3, planes, 1), -1, 1, 1, rows)
-    c1 = scale(1)
-
-    def last(z, _):
+    start_level(first, mid, grown, (1, planes + 9), -1, -1, 1, rows)
+    blank_outside(first, me, size, 4, planes, rows)
+    sweep_level(second, first, mid, (1, planes + 7), -1, 1, 1, rows)
+    blank_outside(second, me, size, 3, planes, rows)
+    ratio = scale(1) / NINTH
+
+    def last(z):
         for r in range(0, rows, ROWS):
             centre, total = neighbours(second, z + 1, r, ROWS)
-            value = centre[0] * THIRD + total[0] * NINTH
-            result[z, pl.ds(r, ROWS), :] = value + mid[z + 3, 0, pl.ds(PAD + r, ROWS), :] * c1
-        return 0
-
-    lax.fori_loop(*span(me, size, 2, planes), last, 0)
-
-
-def top_kernel(size, cells, own_a, own_b, got_a, got_b, once, correction, weight, potential, sums, *scratch):
+            value = mid[z + 3, 0, pl.ds(PAD + r, ROWS), :] * ratio
+            result[z, pl.ds(r, ROWS), :] = (centre[0] * 3.0 + total[0] + value) * NINTH
+
+    each_plane(0, planes + 4, last)
+
+
+def top_kernel(size, cells, cuts, *refs):
+    own, got = refs[: 2 * len(cuts)], refs[2 * len(cuts) : 4 * len(cuts)]
+    once, correction, weight, potential, sums, *scratch = refs[4 * len(cuts) :]
     field, first, second, third, grown, plain, in_sem, out_sem = scratch
-    half, parts, rows = own_a.shape[0], own_a.shape[1], own_a.shape[2]
-    planes = 2 * half
+    planes, parts, rows = once.shape[0], once.shape[1], once.shape[2]
+    half = planes // 2
     mid_rows = correction.shape[1]
     me = lax.axis_index("gz")
     odd = me % 2
 
-    def into(plane):
-        return field.at[pl.ds(plane, half), :, pl.ds(PAD, rows), :]
-
-    copies = bring_all(
-        [
-            (own_a, into(half + half * (1 - odd))),
-            (own_b, into(half + half * odd)),
-            (got_a, into(3 * half * (1 - odd))),
-            (got_b, into(3 * half * odd)),
-        ],
-        in_sem,
-    )
+    def into(origin, plane):
+        return origin, field.at[pl.ds(plane, origin.shape[0]), :, pl.ds(PAD, rows), :]
+
+    moves = []
+    for k, cut in enumerate(cuts):
+        moves += [
+            into(own[2 * k], half + half * (1 - odd) + cut),
+            into(own[2 * k + 1], half + half * odd + cut),
+            into(got[2 * k], 3 * half * (1 - odd) + cut),
+            into(got[2 * k + 1], 3 * half * odd + cut),
+        ]
+    copies = bring_all(moves, in_sem)
     for ref in (field, first, second, third):
         zero_pads(ref, rows)
-    blank_outside(first, me, size, 3, planes, rows)
-    blank_outside(second, me, size, 2, planes, rows)
-    blank_outside(third, me, size, 1, planes, rows)
-
-    def widen(z, _):
+
+    def widen(z):
         value = correction[z]
         grown[z, pl.ds(0, mid_rows, stride=2), :] = value
         grown[z, pl.ds(1, mid_rows, stride=2), :] = value
-        return 0
-
-    lax.fori_loop(*span(me, size, 2, half), widen, 0)
+
+    each_plane(0, half + 4, widen)
 
     for copy in copies:
         copy.wait()
-    low, high = span(me, size, 3, planes, 1)
-    start_level(first, field, grown, (low, 4), -1, 0, 0, rows)
-    start_level(first, field, grown, (4 + planes, high), -1, 0, 0, rows)
+    start_level(first, field, grown, (1, half), -1, 0, 0, rows)
+    start_level(first, field, grown, (half + planes, 2 * half + planes - 1), -1, 0, 0, rows)
     c0 = scale(0)
 
     def begin(z, beside=None):
@@ -519,13 +520,15 @@
                 if beside is not None:
                     value += field[beside, h, pl.ds(PAD + r, ROWS), :] * NINTH
                 first[z + 3, h, pl.ds(PAD + r, ROWS), :] = value * c0 + spread
-        return 0
 
     begin(0, half - 1)
-    lax.fori_loop(1, planes - 1, lambda z, _: begin(z), 0)
+    each_plane(1, planes - 1, begin)
     begin(planes - 1, half + planes)
-    sweep_level(second, first, field, span(me, size, 2, planes, 1), -1, 1, 0, rows)
-    sweep_level(third, second, field, span(me, size, 1, planes, 1), -1, 2, 0, rows)
+    blank_outside(first, me, size, 3, planes, rows)
+    sweep_level(second, first, field, (1, planes + 5), -1, 1, 0, rows)
+    blank_outside(second, me, size, 2, planes, rows)
+    sweep_level(third, second, field, (1, planes + 3), -1, 2, 0, rows)
+    blank_outside(third, me, size, 1, planes, rows)
 
     def give(z):
         return pltpu.make_async_copy(plain.at[z], potential.at[0, z], out_sem.at[z])
@@ -594,11 +597,14 @@
         return pltpu.VMEM(dims, F32)
 
     three = (half + 2) // 2
-    own_a, own_b, coarse_a, coarse_b, once = pl.pallas_call(
-        functools.partial(fine_kernel, size),
-        out_shape=[shape(half, parts, rows, LANES)] * 2 + [shape(three, mid_rows, LANES)] * 2 + [shape(planes, parts, rows, LANES)],
+    counts = (half - half // 2, half // 2)
+    cuts = (0, counts[0])
+    own_shapes = [shape(count, parts, rows, LANES) for count in counts for _ in range(2)]
+    *own, coarse_a, coarse_b, once = pl.pallas_call(
+        functools.partial(fine_kernel, size, cuts),
+        out_shape=own_shapes + [shape(three, mid_rows, LANES)] * 2 + [shape(planes, parts, rows, LANES)],
         in_specs=[HBM, SMEM],
-        out_specs=[ANY, ANY, VMEM, VMEM, ANY],
+        out_specs=[ANY] * len(own_shapes) + [VMEM, VMEM, ANY],
         scratch_shapes=[
             pltpu.VMEM((planes, rows, columns), orbitals.dtype),
             pltpu.VMEM((planes, rows, columns), orbitals.dtype),
@@ -606,7 +612,7 @@
             scratch(planes + 4, parts, tall, LANES),
             scratch(half + 2, mid_rows, LANES),
             pltpu.SemaphoreType.DMA((2, planes)),
-            pltpu.SemaphoreType.DMA((3,)),
+            pltpu.SemaphoreType.DMA((len(own_shapes) + 1,)),
         ],
         compiler_params=params(48),
         name="fine",
@@ -614,6 +620,8 @@
 
     coarse_got_a = exchange(coarse_a, inner)
     coarse_got_b = exchange(coarse_b, outer)
+    got = []
+    got += [exchange(own[0], inner), exchange(own[1], outer)]
 
     whole, next_a, next_b, packed = pl.pallas_call(
         functools.partial(middle_kernel, size),
@@ -631,8 +639,7 @@
         arrived.append(exchange(packed, [(i, i ^ k) for i in range(size) if i < i ^ k]))
     next_got_a = exchange(next_a, inner)
     next_got_b = exchange(next_b, outer)
-    own_got_a = exchange(own_a, inner)
-    own_got_b = exchange(own_b, outer)
+    got += [exchange(own[2], inner), exchange(own[3], outer)]
     mine = pl.pallas_call(
         pack_kernel,
         out_shape=shape(len(partners), low_rows, LANES),
@@ -669,9 +676,9 @@
 
     cells = planes * size * rows * columns
     potential, sums = pl.pallas_call(
-        functools.partial(top_kernel, size, cells),
+        functools.partial(top_kernel, size, cells, cuts),
         out_shape=[shape(1, planes, rows, columns), shape(size * groups, 2, LANES)],
-        in_specs=[ANY] * 4 + [VMEM, VMEM, SMEM],
+        in_specs=[ANY] * 8 + [VMEM, VMEM, SMEM],
         out_specs=[ANY, VMEM],
         scratch_shapes=[
             scratch(planes + 8, parts, tall, LANES),
@@ -680,12 +687,12 @@
             scratch(planes + 2, parts, tall, LANES),
             scratch(half + 4, rows, LANES),
             scratch(planes, rows, columns),
-            pltpu.SemaphoreType.DMA((4,)),
+            pltpu.SemaphoreType.DMA((8,)),
             pltpu.SemaphoreType.DMA((planes,)),
         ],
         compiler_params=params(24),
         name="top",
-    )(own_a, own_b, own_got_a, own_got_b, once, correction, pair_weight)
+    )(*own, *got, once, correction, pair_weight)
 
     everyone = lax.all_to_all(sums, ("gz", "pair"), 0, 0)
     norm, energy = pl.pallas_call(

time: 71.3 us -> 69 us (0.968)
  blocking collectives: 15 us -> 20.1 us
  waiting for transfers between devices: 9.41 us -> 5.66 us
  starting transfers between devices: 24 us -> 20.5 us
    all_to_all x1, blocking collectives: 15 us -> 20.1 us  [per_device(): everyone = lax.all_to_all(sums, ('gz', 'pair'), 0, 0)]
    ppermute x10 -> x12, waiting for transfers between devices: 9.41 us -> 5.66 us  [exchange(): lax.ppermute(value, 'gz', [move for a, b in pairs for move in ((a, b), (b...]
    ppermute x10 -> x12, starting transfers between devices: 24 us -> 20.5 us  [exchange(): lax.ppermute(value, 'gz', [move for a, b in pairs for move in ((a, b), (b...]
  transfers between devices with their start and end apart: 10 -> 12, of which waited for: 5 -> 4; matrix products, arithmetic and copies ran while one was open for 0% -> 0% of each run, Pallas kernels for 9% -> 7%
where the time goes in v4:
time: 69 us; the launch traced here: 68.7 us
  starting transfers between devices  20.5 us (30%)
  Pallas kernels  20.3 us (29%)
  blocking collectives  20.1 us (29%)
  waiting for transfers between devices  5.66 us (8%)
  between operations  1.42 us (2%)
    ppermute x12, starting transfers between devices, exchange(): lax.ppermute(value, 'gz', [move for a, b in pairs for move in ((a, b), (b...  20.5 us
    all_to_all x1, blocking collectives, per_device(): everyone = lax.all_to_all(sums, ('gz', 'pair'), 0, 0)  20.1 us
    pallas_call x1, Pallas kernels, per_device(): pl.pallas_call(functools.partial(top_kernel, size, cells, cuts), out_shap...  7.56 us
    ppermute x12, waiting for transfers between devices, exchange(): lax.ppermute(value, 'gz', [move for a, b in pairs for move in ((a, b), (b...  5.66 us
    pallas_call x1, Pallas kernels, per_device(): pl.pallas_call(functools.partial(fine_kernel, size, cuts), out_shape=own_...  5.31 us
    pallas_call x1, Pallas kernels, per_device(): pl.pallas_call(functools.partial(low_kernel, size, tuple(partners)), out_...  5.09 us
    pallas_call x1, Pallas kernels, per_device(): pl.pallas_call(functools.partial(total_kernel, groups, cells), out_shape=...  1.48 us
  transfers between devices with their start and end apart: 12, of which 4 were waited for; matrix products, arithmetic and copies ran while one was open for 0% of the time, Pallas kernels for 7%

profile of v4, /device:TPU:0, one launch (start us, length us, event | category | flops | bytes accessed | tf_op | source)
XLA Modules:
  0.0 68.7 jit_solution(9032869624332251331)
XLA Ops:
  0.6 0.0 copy-start
  0.6 0.6 copy-done
  1.3 5.3 %fine.1 = (f32[2,2,256,128]{3,2,1,0:T(8,128)S(1)}, f32[2,2,256,128]{3,2,1,0:T(8,128)S(1)}, f32[2,2,256,128]{3,2,1,0:T(8,128)S(1)}, f32[2,2,256,128]{3,2,1,0:T(8,...) custom-call(bf16[8,8,256,256]{3,2,1,0:T(8,128)(2,1)} %orbitals.1, ...), custom_call_target="tpu_custom_call" | custom-call | tf_op jit(solution)/shard_map/fine/pallas_call | solution.py:603
  6.6 0.7 collective-permute-start.4
  7.3 0.7 collective-permute-start.5
  7.9 0.4 collective-permute-done.4.got_a
  8.3 0.0 collective-permute-done.5.got_b
  8.3 0.8 %middle.1 = (f32[8,128,128]{2,1,0:T(8,128)S(1)}, f32[3,128,128]{2,1,0:T(8,128)S(1)}, f32[3,128,128]{2,1,0:T(8,128)S(1)}, f32[64,128]{1,0:T(8,128)S(1)}) custom-call(f32[3,128,128]{2,1,0:T(8,128)S(1)} %get-tuple-element.23.sent_a, f32[3,128,128]{2,1,0:T(8,128)S(1)} %get-tuple-element.24.sent_b, f32[3,128,128]{2,1,0:T(8,128)S(1)} %collective-permute-done.4.got_a, ...), custom_call_target="tpu_custom_call" | custom-call | tf_op jit(solution)/shard_map/middle/pallas_call | solution.py:626
  9.2 10.6 %collective-permute-start.10 = (f32[64,128]{1,0:T(8,128)S(1)}, f32[64,128]{1,0:T(8,128)S(1)}, u32[]{:S(2)}, u32[]{:S(2)}) collective-permute-start(f32[64,128]{1,0:T(8,128)S(1)} %get-tuple-element.28.refs_0_), channel_id=1, source_target_pairs={{0,24},{24,0},{4,28},{28,4},{8,16},{16,8},{12,20},{20,12},{1,25},{... | collective-permute-start | bytes 98312 | tf_op jit(solution)/shard_map/ppermute | solution.py:574
  19.7 0.0 collective-permute-start.9
  19.7 0.6 collective-permute-start.8
  20.4 1.3 %collective-permute-done.10.refs_3_ = f32[64,128]{1,0:T(8,128)S(1)} collective-permute-done((f32[64,128]{1,0:T(8,128)S(1)}, f32[64,128]{1,0:T(8,128)S(1)}, u32[]{:S(2)}, u32[]{:S(2)}) %collective-permute-start.10) | collective-permute-done | bytes 32800 | tf_op jit(solution)/shard_map/ppermute | solution.py:574
  21.6 2.9 %collective-permute-done.9.refs_2_ = f32[64,128]{1,0:T(8,128)S(1)} collective-permute-done((f32[64,128]{1,0:T(8,128)S(1)}, f32[64,128]{1,0:T(8,128)S(1)}, u32[]{:S(2)}, u32[]{:S(2)}) %collective-permute-start.9) | collective-permute-done | bytes 32800 | tf_op jit(solution)/shard_map/ppermute | solution.py:574
  24.5 0.0 collective-permute-done.8.refs_1_
  24.6 0.1 collective-permute-start.11
  24.6 0.5 collective-permute-start
  25.1 0.7 collective-permute-start.1
  25.8 1.4 %collective-permute-start.2 = (f32[2,2,256,128]{3,2,1,0:T(8,128)S(1)}, f32[2,2,256,128]{3,2,1,0:T(8,128)S(1)}, u32[]{:S(2)}, u32[]{:S(2)}) collective-permute-start(f32[2,2,256,128]{3,2,1,0:T(8,128)S(1)} %get-tuple-element.20.refs_2_), channel_id=1, source_target_pairs={{0,4},{4,0},{8,12},{12,8},{16,20},{20,16},{24,28},{28,24},{1,5},{5... | collective-permute-start | bytes 1572872 | tf_op jit(solution)/shard_map/ppermute | solution.py:574
  27.2 0.7 collective-permute-start.3
  27.9 0.0 collective-permute-done.11.other
  27.9 4.0 %collective-permute-start.6 = (f32[3,128,128]{2,1,0:T(8,128)S(1)}, f32[3,128,128]{2,1,0:T(8,128)S(1)}, u32[]{:S(2)}, u32[]{:S(2)}) collective-permute-start(f32[3,128,128]{2,1,0:T(8,128)S(1)} %get-tuple-element.26), channel_id=1, source_target_pairs={{0,4},{4,0},{8,12},{12,8},{16,20},{20,16},{24,28},{28,24},{1,5},{5... | collective-permute-start | bytes 589832 | tf_op jit(solution)/shard_map/ppermute | solution.py:574
  31.9 1.1 %collective-permute-done.6.next_a = f32[3,128,128]{2,1,0:T(8,128)S(1)} collective-permute-done((f32[3,128,128]{2,1,0:T(8,128)S(1)}, f32[3,128,128]{2,1,0:T(8,128)S(1)}, u32[]{:S(2)}, u32[]{:S(2)}) %collective-permute-start.6) | collective-permute-done | bytes 196640 | tf_op jit(solution)/shard_map/ppermute | solution.py:574
  33.0 0.7 collective-permute-start.7
  34.3 0.0 collective-permute-done.7.next_b
  34.3 5.1 %low.1.refs_9_ = f32[8,128,128]{2,1,0:T(8,128)S(1)} custom-call(f32[8,128,128]{2,1,0:T(8,128)S(1)} %get-tuple-element.25.whole, f32[3,128,128]{2,1,0:T(8,128)S(1)} %collective-permute-done.6.next_a, f32[3,128,128]{2,1,0:T(8,128)S(1)} %collective-permute-done.7.next_b, f32[4,64,128]{2,1,0:T(8,128)S(1)} %pack.1.mine, ...), custom_call_target="tpu_custom_call" | custom-call | tf_op jit(solution)/shard_map/low/pallas_call | solution.py:653
  39.4 0.0 collective-permute-done.refs_4_
  39.4 0.0 collective-permute-done.1.refs_5_
  39.4 0.0 collective-permute-done.2.refs_6_
  39.4 0.0 collective-permute-done.3.refs_7_
  39.4 7.6 %top.1 = (f32[1,8,256,256]{3,2,1,0:T(8,128)}, f32[32,2,128]{2,1,0:T(2,128)S(1)}) custom-call(f32[2,2,256,128]{3,2,1,0:T(8,128)S(1)} %get-tuple-element.18.refs_0_, f32[2,2,256,128]{3,2,1,0:T(8,128)S(1)} %get-tuple-element.19.refs_1_, f32[2,2,256,128]{3,2,1,0:T(8,128)S(1)} %get-tuple-element.20.refs_2_, f32[2,2,256,128]{3,2,1,0:T(8,128)S(1)} %get-tuple-element.21.refs_3_, ...), custom_call_target="tpu_custom_call" | custom-call | tf_op jit(solution)/shard_map/top/pallas_call | solution.py:678
  47.0 20.1 %all_to_all.5.everyone = f32[32,2,128]{2,1,0:T(2,128)} all-to-all(f32[32,2,128]{2,1,0:T(2,128)S(1)} %get-tuple-element.30), channel_id=1, replica_groups=mesh['gz'=8,'pair'=4] {'gz','pair'}, dimensions={0} | all-to-all | bytes 65536 | tf_op jit(solution)/shard_map/all_to_all | solution.py:697
  67.2 1.5 %total.1 = (f32[1]{0:T(128)}, f32[1]{0:T(128)}) custom-call(f32[32,2,128]{2,1,0:T(2,128)} %all_to_all.5.everyone), custom_call_target="tpu_custom_call" | custom-call | tf_op jit(solution)/shard_map/total/pallas_call | solution.py:698
  (1 shorter events, 0.0 us)
Async XLA Ops:
  0.6 0.7 copy-start
  6.6 1.7 %collective-permute-start.4 = (f32[3,128,128]{2,1,0:T(8,128)S(1)}, f32[3,128,128]{2,1,0:T(8,128)S(1)}, u32[]{:S(2)}, u32[]{:S(2)}) collective-permute-start(f32[3,128,128]{2,1,0:T(8,128)S(1)} %get-tuple-element.23.sent_a), channel_id=1, source_target_pairs={{0,4},{4,0},{8,12},{12,8},{16,20},{20,16},{24,28},{28,24},{1,5},{5... | collective-permute-start | bytes 589832 | tf_op jit(solution)/shard_map/ppermute | solution.py:574
  7.3 1.1 %collective-permute-start.5 = (f32[3,128,128]{2,1,0:T(8,128)S(1)}, f32[3,128,128]{2,1,0:T(8,128)S(1)}, u32[]{:S(2)}, u32[]{:S(2)}) collective-permute-start(f32[3,128,128]{2,1,0:T(8,128)S(1)} %get-tuple-element.24.sent_b), channel_id=1, source_target_pairs={{4,8},{8,4},{12,16},{16,12},{20,24},{24,20},{5,9},{9,5},{13,17},{1... | collective-permute-start | bytes 589832 | tf_op jit(solution)/shard_map/ppermute | solution.py:574
  9.2 12.5 %collective-permute-start.10 = (f32[64,128]{1,0:T(8,128)S(1)}, f32[64,128]{1,0:T(8,128)S(1)}, u32[]{:S(2)}, u32[]{:S(2)}) collective-permute-start(f32[64,128]{1,0:T(8,128)S(1)} %get-tuple-element.28.refs_0_), channel_id=1, source_target_pairs={{0,24},{24,0},{4,28},{28,4},{8,16},{16,8},{12,20},{20,12},{1,25},{... | collective-permute-start | bytes 98312 | tf_op jit(solution)/shard_map/ppermute | solution.py:574
  19.7 4.8 %collective-permute-start.9 = (f32[64,128]{1,0:T(8,128)S(1)}, f32[64,128]{1,0:T(8,128)S(1)}, u32[]{:S(2)}, u32[]{:S(2)}) collective-permute-start(f32[64,128]{1,0:T(8,128)S(1)} %get-tuple-element.28.refs_0_), channel_id=1, source_target_pairs={{0,16},{16,0},{4,20},{20,4},{8,24},{24,8},{12,28},{28,12},{1,17},{... | collective-permute-start | bytes 98312 | tf_op jit(solution)/shard_map/ppermute | solution.py:574
  19.7 4.8 %collective-permute-start.8 = (f32[64,128]{1,0:T(8,128)S(1)}, f32[64,128]{1,0:T(8,128)S(1)}, u32[]{:S(2)}, u32[]{:S(2)}) collective-permute-start(f32[64,128]{1,0:T(8,128)S(1)} %get-tuple-element.28.refs_0_), channel_id=1, source_target_pairs={{0,8},{8,0},{4,12},{12,4},{16,24},{24,16},{20,28},{28,20},{1,9},{9... | collective-permute-start | bytes 98312 | tf_op jit(solution)/shard_map/ppermute | solution.py:574
  24.6 3.3 %collective-permute-start.11 = (f32[4,64,128]{2,1,0:T(8,128)S(1)}, f32[4,64,128]{2,1,0:T(8,128)S(1)}, u32[]{:S(2)}, u32[]{:S(2)}) collective-permute-start(f32[4,64,128]{2,1,0:T(8,128)S(1)} %pack.1.mine), channel_id=1, source_target_pairs={{0,4},{4,0},{8,12},{12,8},{16,20},{20,16},{24,28},{28,24},{1,5},{5... | collective-permute-start | bytes 393224 | tf_op jit(solution)/shard_map/ppermute | solution.py:574
  24.6 14.8 %collective-permute-start = (f32[2,2,256,128]{3,2,1,0:T(8,128)S(1)}, f32[2,2,256,128]{3,2,1,0:T(8,128)S(1)}, u32[]{:S(2)}, u32[]{:S(2)}) collective-permute-start(f32[2,2,256,128]{3,2,1,0:T(8,128)S(1)} %get-tuple-element.18.refs_0_), channel_id=1, source_target_pairs={{0,4},{4,0},{8,12},{12,8},{16,20},{20,16},{24,28},{28,24},{1,5},{5... | collective-permute-start | bytes 1572872 | tf_op jit(solution)/shard_map/ppermute | solution.py:574
  25.1 14.3 %collective-permute-start.1 = (f32[2,2,256,128]{3,2,1,0:T(8,128)S(1)}, f32[2,2,256,128]{3,2,1,0:T(8,128)S(1)}, u32[]{:S(2)}, u32[]{:S(2)}) collective-permute-start(f32[2,2,256,128]{3,2,1,0:T(8,128)S(1)} %get-tuple-element.19.refs_1_), channel_id=1, source_target_pairs={{4,8},{8,4},{12,16},{16,12},{20,24},{24,20},{5,9},{9,5},{13,17},{1... | collective-permute-start | bytes 1572872 | tf_op jit(solution)/shard_map/ppermute | solution.py:574
  25.8 13.6 %collective-permute-start.2 = (f32[2,2,256,128]{3,2,1,0:T(8,128)S(1)}, f32[2,2,256,128]{3,2,1,0:T(8,128)S(1)}, u32[]{:S(2)}, u32[]{:S(2)}) collective-permute-start(f32[2,2,256,128]{3,2,1,0:T(8,128)S(1)} %get-tuple-element.20.refs_2_), channel_id=1, source_target_pairs={{0,4},{4,0},{8,12},{12,8},{16,20},{20,16},{24,28},{28,24},{1,5},{5... | collective-permute-start | bytes 1572872 | tf_op jit(solution)/shard_map/ppermute | solution.py:574
  27.2 12.2 %collective-permute-start.3 = (f32[2,2,256,128]{3,2,1,0:T(8,128)S(1)}, f32[2,2,256,128]{3,2,1,0:T(8,128)S(1)}, u32[]{:S(2)}, u32[]{:S(2)}) collective-permute-start(f32[2,2,256,128]{3,2,1,0:T(8,128)S(1)} %get-tuple-element.21.refs_3_), channel_id=1, source_target_pairs={{4,8},{8,4},{12,16},{16,12},{20,24},{24,20},{5,9},{9,5},{13,17},{1... | collective-permute-start | bytes 1572872 | tf_op jit(solution)/shard_map/ppermute | solution.py:574
  27.9 5.1 %collective-permute-start.6 = (f32[3,128,128]{2,1,0:T(8,128)S(1)}, f32[3,128,128]{2,1,0:T(8,128)S(1)}, u32[]{:S(2)}, u32[]{:S(2)}) collective-permute-start(f32[3,128,128]{2,1,0:T(8,128)S(1)} %get-tuple-element.26), channel_id=1, source_target_pairs={{0,4},{4,0},{8,12},{12,8},{16,20},{20,16},{24,28},{28,24},{1,5},{5... | collective-permute-start | bytes 589832 | tf_op jit(solution)/shard_map/ppermute | solution.py:574
  33.0 1.3 %collective-permute-start.7 = (f32[3,128,128]{2,1,0:T(8,128)S(1)}, f32[3,128,128]{2,1,0:T(8,128)S(1)}, u32[]{:S(2)}, u32[]{:S(2)}) collective-permute-start(f32[3,128,128]{2,1,0:T(8,128)S(1)} %get-tuple-element.27), channel_id=1, source_target_pairs={{4,8},{8,4},{12,16},{16,12},{20,24},{24,20},{5,9},{9,5},{13,17},{1... | collective-permute-start | bytes 589832 | tf_op jit(solution)/shard_map/ppermute | solution.py:574

commit v5 on v4

--- a/solution.py
+++ b/solution.py
@@ -476,8 +476,8 @@
 
 def top_kernel(size, cells, cuts, *refs):
     own, got = refs[: 2 * len(cuts)], refs[2 * len(cuts) : 4 * len(cuts)]
-    once, correction, weight, potential, sums, *scratch = refs[4 * len(cuts) :]
-    field, first, second, third, grown, plain, in_sem, out_sem = scratch
+    once, correction, weight, third, sums, *scratch = refs[4 * len(cuts) :]
+    field, first, second, grown, in_sem = scratch
     planes, parts, rows = once.shape[0], once.shape[1], once.shape[2]
     half = planes // 2
     mid_rows = correction.shape[1]
@@ -530,20 +530,8 @@
     sweep_level(third, second, field, (1, planes + 3), -1, 2, 0, rows)
     blank_outside(third, me, size, 1, planes, rows)
 
-    def give(z):
-        return pltpu.make_async_copy(plain.at[z], potential.at[0, z], out_sem.at[z])
-
-    row, column = iota((2 * parts * LANES, parts * LANES), 0), iota((2 * parts * LANES, parts * LANES), 1)
-    in_order = to_bf16(column == parts * (row & (LANES - 1)) + ((row >> 7) & (parts - 1)))
-
     def final(z, totals):
         squares, products = totals
-        here = pl.ds(PAD, rows)
-        whole = [third[z + 1, h, here, :] for h in range(parts)]
-        upper = [value.astype(BF16) for value in whole]
-        lower = [(value - part.astype(F32)).astype(BF16) for value, part in zip(whole, upper)]
-        plain[z] = jnp.dot(jnp.concatenate(upper + lower, axis=1), in_order, preferred_element_type=F32)
-        give(z).start()
         for r in range(0, rows, ROWS):
             centre, total = neighbours(third, z + 1, r, ROWS)
             for h in range(parts):
@@ -553,10 +541,28 @@
                 products += jnp.sum((f * centre[h]).reshape(ROWS // 8, 8, LANES), axis=0)
         return squares, products
 
-    squares, products = lax.fori_loop(0, planes, final, (jnp.zeros((8, LANES), F32),) * 2)
+    squares, products = lax.fori_loop(0, planes // 2, lambda k, t: final(2 * k + 1, final(2 * k, t)), (jnp.zeros((8, LANES), F32),) * 2)
     products = products * (weight[0] * (-0.5 / cells))
     both = jnp.concatenate([jnp.sum(squares, axis=0, keepdims=True), jnp.sum(products, axis=0, keepdims=True)], axis=0)
     sums[...] = jnp.broadcast_to(both[None], sums.shape)
+
+
+def output_kernel(third, potential, plain, sem):
+    planes, parts, rows = plain.shape[0], third.shape[1], plain.shape[1]
+    row, column = iota((2 * parts * LANES, parts * LANES), 0), iota((2 * parts * LANES, parts * LANES), 1)
+    in_order = to_bf16(column == parts * (row & (LANES - 1)) + ((row >> 7) & (parts - 1)))
+
+    def give(z):
+        return pltpu.make_async_copy(plain.at[z], potential.at[0, z], sem.at[z])
+
+    def plane(z):
+        value = [third[z + 1, h, pl.ds(PAD, rows), :] for h in range(parts)]
+        upper = [part.astype(BF16) for part in value]
+        lower = [(part - high.astype(F32)).astype(BF16) for part, high in zip(value, upper)]
+        plain[z] = jnp.dot(jnp.concatenate(upper + lower, axis=1), in_order, preferred_element_type=F32)
+        give(z).start()
+
+    each_plane(0, planes, plane)
     for z in range(planes):
         give(z).wait()
 
@@ -597,7 +603,7 @@
         return pltpu.VMEM(dims, F32)
 
     three = (half + 2) // 2
-    counts = (half - half // 2, half // 2)
+    counts = (half // 2, half // 2)
     cuts = (0, counts[0])
     own_shapes = [shape(count, parts, rows, LANES) for count in counts for _ in range(2)]
     *own, coarse_a, coarse_b, once = pl.pallas_call(
@@ -675,31 +681,39 @@
     )(whole, next_got_a, next_got_b, mine, other)
 
     cells = planes * size * rows * columns
-    potential, sums = pl.pallas_call(
+    third, sums = pl.pallas_call(
         functools.partial(top_kernel, size, cells, cuts),
-        out_shape=[shape(1, planes, rows, columns), shape(size * groups, 2, LANES)],
+        out_shape=[shape(planes + 2, parts, tall, LANES), shape(size * groups, 2, LANES)],
         in_specs=[ANY] * 8 + [VMEM, VMEM, SMEM],
-        out_specs=[ANY, VMEM],
+        out_specs=[VMEM, VMEM],
         scratch_shapes=[
             scratch(planes + 8, parts, tall, LANES),
             scratch(planes + 6, parts, tall, LANES),
             scratch(planes + 4, parts, tall, LANES),
-            scratch(planes + 2, parts, tall, LANES),
             scratch(half + 4, rows, LANES),
-            scratch(planes, rows, columns),
             pltpu.SemaphoreType.DMA((8,)),
-            pltpu.SemaphoreType.DMA((planes,)),
         ],
         compiler_params=params(24),
         name="top",
     )(*own, *got, once, correction, pair_weight)
 
+    potential = pl.pallas_call(
+        output_kernel,
+        out_shape=shape(1, planes, rows, columns),
+        in_specs=[VMEM],
+        out_specs=ANY,
+        scratch_shapes=[scratch(planes, rows, columns), pltpu.SemaphoreType.DMA((planes,))],
+        compiler_params=params(8),
+        cost_estimate=pl.CostEstimate(flops=10**9, bytes_accessed=10**7, transcendentals=0),
+        name="output",
+    )(third)
     everyone = lax.all_to_all(sums, ("gz", "pair"), 0, 0)
     norm, energy = pl.pallas_call(
         functools.partial(total_kernel, groups, cells),
         out_shape=[shape(1)] * 2,
         in_specs=[VMEM],
         out_specs=[SMEM] * 2,
+        compiler_params=params(4),
         name="total",
     )(everyone)
     return (potential, norm, energy)

time: 69 us -> 67 us (0.971)
  blocking collectives: 20.1 us -> 0 us
  starting transfers between devices: 20.5 us -> 33.6 us
  waiting for transfers between devices: 5.66 us -> 10.6 us
    all_to_all x1 -> x0, blocking collectives: 20.1 us -> none  [per_device(): everyone = lax.all_to_all(sums, ('gz', 'pair'), 0, 0)]
    all_to_all x0 -> x1, starting transfers between devices: none -> 13.1 us  [per_device(): everyone = lax.all_to_all(sums, ('gz', 'pair'), 0, 0)]
    all_to_all x0 -> x1, waiting for transfers between devices: none -> 4.97 us  [per_device(): everyone = lax.all_to_all(sums, ('gz', 'pair'), 0, 0)]
    pallas_call x0 -> x1, Pallas kernels: none -> 2.32 us  [per_device(): pl.pallas_call(output_kernel, out_shape=shape(1, planes, rows, columns),...]
    pallas_call x1, Pallas kernels: 7.56 us -> 6.15 us  [per_device(): pl.pallas_call(functools.partial(top_kernel, size, cells, cuts), out_shap...]
    pallas_call x1, Pallas kernels: 1.48 us -> 0.73 us  [per_device(): pl.pallas_call(functools.partial(total_kernel, groups, cells), out_shape=...]
  transfers between devices with their start and end apart: 12 -> 13, of which waited for: 4 -> 5; matrix products, arithmetic and copies ran while one was open for 0% -> 0% of each run, Pallas kernels for 7% -> 11%
where the time goes in v5:
time: 67 us; the launch traced here: 66.7 us
  starting transfers between devices  33.6 us (50%)
  Pallas kernels  20.4 us (30%)
  waiting for transfers between devices  10.6 us (16%)
  between operations  1.43 us (2%)
    ppermute x12, starting transfers between devices, exchange(): lax.ppermute(value, 'gz', [move for a, b in pairs for move in ((a, b), (b...  20.5 us
    all_to_all x1, starting transfers between devices, per_device(): everyone = lax.all_to_all(sums, ('gz', 'pair'), 0, 0)  13.1 us
    pallas_call x1, Pallas kernels, per_device(): pl.pallas_call(functools.partial(top_kernel, size, cells, cuts), out_shap...  6.15 us
    ppermute x12, waiting for transfers between devices, exchange(): lax.ppermute(value, 'gz', [move for a, b in pairs for move in ((a, b), (b...  5.66 us
    pallas_call x1, Pallas kernels, per_device(): pl.pallas_call(functools.partial(fine_kernel, size, cuts), out_shape=own_...  5.31 us
    pallas_call x1, Pallas kernels, per_device(): pl.pallas_call(functools.partial(low_kernel, size, tuple(partners)), out_...  5.09 us
    all_to_all x1, waiting for transfers between devices, per_device(): everyone = lax.all_to_all(sums, ('gz', 'pair'), 0, 0)  4.97 us
    pallas_call x1, Pallas kernels, per_device(): pl.pallas_call(output_kernel, out_shape=shape(1, planes, rows, columns),...  2.32 us
  transfers between devices with their start and end apart: 13, of which 5 were waited for; matrix products, arithmetic and copies ran while one was open for 0% of the time, Pallas kernels for 11%

profile of v5, /device:TPU:0, one launch (start us, length us, event | category | flops | bytes accessed | tf_op | source)
XLA Modules:
  0.0 66.7 jit_solution(6622197811713623611)
XLA Ops:
  0.6 0.0 copy-start
  0.6 0.6 copy-done
  1.3 5.3 %fine.1 = (f32[2,2,256,128]{3,2,1,0:T(8,128)S(1)}, f32[2,2,256,128]{3,2,1,0:T(8,128)S(1)}, f32[2,2,256,128]{3,2,1,0:T(8,128)S(1)}, f32[2,2,256,128]{3,2,1,0:T(8,...) custom-call(bf16[8,8,256,256]{3,2,1,0:T(8,128)(2,1)} %orbitals.1, ...), custom_call_target="tpu_custom_call" | custom-call | tf_op jit(solution)/shard_map/fine/pallas_call | solution.py:609
  6.6 0.7 collective-permute-start.4
  7.3 0.7 collective-permute-start.5
  7.9 0.4 collective-permute-done.4.got_a
  8.3 0.0 collective-permute-done.5.got_b
  8.3 0.8 %middle.1 = (f32[8,128,128]{2,1,0:T(8,128)S(1)}, f32[3,128,128]{2,1,0:T(8,128)S(1)}, f32[3,128,128]{2,1,0:T(8,128)S(1)}, f32[64,128]{1,0:T(8,128)S(1)}) custom-call(f32[3,128,128]{2,1,0:T(8,128)S(1)} %get-tuple-element.23.sent_a, f32[3,128,128]{2,1,0:T(8,128)S(1)} %get-tuple-element.24.sent_b, f32[3,128,128]{2,1,0:T(8,128)S(1)} %collective-permute-done.4.got_a, ...), custom_call_target="tpu_custom_call" | custom-call | tf_op jit(solution)/shard_map/middle/pallas_call | solution.py:632
  9.2 10.6 %collective-permute-start.10 = (f32[64,128]{1,0:T(8,128)S(1)}, f32[64,128]{1,0:T(8,128)S(1)}, u32[]{:S(2)}, u32[]{:S(2)}) collective-permute-start(f32[64,128]{1,0:T(8,128)S(1)} %get-tuple-element.28.refs_0_), channel_id=1, source_target_pairs={{0,24},{24,0},{4,28},{28,4},{8,16},{16,8},{12,20},{20,12},{1,25},{... | collective-permute-start | bytes 98312 | tf_op jit(solution)/shard_map/ppermute | solution.py:580
  19.7 0.0 collective-permute-start.9
  19.7 0.6 collective-permute-start.8
  20.4 1.3 %collective-permute-done.10.refs_3_ = f32[64,128]{1,0:T(8,128)S(1)} collective-permute-done((f32[64,128]{1,0:T(8,128)S(1)}, f32[64,128]{1,0:T(8,128)S(1)}, u32[]{:S(2)}, u32[]{:S(2)}) %collective-permute-start.10) | collective-permute-done | bytes 32800 | tf_op jit(solution)/shard_map/ppermute | solution.py:580
  21.6 2.9 %collective-permute-done.9.refs_2_ = f32[64,128]{1,0:T(8,128)S(1)} collective-permute-done((f32[64,128]{1,0:T(8,128)S(1)}, f32[64,128]{1,0:T(8,128)S(1)}, u32[]{:S(2)}, u32[]{:S(2)}) %collective-permute-start.9) | collective-permute-done | bytes 32800 | tf_op jit(solution)/shard_map/ppermute | solution.py:580
  24.5 0.0 collective-permute-done.8.refs_1_
  24.6 0.1 collective-permute-start.11
  24.6 0.5 collective-permute-start
  25.1 0.7 %collective-permute-start.1 = (f32[2,2,256,128]{3,2,1,0:T(8,128)S(1)}, f32[2,2,256,128]{3,2,1,0:T(8,128)S(1)}, u32[]{:S(2)}, u32[]{:S(2)}) collective-permute-start(f32[2,2,256,128]{3,2,1,0:T(8,128)S(1)} %get-tuple-element.19.refs_1_), channel_id=1, source_target_pairs={{4,8},{8,4},{12,16},{16,12},{20,24},{24,20},{5,9},{9,5},{13,17},{1... | collective-permute-start | bytes 1572872 | tf_op jit(solution)/shard_map/ppermute | solution.py:580
  25.8 1.4 %collective-permute-start.2 = (f32[2,2,256,128]{3,2,1,0:T(8,128)S(1)}, f32[2,2,256,128]{3,2,1,0:T(8,128)S(1)}, u32[]{:S(2)}, u32[]{:S(2)}) collective-permute-start(f32[2,2,256,128]{3,2,1,0:T(8,128)S(1)} %get-tuple-element.20.refs_2_), channel_id=1, source_target_pairs={{0,4},{4,0},{8,12},{12,8},{16,20},{20,16},{24,28},{28,24},{1,5},{5... | collective-permute-start | bytes 1572872 | tf_op jit(solution)/shard_map/ppermute | solution.py:580
  27.2 0.7 %collective-permute-start.3 = (f32[2,2,256,128]{3,2,1,0:T(8,128)S(1)}, f32[2,2,256,128]{3,2,1,0:T(8,128)S(1)}, u32[]{:S(2)}, u32[]{:S(2)}) collective-permute-start(f32[2,2,256,128]{3,2,1,0:T(8,128)S(1)} %get-tuple-element.21.refs_3_), channel_id=1, source_target_pairs={{4,8},{8,4},{12,16},{16,12},{20,24},{24,20},{5,9},{9,5},{13,17},{1... | collective-permute-start | bytes 1572872 | tf_op jit(solution)/shard_map/ppermute | solution.py:580
  27.9 0.0 collective-permute-done.11.other
  27.9 4.0 %collective-permute-start.6 = (f32[3,128,128]{2,1,0:T(8,128)S(1)}, f32[3,128,128]{2,1,0:T(8,128)S(1)}, u32[]{:S(2)}, u32[]{:S(2)}) collective-permute-start(f32[3,128,128]{2,1,0:T(8,128)S(1)} %get-tuple-element.26), channel_id=1, source_target_pairs={{0,4},{4,0},{8,12},{12,8},{16,20},{20,16},{24,28},{28,24},{1,5},{5... | collective-permute-start | bytes 589832 | tf_op jit(solution)/shard_map/ppermute | solution.py:580
  31.9 1.1 %collective-permute-done.6.next_a = f32[3,128,128]{2,1,0:T(8,128)S(1)} collective-permute-done((f32[3,128,128]{2,1,0:T(8,128)S(1)}, f32[3,128,128]{2,1,0:T(8,128)S(1)}, u32[]{:S(2)}, u32[]{:S(2)}) %collective-permute-start.6) | collective-permute-done | bytes 196640 | tf_op jit(solution)/shard_map/ppermute | solution.py:580
  33.0 0.7 collective-permute-start.7
  34.3 0.0 collective-permute-done.7.next_b
  34.3 5.1 %low.1.refs_9_ = f32[8,128,128]{2,1,0:T(8,128)S(1)} custom-call(f32[8,128,128]{2,1,0:T(8,128)S(1)} %get-tuple-element.25.whole, f32[3,128,128]{2,1,0:T(8,128)S(1)} %collective-permute-done.6.next_a, f32[3,128,128]{2,1,0:T(8,128)S(1)} %collective-permute-done.7.next_b, f32[4,64,128]{2,1,0:T(8,128)S(1)} %pack.1.mine, ...), custom_call_target="tpu_custom_call" | custom-call | tf_op jit(solution)/shard_map/low/pallas_call | solution.py:659
  39.4 0.0 collective-permute-done.refs_4_
  39.4 0.0 collective-permute-done.1.refs_5_
  39.4 0.0 collective-permute-done.2.refs_6_
  39.4 0.0 collective-permute-done.3.refs_7_
  39.4 6.1 %top.1 = (f32[10,2,272,128]{3,2,1,0:T(8,128)S(1)}, f32[32,2,128]{2,1,0:T(2,128)}) custom-call(f32[2,2,256,128]{3,2,1,0:T(8,128)S(1)} %get-tuple-element.18.refs_0_, f32[2,2,256,128]{3,2,1,0:T(8,128)S(1)} %get-tuple-element.19.refs_1_, f32[2,2,256,128]{3,2,1,0:T(8,128)S(1)} %get-tuple-element.20.refs_2_, f32[2,2,256,128]{3,2,1,0:T(8,128)S(1)} %get-tuple-element.21.refs_3_, ...), custom_call_target="tpu_custom_call" | custom-call | tf_op jit(solution)/shard_map/top/pallas_call | solution.py:684
  45.6 13.1 %all-to-all-start = ((f32[32,2,128]{2,1,0:T(2,128)}), f32[32,2,128]{2,1,0:T(2,128)S(1)}, u32[]{:S(2)}, u32[]{:S(2)}) async-start(f32[32,2,128]{2,1,0:T(2,128)} %get-tuple-element.30), calls=%async_computation | async-start | bytes 65536 | tf_op jit(solution)/shard_map/all_to_all | solution.py:710
  58.7 2.3 %output.1 = f32[1,8,256,256]{3,2,1,0:T(8,128)} custom-call(f32[10,2,272,128]{3,2,1,0:T(8,128)S(1)} %get-tuple-element.29.third), custom_call_target="tpu_custom_call" | custom-call | flops 1000000000 | bytes 10000000 | tf_op jit(solution)/shard_map/output/pallas_call | solution.py:700
  61.0 5.0 %all-to-all-done.everyone = f32[32,2,128]{2,1,0:T(2,128)S(1)} async-done(((f32[32,2,128]{2,1,0:T(2,128)}), f32[32,2,128]{2,1,0:T(2,128)S(1)}, u32[]{:S(2)}, u32[]{:S(2)}) %all-to-all-start) | async-done | bytes 32800 | tf_op jit(solution)/shard_map/all_to_all | solution.py:710
  66.0 0.7 %total.1 = (f32[1]{0:T(128)}, f32[1]{0:T(128)}) custom-call(f32[32,2,128]{2,1,0:T(2,128)S(1)} %all-to-all-done.everyone), custom_call_target="tpu_custom_call" | custom-call | tf_op jit(solution)/shard_map/total/pallas_call | solution.py:711
  (1 shorter events, 0.0 us)
Async XLA Ops:
  0.6 0.7 copy-start
  6.6 1.7 %collective-permute-start.4 = (f32[3,128,128]{2,1,0:T(8,128)S(1)}, f32[3,128,128]{2,1,0:T(8,128)S(1)}, u32[]{:S(2)}, u32[]{:S(2)}) collective-permute-start(f32[3,128,128]{2,1,0:T(8,128)S(1)} %get-tuple-element.23.sent_a), channel_id=1, source_target_pairs={{0,4},{4,0},{8,12},{12,8},{16,20},{20,16},{24,28},{28,24},{1,5},{5... | collective-permute-start | bytes 589832 | tf_op jit(solution)/shard_map/ppermute | solution.py:580
  7.3 1.1 %collective-permute-start.5 = (f32[3,128,128]{2,1,0:T(8,128)S(1)}, f32[3,128,128]{2,1,0:T(8,128)S(1)}, u32[]{:S(2)}, u32[]{:S(2)}) collective-permute-start(f32[3,128,128]{2,1,0:T(8,128)S(1)} %get-tuple-element.24.sent_b), channel_id=1, source_target_pairs={{4,8},{8,4},{12,16},{16,12},{20,24},{24,20},{5,9},{9,5},{13,17},{1... | collective-permute-start | bytes 589832 | tf_op jit(solution)/shard_map/ppermute | solution.py:580
  9.2 12.5 %collective-permute-start.10 = (f32[64,128]{1,0:T(8,128)S(1)}, f32[64,128]{1,0:T(8,128)S(1)}, u32[]{:S(2)}, u32[]{:S(2)}) collective-permute-start(f32[64,128]{1,0:T(8,128)S(1)} %get-tuple-element.28.refs_0_), channel_id=1, source_target_pairs={{0,24},{24,0},{4,28},{28,4},{8,16},{16,8},{12,20},{20,12},{1,25},{... | collective-permute-start | bytes 98312 | tf_op jit(solution)/shard_map/ppermute | solution.py:580
  19.7 4.8 %collective-permute-start.9 = (f32[64,128]{1,0:T(8,128)S(1)}, f32[64,128]{1,0:T(8,128)S(1)}, u32[]{:S(2)}, u32[]{:S(2)}) collective-permute-start(f32[64,128]{1,0:T(8,128)S(1)} %get-tuple-element.28.refs_0_), channel_id=1, source_target_pairs={{0,16},{16,0},{4,20},{20,4},{8,24},{24,8},{12,28},{28,12},{1,17},{... | collective-permute-start | bytes 98312 | tf_op jit(solution)/shard_map/ppermute | solution.py:580
  19.7 4.8 %collective-permute-start.8 = (f32[64,128]{1,0:T(8,128)S(1)}, f32[64,128]{1,0:T(8,128)S(1)}, u32[]{:S(2)}, u32[]{:S(2)}) collective-permute-start(f32[64,128]{1,0:T(8,128)S(1)} %get-tuple-element.28.refs_0_), channel_id=1, source_target_pairs={{0,8},{8,0},{4,12},{12,4},{16,24},{24,16},{20,28},{28,20},{1,9},{9... | collective-permute-start | bytes 98312 | tf_op jit(solution)/shard_map/ppermute | solution.py:580
  24.6 3.3 %collective-permute-start.11 = (f32[4,64,128]{2,1,0:T(8,128)S(1)}, f32[4,64,128]{2,1,0:T(8,128)S(1)}, u32[]{:S(2)}, u32[]{:S(2)}) collective-permute-start(f32[4,64,128]{2,1,0:T(8,128)S(1)} %pack.1.mine), channel_id=1, source_target_pairs={{0,4},{4,0},{8,12},{12,8},{16,20},{20,16},{24,28},{28,24},{1,5},{5... | collective-permute-start | bytes 393224 | tf_op jit(solution)/shard_map/ppermute | solution.py:580
  24.6 14.8 %collective-permute-start = (f32[2,2,256,128]{3,2,1,0:T(8,128)S(1)}, f32[2,2,256,128]{3,2,1,0:T(8,128)S(1)}, u32[]{:S(2)}, u32[]{:S(2)}) collective-permute-start(f32[2,2,256,128]{3,2,1,0:T(8,128)S(1)} %get-tuple-element.18.refs_0_), channel_id=1, source_target_pairs={{0,4},{4,0},{8,12},{12,8},{16,20},{20,16},{24,28},{28,24},{1,5},{5... | collective-permute-start | bytes 1572872 | tf_op jit(solution)/shard_map/ppermute | solution.py:580
  25.1 14.3 %collective-permute-start.1 = (f32[2,2,256,128]{3,2,1,0:T(8,128)S(1)}, f32[2,2,256,128]{3,2,1,0:T(8,128)S(1)}, u32[]{:S(2)}, u32[]{:S(2)}) collective-permute-start(f32[2,2,256,128]{3,2,1,0:T(8,128)S(1)} %get-tuple-element.19.refs_1_), channel_id=1, source_target_pairs={{4,8},{8,4},{12,16},{16,12},{20,24},{24,20},{5,9},{9,5},{13,17},{1... | collective-permute-start | bytes 1572872 | tf_op jit(solution)/shard_map/ppermute | solution.py:580
  25.8 13.6 %collective-permute-start.2 = (f32[2,2,256,128]{3,2,1,0:T(8,128)S(1)}, f32[2,2,256,128]{3,2,1,0:T(8,128)S(1)}, u32[]{:S(2)}, u32[]{:S(2)}) collective-permute-start(f32[2,2,256,128]{3,2,1,0:T(8,128)S(1)} %get-tuple-element.20.refs_2_), channel_id=1, source_target_pairs={{0,4},{4,0},{8,12},{12,8},{16,20},{20,16},{24,28},{28,24},{1,5},{5... | collective-permute-start | bytes 1572872 | tf_op jit(solution)/shard_map/ppermute | solution.py:580
  27.2 12.2 %collective-permute-start.3 = (f32[2,2,256,128]{3,2,1,0:T(8,128)S(1)}, f32[2,2,256,128]{3,2,1,0:T(8,128)S(1)}, u32[]{:S(2)}, u32[]{:S(2)}) collective-permute-start(f32[2,2,256,128]{3,2,1,0:T(8,128)S(1)} %get-tuple-element.21.refs_3_), channel_id=1, source_target_pairs={{4,8},{8,4},{12,16},{16,12},{20,24},{24,20},{5,9},{9,5},{13,17},{1... | collective-permute-start | bytes 1572872 | tf_op jit(solution)/shard_map/ppermute | solution.py:580
  27.9 5.1 %collective-permute-start.6 = (f32[3,128,128]{2,1,0:T(8,128)S(1)}, f32[3,128,128]{2,1,0:T(8,128)S(1)}, u32[]{:S(2)}, u32[]{:S(2)}) collective-permute-start(f32[3,128,128]{2,1,0:T(8,128)S(1)} %get-tuple-element.26), channel_id=1, source_target_pairs={{0,4},{4,0},{8,12},{12,8},{16,20},{20,16},{24,28},{28,24},{1,5},{5... | collective-permute-start | bytes 589832 | tf_op jit(solution)/shard_map/ppermute | solution.py:580
  33.0 1.3 %collective-permute-start.7 = (f32[3,128,128]{2,1,0:T(8,128)S(1)}, f32[3,128,128]{2,1,0:T(8,128)S(1)}, u32[]{:S(2)}, u32[]{:S(2)}) collective-permute-start(f32[3,128,128]{2,1,0:T(8,128)S(1)} %get-tuple-element.27), channel_id=1, source_target_pairs={{4,8},{8,4},{12,16},{16,12},{20,24},{24,20},{5,9},{9,5},{13,17},{1... | collective-permute-start | bytes 589832 | tf_op jit(solution)/shard_map/ppermute | solution.py:580
  45.6 20.4 %all-to-all-start = ((f32[32,2,128]{2,1,0:T(2,128)}), f32[32,2,128]{2,1,0:T(2,128)S(1)}, u32[]{:S(2)}, u32[]{:S(2)}) async-start(f32[32,2,128]{2,1,0:T(2,128)} %get-tuple-element.30), calls=%async_computation | async-start | bytes 65536 | tf_op jit(solution)/shard_map/all_to_all | solution.py:710
